TPU v7x, 32 devices: a whole 2x2x4 slice. The times are simulated.
32 devices in a mesh: groups: 2 (over y), depth: 4 (over z), cols: 2 (over x), heads: 2 (over core).
Axes of the slice: x: 2, y: 2, z: 4, core: 2. Of those that a mesh axis runs over, the one named last changes fastest.
Arguments:
- alignment: bfloat16 [64, 256, 768], P(('groups', 'depth'), 'cols'), parts along dimension 0, may hold values from -6 to 6
- norm_gain: float32 [768], replicated, may hold values from 0.25 to 1.75
- w_query: bfloat16 [768, 768], P(None, 'heads'), may hold values from -1 to 1
- w_key: bfloat16 [768, 768], P(None, 'heads'), may hold values from -2 to 2
- w_value: bfloat16 [768, 768], P(None, 'heads'), may hold values from -0.21875 to 0.21875
- w_out: bfloat16 [768, 768], P(None, 'heads'), may hold values from -0.21875 to 0.21875
- row_mask: int32 [64], P(('groups', 'depth')), parts along dimension 0, may hold values 0 or 1
- col_valid: int32 [512], P(('groups', 'cols')), parts along dimension 0, may hold values 0 or 1
Outputs:
- attended: bfloat16 [64, 256, 768], P(('groups', 'depth'), 'cols', 'heads'), parts along dimension 0
There are 2 independent parts, one for each index of `groups`. A program takes and returns all parts, laid end to end along the dimension named above; an argument that names none is the same for every part. Nothing has to cross between parts.
Inputs may be any that keep to these rules, and one draw needn't show every extreme that they name: `col_valid`: some column of every family is valid. `row_mask`: some row of every family is real.
All inputs are finite; a program needn't handle non-finite values. No bound on the sum of `row_mask` or of `col_valid` on one device may be relied on, other than what follows from the above.
Results may differ from a plain program's by a relative error of at most 0.009.
Values may be sent and summed in bfloat16 or wider, within the bound.
No kernel may reach another device: no remote copies, remote signals or barrier semaphores. Data moves between devices by JAX's collectives and lax.ppermute only.
A program may use at most 64 MiB of HBM per device.

v0:
```python
import jax
import jax.numpy as jnp
from jax import lax
from jax.sharding import PartitionSpec as P

HEADS = 12


def from_behind(value, axis, steps):
    count = lax.axis_size(axis)
    pairs = [(source, (source + steps) % count) for source in range(count)]
    return lax.ppermute(value, axis, pairs)


def to_heads(matrix, rows_here, cols_here, local_heads, head_width):
    shaped = matrix.reshape(rows_here, cols_here, local_heads, head_width)
    return jnp.transpose(shaped, (2, 1, 0, 3)).reshape(
        local_heads, cols_here, rows_here * head_width
    )


def tile_logits(query_tile, key_tile):
    return lax.dot_general(
        query_tile, key_tile, (((2,), (2,)), ((0,), (0,))), preferred_element_type=jnp.float32
    )


def apply_probs(prob_tile, value_tile):
    return lax.dot_general(
        prob_tile, value_tile, (((2,), (1,)), ((0,), (0,))), preferred_element_type=jnp.float32
    )


def normalize(scores, valid_row, factor):
    valid_cols = valid_row[0] > 0.5
    scaled = jnp.where(valid_cols[None, None, :], scores * factor, -1e30)
    top = jnp.max(scaled, axis=-1, keepdims=True)
    expo = jnp.where(valid_cols[None, None, :], jnp.exp(scaled - top), 0.0)
    return (expo / jnp.sum(expo, axis=-1, keepdims=True)).astype(jnp.bfloat16)


def on_device(alignment, norm_gain, w_query, w_key, w_value, w_out, row_mask, col_valid):
    rows_here, cols_here, width = alignment.shape
    local_width = w_query.shape[1]
    head_width = width // HEADS
    local_heads = local_width // head_width
    blocks = lax.axis_size("cols")
    total_cols = blocks * cols_here
    column_index = lax.axis_index("cols")
    values_f = alignment.astype(jnp.float32)
    average = jnp.mean(values_f, axis=-1, keepdims=True)
    centred = values_f - average
    spread = jnp.mean(centred * centred, axis=-1, keepdims=True)
    normed = (centred * lax.rsqrt(spread + 1e-05) * norm_gain).astype(jnp.bfloat16)
    flattened = normed.reshape(-1, width)
    alive_rows = row_mask.astype(jnp.float32)
    count = lax.psum(jnp.sum(alive_rows), "depth")
    row_scale = jnp.repeat(alive_rows, cols_here)[:, None]
    queries = (jnp.dot(flattened, w_query, preferred_element_type=jnp.float32) * row_scale).astype(
        jnp.bfloat16
    )
    key_rows = jnp.dot(flattened, w_key, preferred_element_type=jnp.float32).astype(jnp.bfloat16)
    value_rows = jnp.dot(flattened, w_value, preferred_element_type=jnp.float32).astype(
        jnp.bfloat16
    )
    query_tile = to_heads(queries, rows_here, cols_here, local_heads, head_width)
    key_tile = to_heads(key_rows, rows_here, cols_here, local_heads, head_width)
    value_tile = to_heads(value_rows, rows_here, cols_here, local_heads, head_width)
    valid_here = col_valid.astype(jnp.bfloat16)[None, :]
    empty_logits = jnp.zeros((local_heads, cols_here, total_cols), jnp.float32)
    empty_valid = jnp.zeros((1, total_cols), jnp.float32)
    logits, valid_row = (empty_logits, empty_valid)
    current = (key_tile, valid_here)
    for offset in range(blocks):
        source = (column_index - offset) % blocks
        begin = source * cols_here
        zero = jnp.zeros((), jnp.int32)
        logits = lax.dynamic_update_slice(
            logits, tile_logits(query_tile, current[0]), (zero, zero, begin)
        )
        valid_row = lax.dynamic_update_slice(
            valid_row, current[1].astype(jnp.float32), (zero, begin)
        )
        if offset + 1 < blocks:
            current = from_behind((current[0], current[1]), "cols", 1)
    factor = lax.rsqrt(jnp.float32(head_width) * count)
    share = lax.psum_scatter(logits, "depth", scatter_dimension=1, tiled=True)
    probs_share = normalize(share, valid_row, factor)
    probs = lax.all_gather(probs_share, "depth", axis=1, tiled=True)
    accumulated = jnp.zeros((local_heads, cols_here, rows_here * head_width), jnp.float32)
    current_values = value_tile
    for offset in range(blocks):
        source = (column_index - offset) % blocks
        begin = source * cols_here
        prob_tile = lax.dynamic_slice_in_dim(probs, begin, cols_here, 2)
        accumulated = accumulated + apply_probs(prob_tile, current_values)
        if offset + 1 < blocks:
            current_values = from_behind(current_values, "cols", 1)
    heads_out = accumulated.astype(jnp.bfloat16).reshape(
        local_heads, cols_here, rows_here, head_width
    )
    heads_out = jnp.transpose(heads_out, (2, 1, 0, 3)).reshape(rows_here, cols_here, local_width)
    all_heads = lax.all_gather(heads_out, "heads", axis=2, tiled=True)
    attended = (
        jnp.dot(all_heads.reshape(-1, width), w_out, preferred_element_type=jnp.float32) * row_scale
    )
    return attended.astype(jnp.bfloat16).reshape(rows_here, cols_here, w_out.shape[1])


def solution(mesh):
    in_specs = (
        P(("groups", "depth"), "cols", None),
        P(),
        P(None, "heads"),
        P(None, "heads"),
        P(None, "heads"),
        P(None, "heads"),
        P(("groups", "depth")),
        P(("groups", "cols")),
    )
    out_specs = P(("groups", "depth"), "cols", "heads")
    return jax.shard_map(
        on_device, mesh=mesh, in_specs=in_specs, out_specs=out_specs, check_vma=False
    )
```

profile of v0, /device:TPU:0, one launch (start us, length us, event | category | flops | bytes accessed | tf_op | source)
XLA Modules:
  0.0 100.3 jit_solution(16694450081437156341)
XLA Ops:
  6.5 0.0 copy-start
  6.5 0.0 copy-start.5
  6.5 0.0 reduce-scatter.2.cloned.1.call-start
  6.5 1.8 %convert_reduce_fusion = f32[8,128]{1,0:T(8,128)S(1)} fusion(bf16[8,128,768]{2,1,0:T(8,128)(2,1)} %param.8), kind=kLoop, calls=%fused_computation.3 | loop fusion | flops 1571840 | bytes 1576960 | tf_op jit(solution)/shard_map/reduce_sum | solution.py:51
  8.4 0.1 copy-done.1
  8.5 0.6 fusion.4
  9.1 0.0 copy-done.5
  9.1 0.5 fusion.6
  9.6 0.0 copy-start.3
  9.6 1.1 %copy-done.3 = bf16[8,128,768]{2,1,0:T(8,128)(2,1)} copy-done((bf16[8,128,768]{2,1,0:T(8,128)(2,1)}, bf16[8,128,768]{2,1,0:T(8,128)(2,1)S(1)}, u32[]{:S(2)}) %copy-start.3) | copy-done | bytes 1572888
  10.8 0.0 copy-done
  10.8 1.0 convolution_convert_fusion.1
  11.8 0.3 copy.28
  12.1 0.2 copy.46
  12.2 0.0 copy-start.8
  12.3 0.0 copy-start.4
  12.3 0.2 copy.29
  12.5 1.2 %copy.32 = bf16[6,128,512]{2,1,0:T(8,128)(2,1)} copy(bf16[6,128,512]{1,2,0:T(8,128)(2,1)S(1)} %bitcast.52) | data formatting | bytes 1572864 | tf_op jit(solution)/shard_map/reshape | solution.py:17
  13.6 3.0 %collective-permute-start.1 = (bf16[6,128,512]{2,1,0:T(8,128)(2,1)}, bf16[6,128,512]{2,1,0:T(8,128)(2,1)}, u32[]{:S(2)}, u32[]{:S(2)}) collective-permute-start(bf16[6,128,512]{2,1,0:T(8,128)(2,1)} %copy.32), channel_id=1, source_target_pairs={{0,2},{2,0},{1,3},{3,1},{4,6},{6,4},{5,7},{7,5},{8,10},{10,8},{9,1... | collective-permute-start | bytes 2359304 | tf_op jit(solution)/shard_map/ppermute | solution.py:12
  16.6 0.0 copy-done.8
  16.6 0.1 broadcast_bitcast_fusion
  16.7 0.0 copy-done.4
  16.7 2.9 %multiply_convert_fusion.1 = bf16[1024,384]{1,0:T(8,128)(2,1)} fusion(bf16[1024,768]{1,0:T(8,128)(2,1)S(1)} %bitcast.68, bf16[768,384]{1,0:T(8,128)(2,1)} %param.10, f32[1024]{0:T(1024)S(1)} %broadcast_bitcast_fusion), kind=kOutput, calls=%fused_computation.11 | convolution fusion | flops 604766208 | bytes 2953216 | tf_op jit(solution)/shard_map/dot_general | solution.py:59
  19.6 1.4 %copy.26 = bf16[1024,384]{0,1:T(8,128)(2,1)S(1)} copy(bf16[1024,384]{1,0:T(8,128)(2,1)} %multiply_convert_fusion.1) | data formatting | bytes 1572864 | tf_op jit(solution)/shard_map/convert_element_type | solution.py:59
  21.0 0.2 copy.45
  21.2 0.2 copy.27
  21.4 0.1 broadcast_in_dim.37
  21.5 0.4 convolution_dynamic-update-slice_fusion.1
  21.9 0.0 copy-start.9
  21.9 0.0 copy-start.6
  21.9 12.5 %collective-permute-done.1 = bf16[6,128,512]{2,1,0:T(8,128)(2,1)} collective-permute-done((bf16[6,128,512]{2,1,0:T(8,128)(2,1)}, bf16[6,128,512]{2,1,0:T(8,128)(2,1)}, u32[]{:S(2)}, u32[]{:S(2)}) %collective-permute-start.1) | collective-permute-done | bytes 786464 | tf_op jit(solution)/shard_map/ppermute | solution.py:12
  34.5 1.5 %convolution_dynamic-update-slice_fusion = f32[6,128,256]{2,1,0:T(8,128)S(1)} fusion(f32[6,128,256]{2,1,0:T(8,128)S(1)} %convolution_dynamic-update-slice_fusion.1, s32[]{:T(128)S(6)} %select_n.35, bf16[6,128,512]{1,2,0:T(8,128)(2,1)S(1)} %bitcast.55, bf16[6,128,512]{2,1,0:T(8,128)(2,1)} %collective-permute-done.1), kind=kOutput, calls=%fused_computation.14 | convolution fusion | flops 100663296 | bytes 1966084 | tf_op jit(solution)/shard_map/dot_general | solution.py:23
  36.0 0.0 copy-start.2
  36.0 0.9 copy-done.2
  36.9 0.0 reduce-scatter.2.cloned.1.call-update
  36.9 0.0 all-gather.2.cloned.1.call-start
  37.0 0.0 copy-done.9
  37.0 1.8 %collective-permute-start = (bf16[1,128]{1,0:T(2,128)(2,1)S(1)}, bf16[1,128]{1,0:T(2,128)(2,1)S(1)}, u32[]{:S(2)}, u32[]{:S(2)}) collective-permute-start(bf16[1,128]{1,0:T(2,128)(2,1)S(1)} %convert_bitcast_fusion), channel_id=1, source_target_pairs={{0,2},{2,0},{1,3},{3,1},{4,6},{6,4},{5,7},{7,5},{8,10},{10,8},{9,1... | collective-permute-start | bytes 776 | tf_op jit(solution)/shard_map/ppermute | solution.py:12
  38.8 0.0 copy-done.6
  38.8 2.4 %convolution_convert_fusion = bf16[1024,384]{1,0:T(8,128)(2,1)S(1)} fusion(bf16[1024,768]{1,0:T(8,128)(2,1)} %bitcast.67, bf16[768,384]{1,0:T(8,128)(2,1)S(1)} %copy-done.6), kind=kOutput, calls=%fused_computation.12 | convolution fusion | flops 604372992 | bytes 2949120 | tf_op jit(solution)/shard_map/dot_general | solution.py:63
  41.2 0.3 copy.34
  41.5 0.2 copy.47
  41.7 0.2 copy.35
  41.9 0.3 copy.37
  42.2 0.3 collective-permute-start.2
  42.5 0.7 convert_reduce_fusion.1
  43.2 0.1 convert_dynamic-update-slice_fusion.1
  43.3 13.1 %psum.7 = f32[]{:T(128)} all-reduce(f32[]{:T(128)} %convert_reduce_fusion.1), channel_id=1, replica_groups=mesh['groups'=2,'depth'=4,'cols'=2,'heads'=2] {'depth'}, use_global_device_ids=true, to_apply=%region_4.5 | all-reduce | flops 1 | bytes 8 | tf_op jit(solution)/shard_map/psum | solution.py:57
  57.1 0.0 collective-permute-done
  57.2 0.1 convert_dynamic-update-slice_fusion
  57.3 4.6 %reduce-scatter.2.cloned.1.call-done = f32[6,32,256]{2,1,0:T(8,128)} async-done(((f32[6,128,256]{2,1,0:T(8,128)}), f32[6,32,256]{2,1,0:T(8,128)}) %reduce-scatter.2.cloned.1.call-update) | async-done | bytes 196624 | tf_op jit(solution)/shard_map/reduce_scatter | solution.py:87
  61.9 1.3 %fusion.11 = bf16[6,32,256]{2,1,0:T(8,128)(2,1)S(1)} fusion(f32[6,32,256]{2,1,0:T(8,128)} %reduce-scatter.2.cloned.1.call-done, f32[]{:T(128)S(6)} %rsqrt.12, pred[256]{0:T(512)(128)(4,1)S(1)} %broadcast_compare_fusion), kind=kOutput, calls=%fused_computation.20 | output fusion | flops 295806 | bytes 295172 | tf_op jit(solution)/shard_map/div | solution.py:39
  63.2 15.0 %all_gather.6 = bf16[6,128,256]{2,1,0:T(8,128)(2,1)S(1)} all-gather(bf16[6,32,256]{2,1,0:T(8,128)(2,1)S(1)} %fusion.11), channel_id=1, replica_groups=mesh['groups'=2,'depth'=4,'cols'=2,'heads'=2] {'depth'}, dimensions={1}, use_global_device_ids=true | all-gather | bytes 491520 | tf_op jit(solution)/shard_map/all_gather | solution.py:89
  78.2 0.4 fusion.13
  78.6 0.0 collective-permute-done.2
  78.6 0.4 add_convert_fusion
  79.0 0.4 copy.38
  79.3 0.9 copy.39
  80.3 0.0 all-gather.2.cloned.1.call-update
  80.3 0.0 copy-start.7
  80.3 9.5 %all-gather.2.cloned.1.call-done = bf16[8,128,768]{1,2,0:T(8,128)(2,1)} async-done(((bf16[8,128,384]{1,2,0:T(8,128)(2,1)}), bf16[8,128,768]{1,2,0:T(8,128)(2,1)}) %all-gather.2.cloned.1.call-update) | async-done | bytes 1572880 | tf_op jit(solution)/shard_map/all_gather | solution.py:103
  89.9 1.7 %copy.40 = bf16[8,128,768]{2,1,0:T(8,128)(2,1)S(1)} copy(bf16[8,128,768]{1,2,0:T(8,128)(2,1)} %all-gather.2.cloned.1.call-done) | data formatting | bytes 3145728 | tf_op jit(solution)/shard_map/all_gather | solution.py:103
  91.6 0.0 copy-done.7
  91.6 1.9 %multiply_convert_fusion = bf16[1024,384]{1,0:T(8,128)(2,1)} fusion(bf16[1024,768]{1,0:T(8,128)(2,1)S(1)} %bitcast.69, bf16[768,384]{1,0:T(8,128)(2,1)S(1)} %copy-done.7, f32[1024]{0:T(1024)S(1)} %broadcast_bitcast_fusion), kind=kOutput, calls=%fused_computation.9 | convolution fusion | flops 604766208 | bytes 2953216 | tf_op jit(solution)/shard_map/dot_general | solution.py:105
  (7 shorter events, 0.0 us)
Async XLA Ops:
  6.5 4.2 %copy-start = (bf16[768,384]{1,0:T(8,128)(2,1)S(1)}, bf16[768,384]{1,0:T(8,128)(2,1)}, u32[]{:S(2)}) copy-start(bf16[768,384]{1,0:T(8,128)(2,1)} %param.11) | copy-start | bytes 1769476
  6.5 1.9 %copy-start.1 = (bf16[8,128,768]{2,1,0:T(8,128)(2,1)S(1)}, bf16[8,128,768]{2,1,0:T(8,128)(2,1)}, u32[]{:S(2)}) copy-start(bf16[8,128,768]{2,1,0:T(8,128)(2,1)} %param.8) | copy-start | bytes 4718596
  6.5 2.5 %copy-start.5 = (f32[768]{0:T(1024)S(1)}, f32[768]{0:T(1024)}, u32[]{:S(2)}) copy-start(f32[768]{0:T(1024)} %param.9) | copy-start | bytes 9220
  6.5 55.3 %reduce-scatter.2.cloned.1.call-start = ((), (), s32[]{:S(2)}) async-start(), calls=%async_computation.1 | async-start | bytes 983040 | tf_op jit(solution)/shard_map/reduce_scatter | solution.py:87
  9.6 1.2 %copy-start.3 = (bf16[8,128,768]{2,1,0:T(8,128)(2,1)}, bf16[8,128,768]{2,1,0:T(8,128)(2,1)S(1)}, u32[]{:S(2)}) copy-start(bf16[8,128,768]{2,1,0:T(8,128)(2,1)S(1)} %fusion.6) | copy-start | bytes 4718596
  12.2 4.4 %copy-start.8 = (s32[8]{0:T(128)S(1)}, s32[8]{0:T(128)}, u32[]{:S(2)}) copy-start(s32[8]{0:T(128)} %param.14) | copy-start | bytes 100
  12.3 4.4 %copy-start.4 = (bf16[8,128,768]{2,1,0:T(8,128)(2,1)S(1)}, bf16[8,128,768]{2,1,0:T(8,128)(2,1)}, u32[]{:S(2)}) copy-start(bf16[8,128,768]{2,1,0:T(8,128)(2,1)} %copy-done.3) | copy-start | bytes 4718596
  13.6 20.8 %collective-permute-start.1 = (bf16[6,128,512]{2,1,0:T(8,128)(2,1)}, bf16[6,128,512]{2,1,0:T(8,128)(2,1)}, u32[]{:S(2)}, u32[]{:S(2)}) collective-permute-start(bf16[6,128,512]{2,1,0:T(8,128)(2,1)} %copy.32), channel_id=1, source_target_pairs={{0,2},{2,0},{1,3},{3,1},{4,6},{6,4},{5,7},{7,5},{8,10},{10,8},{9,1... | collective-permute-start | bytes 2359304 | tf_op jit(solution)/shard_map/ppermute | solution.py:12
  21.9 15.1 %copy-start.9 = (s32[128]{0:T(128)S(1)}, s32[128]{0:T(128)}, u32[]{:S(2)}) copy-start(s32[128]{0:T(128)} %param.15) | copy-start | bytes 1540
  21.9 16.9 %copy-start.6 = (bf16[768,384]{1,0:T(8,128)(2,1)S(1)}, bf16[768,384]{1,0:T(8,128)(2,1)}, u32[]{:S(2)}) copy-start(bf16[768,384]{1,0:T(8,128)(2,1)} %param.12) | copy-start | bytes 1769476
  36.0 0.9 copy-start.2
  36.9 52.9 %all-gather.2.cloned.1.call-start = ((), (), s32[]{:S(2)}) async-start(), calls=%async_computation.2 | async-start | bytes 2359296 | tf_op jit(solution)/shard_map/all_gather | solution.py:103
  37.0 20.2 %collective-permute-start = (bf16[1,128]{1,0:T(2,128)(2,1)S(1)}, bf16[1,128]{1,0:T(2,128)(2,1)S(1)}, u32[]{:S(2)}, u32[]{:S(2)}) collective-permute-start(bf16[1,128]{1,0:T(2,128)(2,1)S(1)} %convert_bitcast_fusion), channel_id=1, source_target_pairs={{0,2},{2,0},{1,3},{3,1},{4,6},{6,4},{5,7},{7,5},{8,10},{10,8},{9,1... | collective-permute-start | bytes 776 | tf_op jit(solution)/shard_map/ppermute | solution.py:12
  42.2 36.5 %collective-permute-start.2 = (bf16[6,128,512]{2,1,0:T(8,128)(2,1)S(1)}, bf16[6,128,512]{2,1,0:T(8,128)(2,1)S(1)}, u32[]{:S(2)}, u32[]{:S(2)}) collective-permute-start(bf16[6,128,512]{2,1,0:T(8,128)(2,1)S(1)} %copy.37), channel_id=1, source_target_pairs={{0,2},{2,0},{1,3},{3,1},{4,6},{6,4},{5,7},{7,5},{8,10},{10,8},{9,1... | collective-permute-start | bytes 2359304 | tf_op jit(solution)/shard_map/ppermute | solution.py:12
  80.3 11.3 %copy-start.7 = (bf16[768,384]{1,0:T(8,128)(2,1)S(1)}, bf16[768,384]{1,0:T(8,128)(2,1)}, u32[]{:S(2)}) copy-start(bf16[768,384]{1,0:T(8,128)(2,1)} %param.13) | copy-start | bytes 1769476
Sparse Core Ops, SparseCore 0:
  37.0 24.7 reduce-scatter.1
  80.4 9.3 all-gather.1
where the time goes:
time: 101 us; the launch traced here: 100 us
  blocking collectives  28.2 us (28%)
  waiting for transfers between devices  26.7 us (26%)
  between operations  14.4 us (14%)
  matrix products  10.8 us (11%)
  local copies, waits for them, and re-layouts  9.84 us (10%)
  starting transfers between devices  5.17 us (5%)
  other arithmetic  5.15 us (5%)
    all_gather x1, blocking collectives, on_device(): probs = lax.all_gather(probs_share, 'depth', axis=1, tiled=True)  15 us
    psum x1, blocking collectives, on_device(): count = lax.psum(jnp.sum(alive_rows), 'depth')  13.1 us
    ppermute x3, waiting for transfers between devices, from_behind(): return lax.ppermute(value, axis, pairs)  12.5 us
    all_gather x1, waiting for transfers between devices, on_device(): all_heads = lax.all_gather(heads_out, 'heads', axis=2, tiled=True)  9.53 us
    ppermute x3, starting transfers between devices, from_behind(): return lax.ppermute(value, axis, pairs)  5.13 us
    reduce_scatter x1, waiting for transfers between devices, on_device(): share = lax.psum_scatter(logits, 'depth', scatter_dimension=1, tiled=True)  4.62 us
    dot_general x1, matrix products, on_device(): jnp.dot(flattened, w_query, preferred_element_type=jnp.float32) * row_scale  2.92 us
    unnamed x23, local copies, waits for them, and re-layouts  2.67 us
  transfers between devices with their start and end apart: 5, of which 3 were waited for; matrix products, arithmetic and copies ran while one was open for 11% of the time, Pallas kernels for 0%

commit v1 on v0

v1 whole, which is shorter than its diff:
```python
import functools

import jax
import jax.numpy as jnp
from jax import lax
from jax.experimental import pallas as pl
from jax.experimental.pallas import tpu as pltpu
from jax.sharding import PartitionSpec as P

HEADS = 12
LANES = 128
CHUNKS = 2
SIZE = 2
LIMIT = 16 << 20
LOWEST = -1e30
PAD = 16


VMEM = pltpu.VMEM
SMEM = pltpu.SMEM
HBM = pltpu.HBM
BF16 = jnp.bfloat16
F32 = jnp.float32


def from_behind(value, axis, steps):
    count = lax.axis_size(axis)
    return lax.ppermute(value, axis, [(s, (s + steps) % count) for s in range(count)])


def spec(space=VMEM):
    return pl.BlockSpec(memory_space=space)


def call(kernel, out_shape, in_specs, scratch=(), flops=0, space=VMEM):
    single = not isinstance(out_shape, (list, tuple))
    shapes = [out_shape] if single else list(out_shape)
    nbytes = sum(s.size * s.dtype.itemsize for s in shapes)
    shapes = [space(s.shape, s.dtype) for s in shapes]
    fn = pl.pallas_call(
        kernel,
        out_shape=shapes,
        in_specs=in_specs,
        out_specs=[spec(space) for _ in shapes],
        scratch_shapes=list(scratch),
        compiler_params=pltpu.CompilerParams(vmem_limit_bytes=LIMIT),
        cost_estimate=pl.CostEstimate(flops=flops, transcendentals=0, bytes_accessed=2 * nbytes),
    )

    def run(*args):
        args = [
            arg
            if block.memory_space == SMEM
            else pltpu.with_memory_space_constraint(arg, block.memory_space)
            for arg, block in zip(args, in_specs, strict=True)
        ]
        out = fn(*args)
        return out[0] if single else out

    return run


def dot(left, right):
    return jnp.dot(left, right, preferred_element_type=F32)


def dot_t(left, right):
    return lax.dot_general(left, right, (((1,), (1,)), ((), ())), preferred_element_type=F32)


def normed_rows(rows, gain):
    values_f = rows.astype(F32)
    average = jnp.mean(values_f, axis=-1, keepdims=True)
    centred = values_f - average
    spread = jnp.mean(centred * centred, axis=-1, keepdims=True)
    return (centred * lax.rsqrt(spread + 1e-05) * gain).astype(BF16)


def load_kernel(place, valid, rows_in, resident, *rest, part_cols):
    last, sems = rest
    part_rows = (last.shape[0] - PAD) // part_cols
    cols = rows_in.shape[1]
    begin = place[1] * part_rows
    copies = [
        pltpu.make_async_copy(
            rows_in.at[begin + r, pl.ds(cols - part_cols, part_cols), :],
            last.at[pl.ds(r * part_cols, part_cols)],
            sems.at[r],
        )
        for r in range(part_rows)
    ]
    copies.append(pltpu.make_async_copy(rows_in, resident, sems.at[part_rows]))
    for copy in copies:
        copy.start()
    tail = last.shape[0] - PAD
    last[tail:, :] = jnp.zeros((PAD, last.shape[1]), BF16)
    last[tail:, 0:cols] = jnp.broadcast_to(valid[...].astype(F32), (PAD, cols)).astype(BF16)
    for copy in copies:
        copy.wait()


def side_by_side(block, first, cols, pair):
    at = slice(pair * LANES, (pair + 1) * LANES)
    pieces = [block[(first + r) * cols : (first + r + 1) * cols, at] for r in range(SIZE)]
    return jnp.concatenate(pieces, axis=1)


def write_shards(total, shards, depth_index):
    slots, cols, _ = total.shape
    count = len(shards)
    part = cols // count
    for k, shard in enumerate(shards):
        begin = pl.multiple_of(lax.bitwise_xor(depth_index, k) * part, part)
        for slot in range(slots):
            rows = total[slot, pl.ds(begin, part), :]
            shard[slot * part : (slot + 1) * part, :] = rows


def own_kernel(place, live, rows_in, gain, w_query, w_key, *rest, shards):
    normed_out, query_out = rest[0], rest[1]
    outs = rest[2 : 2 + shards]
    keys, total = rest[2 + shards :]
    groups, pairs = query_out.shape[0], query_out.shape[1]
    _, cols, width = rows_in.shape
    low = lax.broadcasted_iota(jnp.int32, (cols, LANES), 1) < LANES // 2
    zero = jnp.zeros((cols, LANES), BF16)
    for g in range(groups):
        rows = rows_in[g * SIZE : (g + 1) * SIZE].reshape(SIZE * cols, width)
        normed = normed_rows(rows, gain[...])
        normed_out[g] = normed
        query = dot(normed, w_query[...])
        key = dot(normed, w_key[...]).astype(BF16)
        for r in range(SIZE):
            scale = live[g * SIZE + r].astype(F32)
            piece = (query[r * cols : (r + 1) * cols] * scale).astype(BF16)
            for p in range(pairs):
                both = piece[:, p * LANES : (p + 1) * LANES]
                at = slice(r * LANES, (r + 1) * LANES)
                query_out[g, p, 0:cols, at] = jnp.where(low, both, zero)
                query_out[g, p, cols : 2 * cols, at] = jnp.where(low, zero, both)
        for p in range(pairs):
            keys[g, p] = side_by_side(key, 0, cols, p)
    for p in range(pairs):
        score = dot_t(query_out[0, p], keys[0, p])
        for g in range(1, groups):
            score = score + dot_t(query_out[g, p], keys[g, p])
        total[2 * p] = score[:cols]
        total[2 * p + 1] = score[cols:]
    write_shards(total, outs, place[0])
    real = F32(0)
    for r in range(groups * SIZE):
        real = real + live[r].astype(F32)
    for out in outs:
        out[out.shape[0] - 8 :, :] = jnp.full((8, LANES), real, F32)


def value_kernel(*refs, parts, cols):
    normed, w_value, values = refs[:parts], refs[parts], refs[parts + 1]
    inner, pairs = values.shape[1], values.shape[2]
    for k in range(parts):
        value = dot(normed[k][...], w_value[...]).astype(BF16)
        for g in range(inner):
            for p in range(pairs):
                values[k, g, p] = side_by_side(value, g * SIZE, cols, p)


def own_value_kernel(normed, w_value, values, *, cols):
    for g in range(values.shape[0]):
        value = dot(normed[g], w_value[...]).astype(BF16)
        for p in range(values.shape[1]):
            values[g, p] = side_by_side(value, 0, cols, p)


def remote_kernel(place, part, gain, w_key, query, *rest, step, chunk, part_cols, cores, shards):
    if step > 0:
        before, rest = rest[0], rest[1:]
    normed_out, rest = rest[0], rest[1:]
    last = step + 1 == cores
    used = normed_out.shape[0]
    rows, cols = used // part_cols, part_cols
    pairs, full = query.shape[1], query.shape[2] // 2
    normed = normed_rows(part[0:used, :], gain[...])
    normed_out[...] = normed
    key = dot(normed, w_key[...]).astype(BF16)
    total = rest[shards] if last else rest[0]
    source = lax.rem(place[1] + cores - step, cores)
    inner = rows // SIZE
    low = lax.broadcasted_iota(jnp.int32, (full, LANES), 1) < LANES // 2
    for p in range(pairs):
        score = before[p] if step > 0 else None
        whole = None
        for g in range(inner):
            one = side_by_side(key, g * SIZE, cols, p)
            twice = jnp.concatenate([one, one], axis=0)
            extra = dot_t(query[source * inner + g, p], twice)
            whole = extra if whole is None else whole + extra
        left, right = whole[:full], whole[full:]
        if chunk % 2 == 1:
            left, right = right, left
        packed = jnp.where(low, left, right)
        total[p] = packed if score is None else score + packed
    if last:
        write_shards(total, rest[:shards], place[0])


def added(pieces):
    total = pieces[0][...]
    for piece in pieces[1:]:
        total = total + piece[...]
    return total


def soft_kernel(*rest, shards, offsets, heads, head_width):
    valid, rest = rest[: 1 + offsets], rest[1 + offsets :]
    probs = rest[-1]
    tiles = 1 + offsets * CHUNKS
    sums = [added(rest[t * shards : (t + 1) * shards]) for t in range(tiles)]
    part = probs.shape[0] // heads
    factor = lax.rsqrt(F32(head_width) * sums[0][heads * part : heads * part + 1, 0:1])
    low = lax.broadcasted_iota(jnp.int32, (part, LANES), 1) < LANES // 2
    blocks = 1 + offsets
    masks = [
        jnp.broadcast_to(valid[b][...] > 0.5, (part, LANES)) for b in range(blocks)
    ]
    for h in range(heads):
        pieces = [sums[0][h * part : (h + 1) * part]]
        at = slice(h // 2 * part, (h // 2 + 1) * part)
        for o in range(offsets):
            first, second = sums[1 + o * CHUNKS][at], sums[2 + o * CHUNKS][at]
            if h % 2 == 0:
                pieces.append(jnp.where(low, first, second))
            else:
                pieces.append(pltpu.roll(jnp.where(low, second, first), LANES // 2, 1))
        scaled = [jnp.where(masks[b], pieces[b] * factor, LOWEST) for b in range(blocks)]
        top = jnp.max(functools.reduce(jnp.maximum, scaled), axis=-1, keepdims=True)
        expo = [jnp.where(masks[b], jnp.exp(scaled[b] - top), 0.0) for b in range(blocks)]
        whole = jnp.sum(functools.reduce(jnp.add, expo), axis=-1, keepdims=True)
        for b in range(blocks):
            probs[h * part : (h + 1) * part, b * LANES : (b + 1) * LANES] = (
                expo[b] / whole
            ).astype(BF16)


def mix_kernel(place, *rest, shards, side, cores, offsets):
    own = rest[shards]
    remote = rest[shards + 1 : shards + 1 + offsets * CHUNKS]
    out, probs = rest[shards + 1 + offsets * CHUNKS :]
    _, pairs, cols, lanes = own.shape
    inner = out.shape[0] // SIZE
    part = cols // shards
    for k in range(shards):
        begin = lax.bitwise_xor(place[0], k) * part
        for head in range(2 * pairs):
            at = pl.multiple_of(head % 2 * cols + begin, part)
            probs[head // 2, pl.ds(at, part), :] = rest[k][head * part : (head + 1) * part, :]
    lane = lax.broadcasted_iota(jnp.int32, (cols, lanes), 1)
    low = lax.rem(lane, LANES) < LANES // 2
    step = lax.rem(place[1] + cores - side, cores)
    for g in range(inner):
        for p in range(pairs):
            blocks = [own[side * inner + g, p]]
            blocks += [block[step, g, p] for block in remote]
            mixed = dot(probs[p], jnp.concatenate(blocks, axis=0))
            picked = jnp.where(low, mixed[:cols], mixed[cols:]).astype(BF16)
            for r in range(SIZE):
                out[g * SIZE + r, :, p * LANES : (p + 1) * LANES] = picked[
                    :, r * LANES : (r + 1) * LANES
                ]


def order_kernel(place, w_out, ordered, *, cores):
    local = w_out.shape[0] // cores
    for k in range(cores):
        source = lax.rem(place[1] + cores - k, cores)
        rows = w_out[pl.ds(pl.multiple_of(source * local, local), local), :]
        ordered[k * local : (k + 1) * local, :] = rows


def projected(live, parts, weights, begin, first):
    cols, local = parts[0].shape[1], parts[0].shape[2]
    blocks = [part[begin : begin + SIZE].reshape(SIZE * cols, local) for part in parts]
    total = dot(jnp.concatenate(blocks, axis=1), weights[...])
    results = []
    for r in range(SIZE):
        scale = live[first + begin + r].astype(F32)
        results.append((total[r * cols : (r + 1) * cols] * scale).astype(BF16))
    return results


def project_kernel(live, *rest, cores, first):
    parts, weights, out = rest[:cores], rest[cores], rest[cores + 1]
    for begin in range(0, out.shape[0], SIZE):
        for r, rows in enumerate(projected(live, parts, weights, begin, first)):
            out[begin + r] = rows


def finish_kernel(live, *rest, cores):
    parts, weights = rest[:cores], rest[cores]
    ready = rest[cores + 1 : 2 * cores]
    out, buffer, sems = rest[2 * cores :]
    rows = buffer.shape[0]
    copies = []
    for side, done in enumerate(ready):
        copies.append(
            pltpu.make_async_copy(done, out.at[pl.ds(side * rows, rows)], sems.at[len(copies)])
        )
        copies[-1].start()
    first = (cores - 1) * rows
    for begin in range(0, rows, SIZE):
        for r, block in enumerate(projected(live, parts, weights, begin, first)):
            buffer[begin + r] = block
        copies.append(
            pltpu.make_async_copy(
                buffer.at[pl.ds(begin, SIZE)],
                out.at[pl.ds(first + begin, SIZE)],
                sems.at[len(copies)],
            )
        )
        copies[-1].start()
    for copy in copies:
        copy.wait()


def on_device(alignment, norm_gain, w_query, w_key, w_value, w_out, row_mask, col_valid):
    rows_here, cols_here, width = alignment.shape
    local_width = w_query.shape[1]
    head_width = width // HEADS
    local_heads = local_width // head_width
    pairs = local_heads // 2
    offsets = lax.axis_size("cols") - 1
    depth = lax.axis_size("depth")
    cores = lax.axis_size("heads")
    core = lax.axis_index("heads")
    place = jnp.stack([lax.axis_index("depth"), core]).astype(jnp.int32)
    part_rows = rows_here // cores
    inner = part_rows // SIZE
    groups = rows_here // SIZE
    part_cols = cols_here // CHUNKS
    direct = depth in (2, 4, 8) and cols_here % (16 * depth) == 0
    shards = depth if direct else 1
    part = cols_here // shards
    lanes = SIZE * LANES
    total_cols = (1 + offsets) * cols_here
    shape = jax.ShapeDtypeStruct
    gain = norm_gain[None, :]

    first = lax.dynamic_slice(
        alignment, (core * part_rows, 0, 0), (part_rows, cols_here - part_cols, width)
    )
    sent = [
        first[:, c * part_cols : (c + 1) * part_cols].reshape(part_rows * part_cols, width)
        for c in range(CHUNKS - 1)
    ]
    resident, last_chunk = call(
        functools.partial(load_kernel, part_cols=part_cols),
        [
            shape((rows_here, cols_here, width), BF16),
            shape((part_rows * part_cols + PAD, width), BF16),
        ],
        [spec(SMEM), spec(), spec(HBM)],
        [pltpu.SemaphoreType.DMA((part_rows + 1,))],
    )(place, col_valid[None, :], alignment)
    sent.append(last_chunk)
    arrived = {}
    for offset in range(1, offsets + 1):
        for c in range(CHUNKS):
            mine = from_behind(sent[c], "cols", offset)
            arrived[offset, c] = [mine] + [from_behind(mine, "heads", k) for k in range(1, cores)]

    def exchange(values):
        received = [values[0]]
        for k in range(1, shards):
            swapped = [(source, source ^ k) for source in range(depth)]
            received.append(lax.ppermute(values[k], "depth", swapped))
        return received

    own = call(
        functools.partial(own_kernel, shards=shards),
        [
            shape((groups, SIZE * cols_here, width), BF16),
            shape((groups, pairs, 2 * cols_here, lanes), BF16),
        ]
        + [shape((local_heads * part + 8, cols_here), F32)] * shards,
        [spec(SMEM), spec(SMEM)] + [spec()] * 4,
        [
            pltpu.VMEM((groups, pairs, cols_here, lanes), BF16),
            pltpu.VMEM((local_heads, cols_here, cols_here), F32),
        ],
        flops=4 * rows_here * cols_here * width * local_width,
    )(place, row_mask, resident, gain, w_query, w_key)
    normed, query, own_sums = own[0], own[1], exchange(own[2:])

    own_values = call(
        functools.partial(own_value_kernel, cols=cols_here),
        shape((groups, pairs, cols_here, lanes), BF16),
        [spec()] * 2,
        flops=2 * rows_here * cols_here * width * local_width,
    )(normed, w_value)
    ordered = call(
        functools.partial(order_kernel, cores=cores), shape(w_out.shape, BF16), [spec(SMEM), spec()]
    )(place, w_out)

    tiles, remote_values = [], []
    for offset in range(1, offsets + 1):
        for c in range(CHUNKS):
            before, rows_of = [], []
            for k in range(cores):
                outs = [shape((part_rows * part_cols, width), BF16)]
                scratch = []
                if k + 1 == cores:
                    outs += [shape((pairs * part, LANES), F32)] * shards
                    scratch = [pltpu.VMEM((pairs, cols_here, LANES), F32)]
                else:
                    outs += [shape((pairs, cols_here, LANES), F32)]
                result = call(
                    functools.partial(
                        remote_kernel,
                        step=k,
                        chunk=c,
                        part_cols=part_cols,
                        cores=cores,
                        shards=shards,
                    ),
                    outs,
                    [spec(SMEM)] + [spec()] * (4 + len(before)),
                    scratch,
                    flops=2 * part_rows * part_cols * width * local_width,
                )(place, arrived[offset, c][k], gain, w_key, query, *before)
                rows_of.append(result[0])
                before = [result[1]]
            tiles.append(exchange(result[1:]))
            remote_values.append(
                call(
                    functools.partial(value_kernel, parts=cores, cols=part_cols),
                    shape((cores, inner, pairs, part_cols, lanes), BF16),
                    [spec()] * (cores + 1),
                    flops=2 * cores * part_rows * part_cols * width * local_width,
                )(*rows_of, w_value)
            )

    valid_tiles = [col_valid.astype(BF16)[None, :]]
    for offset in range(1, offsets + 1):
        valid_tiles.append(arrived[offset, CHUNKS - 1][0][-PAD : 1 - PAD, :cols_here])
    if direct:
        valid = [tile.astype(F32) for tile in valid_tiles]
        probs = call(
            functools.partial(
                soft_kernel,
                shards=shards,
                offsets=offsets,
                heads=local_heads,
                head_width=head_width,
            ),
            shape((local_heads * part, total_cols), BF16),
            [spec()] * (1 + offsets + shards * (1 + len(tiles))),
            flops=1000000,
        )(*valid, *own_sums, *[piece for tile in tiles for piece in tile])
        probs = exchange([probs] * shards)
    else:
        count = lax.psum(jnp.sum(row_mask.astype(F32)), "depth")
        own_part = own_sums[0][: local_heads * cols_here]
        blocks = [own_part.reshape(local_heads, cols_here, cols_here)]
        for index, tile in enumerate(tiles):
            packed = tile[0].reshape(pairs, cols_here, 2, part_cols)
            packed = packed[:, :, ::-1] if index % CHUNKS % 2 == 1 else packed
            packed = jnp.transpose(packed, (0, 2, 1, 3))
            blocks.append(packed.reshape(local_heads, cols_here, part_cols))
        logits = jnp.concatenate(blocks, axis=2)
        share = lax.psum_scatter(logits, "depth", scatter_dimension=1, tiled=True)
        mask = jnp.concatenate(valid_tiles, axis=1)[None] > 0.5
        scaled = jnp.where(mask, share * lax.rsqrt(F32(head_width) * count), LOWEST)
        expo = jnp.where(mask, jnp.exp(scaled - jnp.max(scaled, axis=-1, keepdims=True)), 0.0)
        probs = (expo / jnp.sum(expo, axis=-1, keepdims=True)).astype(BF16)
        probs = lax.all_gather(probs, "depth", axis=1, tiled=True)
        probs = [probs.reshape(local_heads * cols_here, total_cols)]

    finished = []
    for side in range(cores):
        mine = call(
            functools.partial(
                mix_kernel, shards=shards, side=side, cores=cores, offsets=offsets
            ),
            shape((part_rows, cols_here, local_width), BF16),
            [spec(SMEM)] + [spec()] * (shards + 1 + len(remote_values)),
            [pltpu.VMEM((pairs, 2 * cols_here, total_cols), BF16)],
            flops=4 * part_rows * cols_here * total_cols * local_width,
        )(place, *probs, own_values, *remote_values)
        parts = [mine] + [from_behind(mine, "heads", k) for k in range(1, cores)]
        if side + 1 < cores:
            finished.append(
                call(
                    functools.partial(project_kernel, cores=cores, first=side * part_rows),
                    shape((part_rows, cols_here, local_width), BF16),
                    [spec(SMEM)] + [spec()] * (cores + 1),
                    flops=2 * part_rows * cols_here * width * local_width,
                )(row_mask, *parts, ordered)
            )
    return call(
        functools.partial(finish_kernel, cores=cores),
        shape((rows_here, cols_here, local_width), BF16),
        [spec(SMEM)] + [spec()] * (2 * cores),
        [
            pltpu.VMEM((part_rows, cols_here, local_width), BF16),
            pltpu.SemaphoreType.DMA((cores - 1 + inner,)),
        ],
        flops=2 * part_rows * cols_here * width * local_width,
        space=HBM,
    )(row_mask, *parts, ordered, *finished)


def solution(mesh):
    in_specs = (
        P(("groups", "depth"), "cols", None),
        P(),
        P(None, "heads"),
        P(None, "heads"),
        P(None, "heads"),
        P(None, "heads"),
        P(("groups", "depth")),
        P(("groups", "cols")),
    )
    out_specs = P(("groups", "depth"), "cols", "heads")

    return jax.shard_map(
        on_device, mesh=mesh, in_specs=in_specs, out_specs=out_specs, check_vma=False
    )
```

time: 101 us -> 66.2 us (0.66)
  blocking collectives: 28.2 us -> 0 us
  Pallas kernels: 0 us -> 19.2 us
  starting transfers between devices: 5.17 us -> 21.7 us
  between operations: 14.4 us -> 0.22 us
  matrix products: 10.8 us -> 0 us
  local copies, waits for them, and re-layouts: 9.84 us -> 1.77 us
  other arithmetic: 5.15 us -> 0.08 us
  waiting for transfers between devices: 26.7 us -> 22.9 us
    pallas_call x0 -> x15, Pallas kernels: none -> 19.2 us  [run(): out = fn(*args)]
    ppermute x3 -> x18, starting transfers between devices: 5.13 us -> 21.7 us  [the longest x12 18 us: exchange(): received.append(lax.ppermute(values[k], 'depth', swapped))]
    all_gather x1 -> x0, blocking collectives: 15 us -> none  [on_device(): probs = lax.all_gather(probs_share, 'depth', axis=1, tiled=True)]
    psum x1 -> x0, blocking collectives: 13.1 us -> none  [on_device(): count = lax.psum(jnp.sum(alive_rows), 'depth')]
    dot_general x8 -> x0, matrix products: 10.8 us -> none  [the longest x1 2.92 us: on_device(): jnp.dot(flattened, w_query, preferred_element_type=jnp.float32) * row_scale]
    ppermute x3 -> x18, waiting for transfers between devices: 12.5 us -> 22.9 us  [the longest x6 15 us: from_behind(): lax.ppermute(value, axis, [(s, (s + steps) % count) for s in range(count)])]
    all_gather x1 -> x0, waiting for transfers between devices: 9.53 us -> none  [on_device(): all_heads = lax.all_gather(heads_out, 'heads', axis=2, tiled=True)]
    reduce_scatter x1 -> x0, waiting for transfers between devices: 4.62 us -> none  [on_device(): share = lax.psum_scatter(logits, 'depth', scatter_dimension=1, tiled=True)]
  transfers between devices with their start and end apart: 5 -> 18, of which waited for: 3 -> 6; matrix products, arithmetic and copies ran while one was open for 11% -> 0% of each run, Pallas kernels for 0% -> 25%
where the time goes in v1:
time: 66.2 us; the launch traced here: 66 us
  waiting for transfers between devices  22.9 us (35%)
  starting transfers between devices  21.7 us (33%)
  Pallas kernels  19.2 us (29%)
  local copies, waits for them, and re-layouts  1.77 us (3%)
    pallas_call x15, Pallas kernels, run(): out = fn(*args)  19.2 us
    ppermute x12, starting transfers between devices, exchange(): received.append(lax.ppermute(values[k], 'depth', swapped))  18 us
    ppermute x6, waiting for transfers between devices, from_behind(): lax.ppermute(value, axis, [(s, (s + steps) % count) for s in range(count)])  15 us
    ppermute x12, waiting for transfers between devices, exchange(): received.append(lax.ppermute(values[k], 'depth', swapped))  7.91 us
    ppermute x6, starting transfers between devices, from_behind(): lax.ppermute(value, axis, [(s, (s + steps) % count) for s in range(count)])  3.77 us
  transfers between devices with their start and end apart: 18, of which 6 were waited for; matrix products, arithmetic and copies ran while one was open for 0% of the time, Pallas kernels for 25%

profile of v1, /device:TPU:0, one launch (start us, length us, event | category | flops | bytes accessed | tf_op | source)
XLA Modules:
  0.0 66.0 jit_solution(16269660009449363404)
XLA Ops:
  0.0 0.0 copy-start.6
  0.0 0.0 copy-start
  0.0 0.0 copy-start.3
  0.0 1.1 %constant_dynamic-slice_fusion = bf16[4,64,768]{2,1,0:T(8,128)(2,1)S(1)} fusion(bf16[8,128,768]{2,1,0:T(8,128)(2,1)} %rows_in.1, s32[]{:T(128)S(6)} %select_n.3), kind=kLoop, calls=%fused_computation.3 | loop fusion | bytes 786436 | tf_op jit(solution)/shard_map/dynamic_slice | solution.py:347
  1.1 3.0 %collective-permute-start.4 = (bf16[256,768]{1,0:T(8,128)(2,1)S(1)}, bf16[256,768]{1,0:T(8,128)(2,1)S(1)}, u32[]{:S(2)}, u32[]{:S(2)}) collective-permute-start(bf16[256,768]{1,0:T(8,128)(2,1)S(1)} %bitcast.8), channel_id=1, source_target_pairs={{0,2},{2,0},{1,3},{3,1},{4,6},{6,4},{5,7},{7,5},{8,10},{10,8},{9,1... | collective-permute-start | bytes 1179656 | tf_op jit(solution)/shard_map/ppermute | solution.py:28
  4.1 0.1 pad_add_fusion.place
  4.2 0.7 copy-done.4
  4.9 2.2 %shard_map.82 = (bf16[8,128,768]{2,1,0:T(8,128)(2,1)S(1)}, bf16[272,768]{1,0:T(8,128)(2,1)S(1)}) custom-call(s32[2]{0:T(128)S(1)} %pad_add_fusion.place, s32[1,128]{1,0:T(1,128)S(1)} %bitcast.7, bf16[8,128,768]{2,1,0:T(8,128)(2,1)} %rows_in.1), custom_call_target="tpu_custom_call" | custom-call | bytes 3981312 | tf_op jit(solution)/shard_map/pallas_call | solution.py:57
  7.1 0.1 collective-permute-start
  7.2 6.9 %collective-permute-done.4.part = bf16[256,768]{1,0:T(8,128)(2,1)S(1)} collective-permute-done((bf16[256,768]{1,0:T(8,128)(2,1)S(1)}, bf16[256,768]{1,0:T(8,128)(2,1)S(1)}, u32[]{:S(2)}, u32[]{:S(2)}) %collective-permute-start.4) | collective-permute-done | bytes 393248 | tf_op jit(solution)/shard_map/ppermute | solution.py:28
  14.1 0.0 collective-permute-start.5
  14.1 8.1 %collective-permute-done.part = bf16[272,768]{1,0:T(8,128)(2,1)S(1)} collective-permute-done((bf16[272,768]{1,0:T(8,128)(2,1)S(1)}, bf16[272,768]{1,0:T(8,128)(2,1)S(1)}, u32[]{:S(2)}, u32[]{:S(2)}) %collective-permute-start) | collective-permute-done | bytes 417824 | tf_op jit(solution)/shard_map/ppermute | solution.py:28
  22.2 0.0 collective-permute-start.9
  22.2 0.0 copy-done.6
  22.2 0.0 copy-done
  22.2 0.0 copy-done.3
  22.2 0.0 copy-done.5
  22.3 3.2 %shard_map.83 = (bf16[4,256,768]{2,1,0:T(8,128)(2,1)S(1)}, bf16[4,3,256,256]{3,2,1,0:T(8,128)(2,1)S(1)}, f32[200,128]{1,0:T(8,128)S(1)}, f32[200,128]{1,0:T(8,12...) custom-call(s32[2]{0:T(128)S(1)} %pad_add_fusion.place, s32[8]{0:T(128)S(1)} %copy-done.3, ...), custom_call_target="tpu_custom_call" | custom-call | flops 1207959552 | bytes 7110656 | tf_op jit(solution)/shard_map/pallas_call | solution.py:57
  25.5 1.9 %collective-permute-start.1 = (f32[200,128]{1,0:T(8,128)S(1)}, f32[200,128]{1,0:T(8,128)S(1)}, u32[]{:S(2)}, u32[]{:S(2)}) collective-permute-start(f32[200,128]{1,0:T(8,128)S(1)} %get-tuple-element.30), channel_id=1, source_target_pairs={{0,4},{4,0},{8,12},{12,8},{1,5},{5,1},{9,13},{13,9},{2,6},{6,2},{1... | collective-permute-start | bytes 307208 | tf_op jit(solution)/shard_map/ppermute | solution.py:374
  27.3 2.6 %collective-permute-start.2 = (f32[200,128]{1,0:T(8,128)S(1)}, f32[200,128]{1,0:T(8,128)S(1)}, u32[]{:S(2)}, u32[]{:S(2)}) collective-permute-start(f32[200,128]{1,0:T(8,128)S(1)} %get-tuple-element.31), channel_id=1, source_target_pairs={{0,8},{4,12},{8,0},{12,4},{1,9},{5,13},{9,1},{13,5},{2,10},{6,14},... | collective-permute-start | bytes 307208 | tf_op jit(solution)/shard_map/ppermute | solution.py:374
  29.9 0.0 collective-permute-start.3
  29.9 1.5 %shard_map.84 = (bf16[256,768]{1,0:T(8,128)(2,1)S(1)}, f32[3,128,128]{2,1,0:T(8,128)S(1)}) custom-call(s32[2]{0:T(128)S(1)} %pad_add_fusion.place, bf16[256,768]{1,0:T(8,128)(2,1)S(1)} %collective-permute-done.4.part, f32[1,768]{1,0:T(1,128)S(1)} %broadcast_in_dim.8.gain, bf16[768,384]{1,0:T(8,128)(2,1)S(1)} %copy-done, ...), custom_call_target="tpu_custom_call" | custom-call | flops 150994944 | bytes 1179648 | tf_op jit(solution)/shard_map/pallas_call | solution.py:57
  31.4 0.0 collective-permute-done.5.part
  31.5 1.5 %shard_map.85 = (bf16[256,768]{1,0:T(8,128)(2,1)S(1)}, f32[96,128]{1,0:T(8,128)S(1)}, f32[96,128]{1,0:T(8,128)S(1)}, f32[96,128]{1,0:T(8,128)S(1)}, f32[96,128]{1,0:T(8,128)S(1)}) custom-call(s32[2]{0:T(128)S(1)} %pad_add_fusion.place, bf16[256,768]{1,0:T(8,128)(2,1)S(1)} %collective-permute-done.5.part, f32[1,768]{1,0:T(1,128)S(1)} %broadcast_in_dim.8.gain, ...), custom_call_target="tpu_custom_call" | custom-call | flops 150994944 | bytes 1179648 | tf_op jit(solution)/shard_map/pallas_call | solution.py:57
  33.0 0.9 %collective-permute-start.6 = (f32[96,128]{1,0:T(8,128)S(1)}, f32[96,128]{1,0:T(8,128)S(1)}, u32[]{:S(2)}, u32[]{:S(2)}) collective-permute-start(f32[96,128]{1,0:T(8,128)S(1)} %get-tuple-element.36), channel_id=1, source_target_pairs={{0,4},{4,0},{8,12},{12,8},{1,5},{5,1},{9,13},{13,9},{2,6},{6,2},{1... | collective-permute-start | bytes 147464 | tf_op jit(solution)/shard_map/ppermute | solution.py:374
  33.9 1.5 %shard_map.86 = (bf16[256,768]{1,0:T(8,128)(2,1)S(1)}, f32[3,128,128]{2,1,0:T(8,128)S(1)}) custom-call(s32[2]{0:T(128)S(1)} %pad_add_fusion.place, bf16[272,768]{1,0:T(8,128)(2,1)S(1)} %collective-permute-done.part, f32[1,768]{1,0:T(1,128)S(1)} %broadcast_in_dim.8.gain, bf16[768,384]{1,0:T(8,128)(2,1)S(1)} %copy-done, ...), custom_call_target="tpu_custom_call" | custom-call | flops 150994944 | bytes 1179648 | tf_op jit(solution)/shard_map/pallas_call | solution.py:57
  35.5 0.0 collective-permute-done.9.part
  35.5 3.6 %collective-permute-start.7 = (f32[96,128]{1,0:T(8,128)S(1)}, f32[96,128]{1,0:T(8,128)S(1)}, u32[]{:S(2)}, u32[]{:S(2)}) collective-permute-start(f32[96,128]{1,0:T(8,128)S(1)} %get-tuple-element.37), channel_id=1, source_target_pairs={{0,8},{4,12},{8,0},{12,4},{1,9},{5,13},{9,1},{13,5},{2,10},{6,14},... | collective-permute-start | bytes 147464 | tf_op jit(solution)/shard_map/ppermute | solution.py:374
  39.0 1.5 %shard_map.87 = (bf16[256,768]{1,0:T(8,128)(2,1)S(1)}, f32[96,128]{1,0:T(8,128)S(1)}, f32[96,128]{1,0:T(8,128)S(1)}, f32[96,128]{1,0:T(8,128)S(1)}, f32[96,128]{1,0:T(8,128)S(1)}) custom-call(s32[2]{0:T(128)S(1)} %pad_add_fusion.place, bf16[272,768]{1,0:T(8,128)(2,1)S(1)} %collective-permute-done.9.part, f32[1,768]{1,0:T(1,128)S(1)} %broadcast_in_dim.8.gain, ...), custom_call_target="tpu_custom_call" | custom-call | flops 150994944 | bytes 1179648 | tf_op jit(solution)/shard_map/pallas_call | solution.py:57
  40.6 0.0 collective-permute-done.1.rest_3_
  40.6 0.1 collective-permute-start.8
  40.6 0.0 collective-permute-done.2.rest_4_
  40.7 0.6 collective-permute-start.10
  41.2 0.0 collective-permute-done.3.rest_5_
  41.2 3.8 %collective-permute-start.11 = (f32[96,128]{1,0:T(8,128)S(1)}, f32[96,128]{1,0:T(8,128)S(1)}, u32[]{:S(2)}, u32[]{:S(2)}) collective-permute-start(f32[96,128]{1,0:T(8,128)S(1)} %get-tuple-element.42), channel_id=1, source_target_pairs={{0,8},{4,12},{8,0},{12,4},{1,9},{5,13},{9,1},{13,5},{2,10},{6,14},... | collective-permute-start | bytes 147464 | tf_op jit(solution)/shard_map/ppermute | solution.py:374
  45.0 0.0 collective-permute-done.6.rest_7_
  45.0 0.1 collective-permute-start.12
  45.1 0.0 collective-permute-done.7.rest_8_
  45.1 1.4 %collective-permute-done.8.rest_9_ = f32[96,128]{1,0:T(8,128)S(1)} collective-permute-done((f32[96,128]{1,0:T(8,128)S(1)}, f32[96,128]{1,0:T(8,128)S(1)}, u32[]{:S(2)}, u32[]{:S(2)}) %collective-permute-start.8) | collective-permute-done | bytes 49184 | tf_op jit(solution)/shard_map/ppermute | solution.py:374
  46.5 0.0 collective-permute-done.10.rest_11_
  46.5 1.9 %collective-permute-done.11.rest_12_ = f32[96,128]{1,0:T(8,128)S(1)} collective-permute-done((f32[96,128]{1,0:T(8,128)S(1)}, f32[96,128]{1,0:T(8,128)S(1)}, u32[]{:S(2)}, u32[]{:S(2)}) %collective-permute-start.11) | collective-permute-done | bytes 49184 | tf_op jit(solution)/shard_map/ppermute | solution.py:374
  48.4 3.1 %collective-permute-done.12.rest_13_ = f32[96,128]{1,0:T(8,128)S(1)} collective-permute-done((f32[96,128]{1,0:T(8,128)S(1)}, f32[96,128]{1,0:T(8,128)S(1)}, u32[]{:S(2)}, u32[]{:S(2)}) %collective-permute-start.12) | collective-permute-done | bytes 49184 | tf_op jit(solution)/shard_map/ppermute | solution.py:374
  51.4 0.3 shard_map.88.rest_0_
  51.7 0.1 collective-permute-start.13
  51.8 0.5 collective-permute-start.14
  52.3 3.8 %collective-permute-start.15 = (bf16[192,256]{1,0:T(8,128)(2,1)S(1)}, bf16[192,256]{1,0:T(8,128)(2,1)S(1)}, u32[]{:S(2)}, u32[]{:S(2)}) collective-permute-start(bf16[192,256]{1,0:T(8,128)(2,1)S(1)} %shard_map.88.rest_0_), channel_id=1, source_target_pairs={{0,12},{4,8},{8,4},{12,0},{1,13},{5,9},{9,5},{13,1},{2,14},{6,10},... | collective-permute-start | bytes 294920 | tf_op jit(solution)/shard_map/ppermute | solution.py:374
  56.2 0.0 copy-done.1
  56.2 1.0 %shard_map.89.rest_4_ = bf16[4,3,128,256]{3,2,1,0:T(8,128)(2,1)S(1)} custom-call(bf16[4,256,768]{2,1,0:T(8,128)(2,1)S(1)} %get-tuple-element.44.normed, bf16[768,384]{1,0:T(8,128)(2,1)S(1)} %copy-done.1), custom_call_target="tpu_custom_call" | custom-call | flops 603979776 | bytes 1572864 | tf_op jit(solution)/shard_map/pallas_call | solution.py:57
  57.2 0.6 shard_map.90.rest_5_
  57.8 0.6 shard_map.91.rest_6_
  58.3 0.0 collective-permute-done.13.rest_1_
  58.3 0.0 collective-permute-done.14.rest_2_
  58.4 1.6 %collective-permute-done.15.rest_3_ = bf16[192,256]{1,0:T(8,128)(2,1)S(1)} collective-permute-done((bf16[192,256]{1,0:T(8,128)(2,1)S(1)}, bf16[192,256]{1,0:T(8,128)(2,1)S(1)}, u32[]{:S(2)}, u32[]{:S(2)}) %collective-permute-start.15) | collective-permute-done | bytes 98336 | tf_op jit(solution)/shard_map/ppermute | solution.py:374
  59.9 0.9 %shard_map.94.rest_0_ = bf16[4,128,384]{2,1,0:T(8,128)(2,1)S(1)} custom-call(s32[2]{0:T(128)S(1)} %pad_add_fusion.place, bf16[192,256]{1,0:T(8,128)(2,1)S(1)} %shard_map.88.rest_0_, bf16[192,256]{1,0:T(8,128)(2,1)S(1)} %collective-permute-done.13.rest_1_, bf16[192,256]{1,0:T(8,128)(2,1)S(1)} %collective-permute-done.14.rest_2_, ...), custom_call_target="tpu_custom_call" | custom-call | flops 201326592 | bytes 786432 | tf_op jit(solution)/shard_map/pallas_call | solution.py:57
  60.9 0.0 copy-start.2
  60.9 0.1 collective-permute-start.17
  60.9 0.9 %shard_map.92.rest_0_ = bf16[4,128,384]{2,1,0:T(8,128)(2,1)S(1)} custom-call(s32[2]{0:T(128)S(1)} %pad_add_fusion.place, bf16[192,256]{1,0:T(8,128)(2,1)S(1)} %shard_map.88.rest_0_, bf16[192,256]{1,0:T(8,128)(2,1)S(1)} %collective-permute-done.13.rest_1_, bf16[192,256]{1,0:T(8,128)(2,1)S(1)} %collective-permute-done.14.rest_2_, ...), custom_call_target="tpu_custom_call" | custom-call | flops 201326592 | bytes 786432 | tf_op jit(solution)/shard_map/pallas_call | solution.py:57
  61.9 0.6 collective-permute-start.16
  62.4 0.0 copy-done.2
  62.4 0.6 shard_map.93.rest_2_
  63.0 0.0 collective-permute-done.17.rest_1_
  63.1 1.1 %shard_map.95.rest_3_ = bf16[4,128,384]{2,1,0:T(8,128)(2,1)S(1)} custom-call(s32[8]{0:T(128)S(1)} %copy-done.3, bf16[4,128,384]{2,1,0:T(8,128)(2,1)S(1)} %shard_map.94.rest_0_, bf16[4,128,384]{2,1,0:T(8,128)(2,1)S(1)} %collective-permute-done.17.rest_1_, bf16[768,384]{1,0:T(8,128)(2,1)S(1)} %shard_map.93.rest_2_), custom_call_target="tpu_custom_call" | custom-call | flops 301989888 | bytes 786432 | tf_op jit(solution)/shard_map/pallas_call | solution.py:57
  64.2 0.0 collective-permute-done.16.rest_1_
  64.2 1.8 %shard_map.96 = bf16[8,128,384]{2,1,0:T(8,128)(2,1)} custom-call(s32[8]{0:T(128)S(1)} %copy-done.3, bf16[4,128,384]{2,1,0:T(8,128)(2,1)S(1)} %shard_map.92.rest_0_, bf16[4,128,384]{2,1,0:T(8,128)(2,1)S(1)} %collective-permute-done.16.rest_1_, bf16[768,384]{1,0:T(8,128)(2,1)S(1)} %shard_map.93.rest_2_, bf16[4,128,384]{2,1,0:T(8,128)(2,1)S(1)} %shard_map.95.rest_3_), custom_call_target="tpu_custom_call" | custom-call | flops 301989888 | bytes 1572864 | tf_op jit(solution)/shard_map/pallas_call | solution.py:57
  (6 shorter events, 0.0 us)
Async XLA Ops:
  0.0 22.2 %copy-start.6 = (f32[768]{0:T(1024)S(1)}, f32[768]{0:T(1024)}, u32[]{:S(2)}) copy-start(f32[768]{0:T(1024)} %param.9) | copy-start | bytes 9220
  0.0 22.2 %copy-start = (bf16[768,384]{1,0:T(8,128)(2,1)S(1)}, bf16[768,384]{1,0:T(8,128)(2,1)}, u32[]{:S(2)}) copy-start(bf16[768,384]{1,0:T(8,128)(2,1)} %w_key.9) | copy-start | bytes 1769476
  0.0 22.2 %copy-start.3 = (s32[8]{0:T(128)S(1)}, s32[8]{0:T(128)}, u32[]{:S(2)}) copy-start(s32[8]{0:T(128)} %live.5) | copy-start | bytes 100
  1.1 13.0 %collective-permute-start.4 = (bf16[256,768]{1,0:T(8,128)(2,1)S(1)}, bf16[256,768]{1,0:T(8,128)(2,1)S(1)}, u32[]{:S(2)}, u32[]{:S(2)}) collective-permute-start(bf16[256,768]{1,0:T(8,128)(2,1)S(1)} %bitcast.8), channel_id=1, source_target_pairs={{0,2},{2,0},{1,3},{3,1},{4,6},{6,4},{5,7},{7,5},{8,10},{10,8},{9,1... | collective-permute-start | bytes 1179656 | tf_op jit(solution)/shard_map/ppermute | solution.py:28
  4.2 0.7 copy-start.4
  4.9 17.4 %copy-start.5 = (bf16[768,384]{1,0:T(8,128)(2,1)S(1)}, bf16[768,384]{1,0:T(8,128)(2,1)}, u32[]{:S(2)}) copy-start(bf16[768,384]{1,0:T(8,128)(2,1)} %w_query.1) | copy-start | bytes 1769476
  7.1 15.1 %collective-permute-start = (bf16[272,768]{1,0:T(8,128)(2,1)S(1)}, bf16[272,768]{1,0:T(8,128)(2,1)S(1)}, u32[]{:S(2)}, u32[]{:S(2)}) collective-permute-start(bf16[272,768]{1,0:T(8,128)(2,1)S(1)} %get-tuple-element.27), channel_id=1, source_target_pairs={{0,2},{2,0},{1,3},{3,1},{4,6},{6,4},{5,7},{7,5},{8,10},{10,8},{9,1... | collective-permute-start | bytes 1253384 | tf_op jit(solution)/shard_map/ppermute | solution.py:28
  14.1 17.3 %collective-permute-start.5 = (bf16[256,768]{1,0:T(8,128)(2,1)S(1)}, bf16[256,768]{1,0:T(8,128)(2,1)S(1)}, u32[]{:S(2)}, u32[]{:S(2)}) collective-permute-start(bf16[256,768]{1,0:T(8,128)(2,1)S(1)} %collective-permute-done.4.part), channel_id=1, source_target_pairs={{0,1},{1,0},{2,3},{3,2},{4,5},{5,4},{6,7},{7,6},{8,9},{9,8},{10,11... | collective-permute-start | bytes 1179656 | tf_op jit(solution)/shard_map/ppermute | solution.py:28
  22.2 13.2 %collective-permute-start.9 = (bf16[272,768]{1,0:T(8,128)(2,1)S(1)}, bf16[272,768]{1,0:T(8,128)(2,1)S(1)}, u32[]{:S(2)}, u32[]{:S(2)}) collective-permute-start(bf16[272,768]{1,0:T(8,128)(2,1)S(1)} %collective-permute-done.part), channel_id=1, source_target_pairs={{0,1},{1,0},{2,3},{3,2},{4,5},{5,4},{6,7},{7,6},{8,9},{9,8},{10,11... | collective-permute-start | bytes 1253384 | tf_op jit(solution)/shard_map/ppermute | solution.py:28
  25.5 15.1 %collective-permute-start.1 = (f32[200,128]{1,0:T(8,128)S(1)}, f32[200,128]{1,0:T(8,128)S(1)}, u32[]{:S(2)}, u32[]{:S(2)}) collective-permute-start(f32[200,128]{1,0:T(8,128)S(1)} %get-tuple-element.30), channel_id=1, source_target_pairs={{0,4},{4,0},{8,12},{12,8},{1,5},{5,1},{9,13},{13,9},{2,6},{6,2},{1... | collective-permute-start | bytes 307208 | tf_op jit(solution)/shard_map/ppermute | solution.py:374
  27.3 13.3 %collective-permute-start.2 = (f32[200,128]{1,0:T(8,128)S(1)}, f32[200,128]{1,0:T(8,128)S(1)}, u32[]{:S(2)}, u32[]{:S(2)}) collective-permute-start(f32[200,128]{1,0:T(8,128)S(1)} %get-tuple-element.31), channel_id=1, source_target_pairs={{0,8},{4,12},{8,0},{12,4},{1,9},{5,13},{9,1},{13,5},{2,10},{6,14},... | collective-permute-start | bytes 307208 | tf_op jit(solution)/shard_map/ppermute | solution.py:374
  29.9 11.3 %collective-permute-start.3 = (f32[200,128]{1,0:T(8,128)S(1)}, f32[200,128]{1,0:T(8,128)S(1)}, u32[]{:S(2)}, u32[]{:S(2)}) collective-permute-start(f32[200,128]{1,0:T(8,128)S(1)} %get-tuple-element.32), channel_id=1, source_target_pairs={{0,12},{4,8},{8,4},{12,0},{1,13},{5,9},{9,5},{13,1},{2,14},{6,10},... | collective-permute-start | bytes 307208 | tf_op jit(solution)/shard_map/ppermute | solution.py:374
  33.0 12.0 %collective-permute-start.6 = (f32[96,128]{1,0:T(8,128)S(1)}, f32[96,128]{1,0:T(8,128)S(1)}, u32[]{:S(2)}, u32[]{:S(2)}) collective-permute-start(f32[96,128]{1,0:T(8,128)S(1)} %get-tuple-element.36), channel_id=1, source_target_pairs={{0,4},{4,0},{8,12},{12,8},{1,5},{5,1},{9,13},{13,9},{2,6},{6,2},{1... | collective-permute-start | bytes 147464 | tf_op jit(solution)/shard_map/ppermute | solution.py:374
  35.5 9.7 %collective-permute-start.7 = (f32[96,128]{1,0:T(8,128)S(1)}, f32[96,128]{1,0:T(8,128)S(1)}, u32[]{:S(2)}, u32[]{:S(2)}) collective-permute-start(f32[96,128]{1,0:T(8,128)S(1)} %get-tuple-element.37), channel_id=1, source_target_pairs={{0,8},{4,12},{8,0},{12,4},{1,9},{5,13},{9,1},{13,5},{2,10},{6,14},... | collective-permute-start | bytes 147464 | tf_op jit(solution)/shard_map/ppermute | solution.py:374
  39.0 17.2 %copy-start.1 = (bf16[768,384]{1,0:T(8,128)(2,1)S(1)}, bf16[768,384]{1,0:T(8,128)(2,1)}, u32[]{:S(2)}) copy-start(bf16[768,384]{1,0:T(8,128)(2,1)} %refs_2_.3) | copy-start | bytes 1769476
  40.6 6.0 %collective-permute-start.8 = (f32[96,128]{1,0:T(8,128)S(1)}, f32[96,128]{1,0:T(8,128)S(1)}, u32[]{:S(2)}, u32[]{:S(2)}) collective-permute-start(f32[96,128]{1,0:T(8,128)S(1)} %get-tuple-element.38), channel_id=1, source_target_pairs={{0,12},{4,8},{8,4},{12,0},{1,13},{5,9},{9,5},{13,1},{2,14},{6,10},... | collective-permute-start | bytes 147464 | tf_op jit(solution)/shard_map/ppermute | solution.py:374
  40.7 5.9 %collective-permute-start.10 = (f32[96,128]{1,0:T(8,128)S(1)}, f32[96,128]{1,0:T(8,128)S(1)}, u32[]{:S(2)}, u32[]{:S(2)}) collective-permute-start(f32[96,128]{1,0:T(8,128)S(1)} %get-tuple-element.41), channel_id=1, source_target_pairs={{0,4},{4,0},{8,12},{12,8},{1,5},{5,1},{9,13},{13,9},{2,6},{6,2},{1... | collective-permute-start | bytes 147464 | tf_op jit(solution)/shard_map/ppermute | solution.py:374
  41.2 7.2 %collective-permute-start.11 = (f32[96,128]{1,0:T(8,128)S(1)}, f32[96,128]{1,0:T(8,128)S(1)}, u32[]{:S(2)}, u32[]{:S(2)}) collective-permute-start(f32[96,128]{1,0:T(8,128)S(1)} %get-tuple-element.42), channel_id=1, source_target_pairs={{0,8},{4,12},{8,0},{12,4},{1,9},{5,13},{9,1},{13,5},{2,10},{6,14},... | collective-permute-start | bytes 147464 | tf_op jit(solution)/shard_map/ppermute | solution.py:374
  45.0 6.4 %collective-permute-start.12 = (f32[96,128]{1,0:T(8,128)S(1)}, f32[96,128]{1,0:T(8,128)S(1)}, u32[]{:S(2)}, u32[]{:S(2)}) collective-permute-start(f32[96,128]{1,0:T(8,128)S(1)} %get-tuple-element.43), channel_id=1, source_target_pairs={{0,12},{4,8},{8,4},{12,0},{1,13},{5,9},{9,5},{13,1},{2,14},{6,10},... | collective-permute-start | bytes 147464 | tf_op jit(solution)/shard_map/ppermute | solution.py:374
  51.7 6.6 %collective-permute-start.13 = (bf16[192,256]{1,0:T(8,128)(2,1)S(1)}, bf16[192,256]{1,0:T(8,128)(2,1)S(1)}, u32[]{:S(2)}, u32[]{:S(2)}) collective-permute-start(bf16[192,256]{1,0:T(8,128)(2,1)S(1)} %shard_map.88.rest_0_), channel_id=1, source_target_pairs={{0,4},{4,0},{8,12},{12,8},{1,5},{5,1},{9,13},{13,9},{2,6},{6,2},{1... | collective-permute-start | bytes 294920 | tf_op jit(solution)/shard_map/ppermute | solution.py:374
  51.8 6.5 %collective-permute-start.14 = (bf16[192,256]{1,0:T(8,128)(2,1)S(1)}, bf16[192,256]{1,0:T(8,128)(2,1)S(1)}, u32[]{:S(2)}, u32[]{:S(2)}) collective-permute-start(bf16[192,256]{1,0:T(8,128)(2,1)S(1)} %shard_map.88.rest_0_), channel_id=1, source_target_pairs={{0,8},{4,12},{8,0},{12,4},{1,9},{5,13},{9,1},{13,5},{2,10},{6,14},... | collective-permute-start | bytes 294920 | tf_op jit(solution)/shard_map/ppermute | solution.py:374
  52.3 7.6 %collective-permute-start.15 = (bf16[192,256]{1,0:T(8,128)(2,1)S(1)}, bf16[192,256]{1,0:T(8,128)(2,1)S(1)}, u32[]{:S(2)}, u32[]{:S(2)}) collective-permute-start(bf16[192,256]{1,0:T(8,128)(2,1)S(1)} %shard_map.88.rest_0_), channel_id=1, source_target_pairs={{0,12},{4,8},{8,4},{12,0},{1,13},{5,9},{9,5},{13,1},{2,14},{6,10},... | collective-permute-start | bytes 294920 | tf_op jit(solution)/shard_map/ppermute | solution.py:374
  60.9 1.6 %copy-start.2 = (bf16[768,384]{1,0:T(8,128)(2,1)S(1)}, bf16[768,384]{1,0:T(8,128)(2,1)}, u32[]{:S(2)}) copy-start(bf16[768,384]{1,0:T(8,128)(2,1)} %w_out.1) | copy-start | bytes 1769476
  60.9 2.2 %collective-permute-start.17 = (bf16[4,128,384]{2,1,0:T(8,128)(2,1)S(1)}, bf16[4,128,384]{2,1,0:T(8,128)(2,1)S(1)}, u32[]{:S(2)}, u32[]{:S(2)}) collective-permute-start(bf16[4,128,384]{2,1,0:T(8,128)(2,1)S(1)} %shard_map.94.rest_0_), channel_id=1, source_target_pairs={{0,1},{1,0},{2,3},{3,2},{4,5},{5,4},{6,7},{7,6},{8,9},{9,8},{10,11... | collective-permute-start | bytes 1179656 | tf_op jit(solution)/shard_map/ppermute | solution.py:28
  61.9 2.3 %collective-permute-start.16 = (bf16[4,128,384]{2,1,0:T(8,128)(2,1)S(1)}, bf16[4,128,384]{2,1,0:T(8,128)(2,1)S(1)}, u32[]{:S(2)}, u32[]{:S(2)}) collective-permute-start(bf16[4,128,384]{2,1,0:T(8,128)(2,1)S(1)} %shard_map.92.rest_0_), channel_id=1, source_target_pairs={{0,1},{1,0},{2,3},{3,2},{4,5},{5,4},{6,7},{7,6},{8,9},{9,8},{10,11... | collective-permute-start | bytes 1179656 | tf_op jit(solution)/shard_map/ppermute | solution.py:28

commit v2 on v1

--- a/solution.py
+++ b/solution.py
@@ -76,11 +76,12 @@
     return (centred * lax.rsqrt(spread + 1e-05) * gain).astype(BF16)
 
 
-def load_kernel(place, valid, rows_in, resident, *rest, part_cols):
-    last, sems = rest
+def load_kernel(place, valid, rows_in, resident, last, flags, sems, *, part_cols):
     part_rows = (last.shape[0] - PAD) // part_cols
-    cols = rows_in.shape[1]
+    rows_here, cols, _ = resident.shape
     begin = place[1] * part_rows
+    first = pltpu.make_async_copy(valid, flags, sems.at[part_rows + rows_here])
+    first.start()
     copies = [
         pltpu.make_async_copy(
             rows_in.at[begin + r, pl.ds(cols - part_cols, part_cols), :],
@@ -89,12 +90,15 @@
         )
         for r in range(part_rows)
     ]
-    copies.append(pltpu.make_async_copy(rows_in, resident, sems.at[part_rows]))
+    for r in range(rows_here):
+        sem = sems.at[part_rows + r]
+        copies.append(pltpu.make_async_copy(rows_in.at[r], resident.at[r], sem))
     for copy in copies:
         copy.start()
+    first.wait()
     tail = last.shape[0] - PAD
     last[tail:, :] = jnp.zeros((PAD, last.shape[1]), BF16)
-    last[tail:, 0:cols] = jnp.broadcast_to(valid[...].astype(F32), (PAD, cols)).astype(BF16)
+    last[tail:, 0:cols] = jnp.broadcast_to(flags[...].astype(F32), (PAD, cols)).astype(BF16)
     for copy in copies:
         copy.wait()
 
@@ -124,12 +128,14 @@
     _, cols, width = rows_in.shape
     low = lax.broadcasted_iota(jnp.int32, (cols, LANES), 1) < LANES // 2
     zero = jnp.zeros((cols, LANES), BF16)
+    local = w_query.shape[1]
+    weights = jnp.concatenate([w_query[...], w_key[...]], axis=1)
     for g in range(groups):
         rows = rows_in[g * SIZE : (g + 1) * SIZE].reshape(SIZE * cols, width)
         normed = normed_rows(rows, gain[...])
         normed_out[g] = normed
-        query = dot(normed, w_query[...])
-        key = dot(normed, w_key[...]).astype(BF16)
+        both_sides = dot(normed, weights)
+        query, key = both_sides[:, :local], both_sides[:, local:].astype(BF16)
         for r in range(SIZE):
             scale = live[g * SIZE + r].astype(F32)
             piece = (query[r * cols : (r + 1) * cols] * scale).astype(BF16)
@@ -210,49 +216,97 @@
     return total
 
 
-def soft_kernel(*rest, shards, offsets, heads, head_width):
-    valid, rest = rest[: 1 + offsets], rest[1 + offsets :]
-    probs = rest[-1]
-    tiles = 1 + offsets * CHUNKS
-    sums = [added(rest[t * shards : (t + 1) * shards]) for t in range(tiles)]
-    part = probs.shape[0] // heads
-    factor = lax.rsqrt(F32(head_width) * sums[0][heads * part : heads * part + 1, 0:1])
+def own_soft_kernel(valid, *rest, heads, head_width):
+    pieces, probs, stats = rest[:-2], rest[-2], rest[-1]
+    total = added(pieces)
+    rows = probs.shape[0]
+    factor = lax.rsqrt(F32(head_width) * total[rows : rows + 1, 0:1])
+    mask = jnp.broadcast_to(valid[...] > 0.5, (rows, LANES))
+    scaled = jnp.where(mask, total[:rows] * factor, LOWEST)
+    top = jnp.max(scaled, axis=-1, keepdims=True)
+    expo = jnp.where(mask, jnp.exp(scaled - top), 0.0)
+    whole = jnp.sum(expo, axis=-1, keepdims=True)
+    probs[...] = expo.astype(BF16)
+    stats[0] = jnp.broadcast_to(top, (rows, LANES))
+    stats[1] = jnp.broadcast_to(whole, (rows, LANES))
+    stats[2] = jnp.broadcast_to(factor, (rows, LANES))
+
+
+def diagonal(rows):
+    row = lax.broadcasted_iota(jnp.int32, (rows, LANES), 0)
+    return row == lax.broadcasted_iota(jnp.int32, (rows, LANES), 1)
+
+
+def last_soft_kernel(*rest, shards, offsets, heads):
+    valid, stats, probs = rest[:offsets], rest[offsets], rest[-1]
+    rest = rest[offsets + 1 : -1]
+    sums = [added(rest[t * shards : (t + 1) * shards]) for t in range(offsets * CHUNKS)]
+    rows = stats.shape[1]
+    part = rows // heads
     low = lax.broadcasted_iota(jnp.int32, (part, LANES), 1) < LANES // 2
-    blocks = 1 + offsets
-    masks = [
-        jnp.broadcast_to(valid[b][...] > 0.5, (part, LANES)) for b in range(blocks)
-    ]
-    for h in range(heads):
-        pieces = [sums[0][h * part : (h + 1) * part]]
-        at = slice(h // 2 * part, (h // 2 + 1) * part)
-        for o in range(offsets):
-            first, second = sums[1 + o * CHUNKS][at], sums[2 + o * CHUNKS][at]
+    old, own, factor = stats[0], stats[1], stats[2]
+    masks, scaled = [], []
+    for o in range(offsets):
+        pieces = []
+        for h in range(heads):
+            at = slice(h // 2 * part, (h // 2 + 1) * part)
+            first, second = sums[o * CHUNKS][at], sums[o * CHUNKS + 1][at]
             if h % 2 == 0:
                 pieces.append(jnp.where(low, first, second))
             else:
                 pieces.append(pltpu.roll(jnp.where(low, second, first), LANES // 2, 1))
-        scaled = [jnp.where(masks[b], pieces[b] * factor, LOWEST) for b in range(blocks)]
-        top = jnp.max(functools.reduce(jnp.maximum, scaled), axis=-1, keepdims=True)
-        expo = [jnp.where(masks[b], jnp.exp(scaled[b] - top), 0.0) for b in range(blocks)]
-        whole = jnp.sum(functools.reduce(jnp.add, expo), axis=-1, keepdims=True)
-        for b in range(blocks):
-            probs[h * part : (h + 1) * part, b * LANES : (b + 1) * LANES] = (
-                expo[b] / whole
-            ).astype(BF16)
-
-
-def mix_kernel(place, *rest, shards, side, cores, offsets):
-    own = rest[shards]
-    remote = rest[shards + 1 : shards + 1 + offsets * CHUNKS]
-    out, probs = rest[shards + 1 + offsets * CHUNKS :]
+        masks.append(jnp.broadcast_to(valid[o][...] > 0.5, (rows, LANES)))
+        piece = jnp.concatenate(pieces, axis=0)
+        scaled.append(jnp.where(masks[o], piece * factor, LOWEST))
+    highest = jnp.max(functools.reduce(jnp.maximum, scaled), axis=-1, keepdims=True)
+    top = jnp.maximum(old, highest)
+    expo = [jnp.where(masks[o], jnp.exp(scaled[o] - top), 0.0) for o in range(offsets)]
+    extra = jnp.sum(functools.reduce(jnp.add, expo), axis=-1, keepdims=True)
+    shift = jnp.exp(old - top)
+    whole = shift * own + extra
+    for o in range(offsets):
+        probs[0:rows, o * LANES : (o + 1) * LANES] = (expo[o] / whole).astype(BF16)
+    scale = shift / whole
+    kept = diagonal(part)
+    lines = []
+    for h in range(heads):
+        block = jnp.where(kept, scale[h * part : (h + 1) * part], 0.0)
+        lines.append(jnp.sum(block, axis=0, keepdims=True))
+    lines = jnp.concatenate(lines + [jnp.zeros((8 - heads, LANES), F32)], axis=0)
+    coarse = lines.astype(BF16).astype(F32)
+    tail = jnp.concatenate([coarse, lines - coarse], axis=0)
+    probs[rows:, 0:LANES] = tail.astype(BF16)
+
+
+def collect(place, owns, others, probs, heads):
+    rows = owns[0].shape[0]
+    part = rows // heads
+    cols = probs.shape[1] // 2
+    kept = diagonal(part)
+    for k in range(len(owns)):
+        begin = lax.bitwise_xor(place[0], k) * part
+        tail = others[k][rows:, 0:LANES].astype(F32)
+        lines = tail[0:8] + tail[8:16]
+        for head in range(heads):
+            at = pl.ds(pl.multiple_of(head % 2 * cols + begin, part), part)
+            mine = slice(head * part, (head + 1) * part)
+            line = jnp.where(kept, jnp.broadcast_to(lines[head : head + 1], (part, LANES)), 0.0)
+            scale = jnp.sum(line, axis=-1, keepdims=True)
+            own = owns[k][mine, :].astype(F32) * scale
+            probs[head // 2, at, 0:LANES] = own.astype(BF16)
+            probs[head // 2, at, LANES:] = others[k][mine, :]
+
+
+def mix_kernel(place, *rest, side, cores, tiles, shards, heads):
+    if shards:
+        rest, probs = rest[:-1], rest[-1]
+        collect(place, rest[:shards], rest[shards : 2 * shards], probs, heads)
+        rest = rest[2 * shards :]
+    else:
+        probs, rest = rest[0], rest[1:]
+    own, remote, out = rest[0], rest[1 : 1 + tiles], rest[1 + tiles]
     _, pairs, cols, lanes = own.shape
     inner = out.shape[0] // SIZE
-    part = cols // shards
-    for k in range(shards):
-        begin = lax.bitwise_xor(place[0], k) * part
-        for head in range(2 * pairs):
-            at = pl.multiple_of(head % 2 * cols + begin, part)
-            probs[head // 2, pl.ds(at, part), :] = rest[k][head * part : (head + 1) * part, :]
     lane = lax.broadcasted_iota(jnp.int32, (cols, lanes), 1)
     low = lax.rem(lane, LANES) < LANES // 2
     step = lax.rem(place[1] + cores - side, cores)
@@ -347,18 +401,18 @@
     first = lax.dynamic_slice(
         alignment, (core * part_rows, 0, 0), (part_rows, cols_here - part_cols, width)
     )
-    sent = [
-        first[:, c * part_cols : (c + 1) * part_cols].reshape(part_rows * part_cols, width)
-        for c in range(CHUNKS - 1)
-    ]
+    sent = [first.reshape(part_rows * part_cols, width)]
     resident, last_chunk = call(
         functools.partial(load_kernel, part_cols=part_cols),
         [
             shape((rows_here, cols_here, width), BF16),
             shape((part_rows * part_cols + PAD, width), BF16),
         ],
-        [spec(SMEM), spec(), spec(HBM)],
-        [pltpu.SemaphoreType.DMA((part_rows + 1,))],
+        [spec(SMEM), spec(HBM), spec(HBM)],
+        [
+            pltpu.VMEM((1, cols_here), jnp.int32),
+            pltpu.SemaphoreType.DMA((part_rows + rows_here + 1,)),
+        ],
     )(place, col_valid[None, :], alignment)
     sent.append(last_chunk)
     arrived = {}
@@ -443,19 +497,24 @@
         valid_tiles.append(arrived[offset, CHUNKS - 1][0][-PAD : 1 - PAD, :cols_here])
     if direct:
         valid = [tile.astype(F32) for tile in valid_tiles]
+        rows = local_heads * part
+        own_probs, stats = call(
+            functools.partial(own_soft_kernel, heads=local_heads, head_width=head_width),
+            [shape((rows, LANES), BF16), shape((3, rows, LANES), F32)],
+            [spec()] * (1 + shards),
+            flops=1000000,
+        )(valid[0], *own_sums)
+        own_probs = exchange([own_probs] * shards)
         probs = call(
             functools.partial(
-                soft_kernel,
-                shards=shards,
-                offsets=offsets,
-                heads=local_heads,
-                head_width=head_width,
+                last_soft_kernel, shards=shards, offsets=offsets, heads=local_heads
             ),
-            shape((local_heads * part, total_cols), BF16),
-            [spec()] * (1 + offsets + shards * (1 + len(tiles))),
+            shape((rows + PAD, offsets * LANES), BF16),
+            [spec()] * (1 + offsets + shards * len(tiles)),
             flops=1000000,
-        )(*valid, *own_sums, *[piece for tile in tiles for piece in tile])
+        )(*valid[1:], stats, *[piece for tile in tiles for piece in tile])
         probs = exchange([probs] * shards)
+        probs = own_probs + probs
     else:
         count = lax.psum(jnp.sum(row_mask.astype(F32)), "depth")
         own_part = own_sums[0][: local_heads * cols_here]
@@ -472,19 +531,28 @@
         expo = jnp.where(mask, jnp.exp(scaled - jnp.max(scaled, axis=-1, keepdims=True)), 0.0)
         probs = (expo / jnp.sum(expo, axis=-1, keepdims=True)).astype(BF16)
         probs = lax.all_gather(probs, "depth", axis=1, tiled=True)
-        probs = [probs.reshape(local_heads * cols_here, total_cols)]
+        probs = [probs.reshape(pairs, 2 * cols_here, total_cols)]
 
     finished = []
     for side in range(cores):
-        mine = call(
+        gathers = len(probs) // 2
+        outs = [shape((part_rows, cols_here, local_width), BF16)]
+        if gathers:
+            outs.append(shape((pairs, 2 * cols_here, total_cols), BF16))
+        mixed = call(
             functools.partial(
-                mix_kernel, shards=shards, side=side, cores=cores, offsets=offsets
+                mix_kernel,
+                side=side,
+                cores=cores,
+                tiles=len(tiles),
+                shards=gathers,
+                heads=local_heads,
             ),
-            shape((part_rows, cols_here, local_width), BF16),
-            [spec(SMEM)] + [spec()] * (shards + 1 + len(remote_values)),
-            [pltpu.VMEM((pairs, 2 * cols_here, total_cols), BF16)],
+            outs,
+            [spec(SMEM)] + [spec()] * (len(probs) + 1 + len(remote_values)),
             flops=4 * part_rows * cols_here * total_cols * local_width,
         )(place, *probs, own_values, *remote_values)
+        mine, probs = mixed[0], mixed[1:] if gathers else probs
         parts = [mine] + [from_behind(mine, "heads", k) for k in range(1, cores)]
         if side + 1 < cores:
             finished.append(

time: 66.2 us -> 72.5 us (1.095)
  starting transfers between devices: 21.7 us -> 29 us
    ppermute x12 -> x15, starting transfers between devices: 18 us -> 25.3 us  [exchange(): received.append(lax.ppermute(values[k], 'depth', swapped))]
    ppermute x12 -> x15, waiting for transfers between devices: 7.91 us -> 6.83 us  [exchange(): received.append(lax.ppermute(values[k], 'depth', swapped))]
    pallas_call x15 -> x16, Pallas kernels: 19.2 us -> 19.3 us  [run(): out = fn(*args)]
  transfers between devices with their start and end apart: 18 -> 21, of which waited for: 6 -> 6; matrix products, arithmetic and copies ran while one was open for 0% -> 0% of each run, Pallas kernels for 25% -> 23%
where the time goes in v2:
time: 72.5 us; the launch traced here: 72.3 us
  starting transfers between devices  29 us (40%)
  waiting for transfers between devices  22.5 us (31%)
  Pallas kernels  19.3 us (27%)
  local copies, waits for them, and re-layouts  1.16 us (2%)
    ppermute x15, starting transfers between devices, exchange(): received.append(lax.ppermute(values[k], 'depth', swapped))  25.3 us
    pallas_call x16, Pallas kernels, run(): out = fn(*args)  19.3 us
    ppermute x6, waiting for transfers between devices, from_behind(): lax.ppermute(value, axis, [(s, (s + steps) % count) for s in range(count)])  15.7 us
    ppermute x15, waiting for transfers between devices, exchange(): received.append(lax.ppermute(values[k], 'depth', swapped))  6.83 us
    ppermute x6, starting transfers between devices, from_behind(): lax.ppermute(value, axis, [(s, (s + steps) % count) for s in range(count)])  3.77 us
  transfers between devices with their start and end apart: 21, of which 6 were waited for; matrix products, arithmetic and copies ran while one was open for 0% of the time, Pallas kernels for 23%

profile of v2, /device:TPU:0, one launch (start us, length us, event | category | flops | bytes accessed | tf_op | source)
XLA Modules:
  0.0 72.3 jit_solution(17057716036708099208)
XLA Ops:
  0.0 1.1 %constant_dynamic-slice_fusion = bf16[4,64,768]{2,1,0:T(8,128)(2,1)S(1)} fusion(bf16[8,128,768]{2,1,0:T(8,128)(2,1)} %rows_in.1, s32[]{:T(128)S(6)} %select_n.3), kind=kLoop, calls=%fused_computation.3 | loop fusion | bytes 786436 | tf_op jit(solution)/shard_map/dynamic_slice | solution.py:401
  1.1 3.0 %collective-permute-start.7 = (bf16[256,768]{1,0:T(8,128)(2,1)S(1)}, bf16[256,768]{1,0:T(8,128)(2,1)S(1)}, u32[]{:S(2)}, u32[]{:S(2)}) collective-permute-start(bf16[256,768]{1,0:T(8,128)(2,1)S(1)} %bitcast.7), channel_id=1, source_target_pairs={{0,2},{2,0},{1,3},{3,1},{4,6},{6,4},{5,7},{7,5},{8,10},{10,8},{9,1... | collective-permute-start | bytes 1179656 | tf_op jit(solution)/shard_map/ppermute | solution.py:28
  4.2 0.1 pad_add_fusion.place
  4.3 2.2 %shard_map.82 = (bf16[8,128,768]{2,1,0:T(8,128)(2,1)S(1)}, bf16[272,768]{1,0:T(8,128)(2,1)S(1)}) custom-call(s32[2]{0:T(128)S(1)} %pad_add_fusion.place, s32[1,128]{1,0:T(1,128)} %bitcast.8, bf16[8,128,768]{2,1,0:T(8,128)(2,1)} %rows_in.1), custom_call_target="tpu_custom_call" | custom-call | bytes 3981312 | tf_op jit(solution)/shard_map/pallas_call | solution.py:57
  6.5 0.1 collective-permute-start.6
  6.6 7.6 %collective-permute-done.7.part = bf16[256,768]{1,0:T(8,128)(2,1)S(1)} collective-permute-done((bf16[256,768]{1,0:T(8,128)(2,1)S(1)}, bf16[256,768]{1,0:T(8,128)(2,1)S(1)}, u32[]{:S(2)}, u32[]{:S(2)}) %collective-permute-start.7) | collective-permute-done | bytes 393248 | tf_op jit(solution)/shard_map/ppermute | solution.py:28
  14.1 0.0 collective-permute-start.8
  14.2 0.0 copy-done.5
  14.2 8.1 %collective-permute-done.6.part = bf16[272,768]{1,0:T(8,128)(2,1)S(1)} collective-permute-done((bf16[272,768]{1,0:T(8,128)(2,1)S(1)}, bf16[272,768]{1,0:T(8,128)(2,1)S(1)}, u32[]{:S(2)}, u32[]{:S(2)}) %collective-permute-start.6) | collective-permute-done | bytes 417824 | tf_op jit(solution)/shard_map/ppermute | solution.py:28
  22.3 0.0 collective-permute-start.12
  22.3 0.0 copy-done.4
  22.3 0.0 copy-start.6
  22.3 2.9 %shard_map.83 = (bf16[4,256,768]{2,1,0:T(8,128)(2,1)S(1)}, bf16[4,3,256,256]{3,2,1,0:T(8,128)(2,1)S(1)}, f32[200,128]{1,0:T(8,128)S(1)}, f32[200,128]{1,0:T(8,12...) custom-call(s32[2]{0:T(128)S(1)} %pad_add_fusion.place, s32[8]{0:T(128)S(1)} %copy-done.3, ...), custom_call_target="tpu_custom_call" | custom-call | flops 1207959552 | bytes 7110656 | tf_op jit(solution)/shard_map/pallas_call | solution.py:57
  25.2 1.9 %collective-permute-start = (f32[200,128]{1,0:T(8,128)S(1)}, f32[200,128]{1,0:T(8,128)S(1)}, u32[]{:S(2)}, u32[]{:S(2)}) collective-permute-start(f32[200,128]{1,0:T(8,128)S(1)} %get-tuple-element.33), channel_id=1, source_target_pairs={{0,4},{4,0},{8,12},{12,8},{1,5},{5,1},{9,13},{13,9},{2,6},{6,2},{1... | collective-permute-start | bytes 307208 | tf_op jit(solution)/shard_map/ppermute | solution.py:428
  27.1 2.6 %collective-permute-start.1 = (f32[200,128]{1,0:T(8,128)S(1)}, f32[200,128]{1,0:T(8,128)S(1)}, u32[]{:S(2)}, u32[]{:S(2)}) collective-permute-start(f32[200,128]{1,0:T(8,128)S(1)} %get-tuple-element.34), channel_id=1, source_target_pairs={{0,8},{4,12},{8,0},{12,4},{1,9},{5,13},{9,1},{13,5},{2,10},{6,14},... | collective-permute-start | bytes 307208 | tf_op jit(solution)/shard_map/ppermute | solution.py:428
  29.7 0.0 collective-permute-start.2
  29.7 1.5 %shard_map.85 = (bf16[256,768]{1,0:T(8,128)(2,1)S(1)}, f32[3,128,128]{2,1,0:T(8,128)S(1)}) custom-call(s32[2]{0:T(128)S(1)} %pad_add_fusion.place, bf16[256,768]{1,0:T(8,128)(2,1)S(1)} %collective-permute-done.7.part, f32[1,768]{1,0:T(1,128)S(1)} %broadcast_in_dim.8.gain, bf16[768,384]{1,0:T(8,128)(2,1)S(1)} %copy-done, ...), custom_call_target="tpu_custom_call" | custom-call | flops 150994944 | bytes 1179648 | tf_op jit(solution)/shard_map/pallas_call | solution.py:57
  31.2 0.0 collective-permute-done.8.part
  31.2 1.5 %shard_map.86 = (bf16[256,768]{1,0:T(8,128)(2,1)S(1)}, f32[96,128]{1,0:T(8,128)S(1)}, f32[96,128]{1,0:T(8,128)S(1)}, f32[96,128]{1,0:T(8,128)S(1)}, f32[96,128]{1,0:T(8,128)S(1)}) custom-call(s32[2]{0:T(128)S(1)} %pad_add_fusion.place, bf16[256,768]{1,0:T(8,128)(2,1)S(1)} %collective-permute-done.8.part, f32[1,768]{1,0:T(1,128)S(1)} %broadcast_in_dim.8.gain, ...), custom_call_target="tpu_custom_call" | custom-call | flops 150994944 | bytes 1179648 | tf_op jit(solution)/shard_map/pallas_call | solution.py:57
  32.8 2.0 %collective-permute-start.10 = (f32[96,128]{1,0:T(8,128)S(1)}, f32[96,128]{1,0:T(8,128)S(1)}, u32[]{:S(2)}, u32[]{:S(2)}) collective-permute-start(f32[96,128]{1,0:T(8,128)S(1)} %get-tuple-element.43), channel_id=1, source_target_pairs={{0,8},{4,12},{8,0},{12,4},{1,9},{5,13},{9,1},{13,5},{2,10},{6,14},... | collective-permute-start | bytes 147464 | tf_op jit(solution)/shard_map/ppermute | solution.py:428
  34.7 0.0 collective-permute-done.rest_1_
  34.7 2.0 %collective-permute-start.11 = (f32[96,128]{1,0:T(8,128)S(1)}, f32[96,128]{1,0:T(8,128)S(1)}, u32[]{:S(2)}, u32[]{:S(2)}) collective-permute-start(f32[96,128]{1,0:T(8,128)S(1)} %get-tuple-element.44), channel_id=1, source_target_pairs={{0,12},{4,8},{8,4},{12,0},{1,13},{5,9},{9,5},{13,1},{2,14},{6,10},... | collective-permute-start | bytes 147464 | tf_op jit(solution)/shard_map/ppermute | solution.py:428
  36.7 1.0 %shard_map.90.rest_8_.rest_1_ = bf16[4,3,128,256]{3,2,1,0:T(8,128)(2,1)S(1)} custom-call(bf16[4,256,768]{2,1,0:T(8,128)(2,1)S(1)} %get-tuple-element.50.normed, bf16[768,384]{1,0:T(8,128)(2,1)S(1)} %copy-done.1), custom_call_target="tpu_custom_call" | custom-call | flops 603979776 | bytes 1572864 | tf_op jit(solution)/shard_map/pallas_call | solution.py:57
  37.7 2.0 %collective-permute-done.1.rest_2_ = f32[200,128]{1,0:T(8,128)S(1)} collective-permute-done((f32[200,128]{1,0:T(8,128)S(1)}, f32[200,128]{1,0:T(8,128)S(1)}, u32[]{:S(2)}, u32[]{:S(2)}) %collective-permute-start.1) | collective-permute-done | bytes 102432 | tf_op jit(solution)/shard_map/ppermute | solution.py:428
  39.7 0.0 collective-permute-done.2.rest_3_
  39.7 0.2 shard_map.84
  40.0 3.3 %collective-permute-start.3 = (bf16[192,128]{1,0:T(8,128)(2,1)S(1)}, bf16[192,128]{1,0:T(8,128)(2,1)S(1)}, u32[]{:S(2)}, u32[]{:S(2)}) collective-permute-start(bf16[192,128]{1,0:T(8,128)(2,1)S(1)} %get-tuple-element.36.rest_0_), channel_id=1, source_target_pairs={{0,4},{4,0},{8,12},{12,8},{1,5},{5,1},{9,13},{13,9},{2,6},{6,2},{1... | collective-permute-start | bytes 147464 | tf_op jit(solution)/shard_map/ppermute | solution.py:428
  43.3 1.5 %shard_map.87 = (bf16[256,768]{1,0:T(8,128)(2,1)S(1)}, f32[3,128,128]{2,1,0:T(8,128)S(1)}) custom-call(s32[2]{0:T(128)S(1)} %pad_add_fusion.place, bf16[272,768]{1,0:T(8,128)(2,1)S(1)} %collective-permute-done.6.part, f32[1,768]{1,0:T(1,128)S(1)} %broadcast_in_dim.8.gain, bf16[768,384]{1,0:T(8,128)(2,1)S(1)} %copy-done, ...), custom_call_target="tpu_custom_call" | custom-call | flops 150994944 | bytes 1179648 | tf_op jit(solution)/shard_map/pallas_call | solution.py:57
  44.8 0.1 collective-permute-start.9
  44.9 0.0 collective-permute-done.12.part
  44.9 1.5 %shard_map.88 = (bf16[256,768]{1,0:T(8,128)(2,1)S(1)}, f32[96,128]{1,0:T(8,128)S(1)}, f32[96,128]{1,0:T(8,128)S(1)}, f32[96,128]{1,0:T(8,128)S(1)}, f32[96,128]{1,0:T(8,128)S(1)}) custom-call(s32[2]{0:T(128)S(1)} %pad_add_fusion.place, bf16[272,768]{1,0:T(8,128)(2,1)S(1)} %collective-permute-done.12.part, f32[1,768]{1,0:T(1,128)S(1)} %broadcast_in_dim.8.gain, ...), custom_call_target="tpu_custom_call" | custom-call | flops 150994944 | bytes 1179648 | tf_op jit(solution)/shard_map/pallas_call | solution.py:57
  46.4 2.1 %collective-permute-start.13 = (f32[96,128]{1,0:T(8,128)S(1)}, f32[96,128]{1,0:T(8,128)S(1)}, u32[]{:S(2)}, u32[]{:S(2)}) collective-permute-start(f32[96,128]{1,0:T(8,128)S(1)} %get-tuple-element.47), channel_id=1, source_target_pairs={{0,4},{4,0},{8,12},{12,8},{1,5},{5,1},{9,13},{13,9},{2,6},{6,2},{1... | collective-permute-start | bytes 147464 | tf_op jit(solution)/shard_map/ppermute | solution.py:428
  48.5 0.0 collective-permute-done.10.rest_4_
  48.5 1.1 %collective-permute-start.14 = (f32[96,128]{1,0:T(8,128)S(1)}, f32[96,128]{1,0:T(8,128)S(1)}, u32[]{:S(2)}, u32[]{:S(2)}) collective-permute-start(f32[96,128]{1,0:T(8,128)S(1)} %get-tuple-element.48), channel_id=1, source_target_pairs={{0,8},{4,12},{8,0},{12,4},{1,9},{5,13},{9,1},{13,5},{2,10},{6,14},... | collective-permute-start | bytes 147464 | tf_op jit(solution)/shard_map/ppermute | solution.py:428
  49.6 0.0 collective-permute-done.11.rest_5_
  49.6 1.4 %collective-permute-start.15 = (f32[96,128]{1,0:T(8,128)S(1)}, f32[96,128]{1,0:T(8,128)S(1)}, u32[]{:S(2)}, u32[]{:S(2)}) collective-permute-start(f32[96,128]{1,0:T(8,128)S(1)} %get-tuple-element.49), channel_id=1, source_target_pairs={{0,12},{4,8},{8,4},{12,0},{1,13},{5,9},{9,5},{13,1},{2,14},{6,10},... | collective-permute-start | bytes 147464 | tf_op jit(solution)/shard_map/ppermute | solution.py:428
  51.1 0.0 collective-permute-done.9.rest_3_
  51.1 2.0 %collective-permute-start.4 = (bf16[192,128]{1,0:T(8,128)(2,1)S(1)}, bf16[192,128]{1,0:T(8,128)(2,1)S(1)}, u32[]{:S(2)}, u32[]{:S(2)}) collective-permute-start(bf16[192,128]{1,0:T(8,128)(2,1)S(1)} %get-tuple-element.36.rest_0_), channel_id=1, source_target_pairs={{0,8},{4,12},{8,0},{12,4},{1,9},{5,13},{9,1},{13,5},{2,10},{6,14},... | collective-permute-start | bytes 147464 | tf_op jit(solution)/shard_map/ppermute | solution.py:428
  53.1 0.0 collective-permute-done.13.rest_7_
  53.1 1.3 %collective-permute-start.5 = (bf16[192,128]{1,0:T(8,128)(2,1)S(1)}, bf16[192,128]{1,0:T(8,128)(2,1)S(1)}, u32[]{:S(2)}, u32[]{:S(2)}) collective-permute-start(bf16[192,128]{1,0:T(8,128)(2,1)S(1)} %get-tuple-element.36.rest_0_), channel_id=1, source_target_pairs={{0,12},{4,8},{8,4},{12,0},{1,13},{5,9},{9,5},{13,1},{2,14},{6,10},... | collective-permute-start | bytes 147464 | tf_op jit(solution)/shard_map/ppermute | solution.py:428
  54.4 1.3 %collective-permute-done.14.rest_8_ = f32[96,128]{1,0:T(8,128)S(1)} collective-permute-done((f32[96,128]{1,0:T(8,128)S(1)}, f32[96,128]{1,0:T(8,128)S(1)}, u32[]{:S(2)}, u32[]{:S(2)}) %collective-permute-start.14) | collective-permute-done | bytes 49184 | tf_op jit(solution)/shard_map/ppermute | solution.py:428
  55.7 0.0 collective-permute-done.15.rest_9_
  55.7 0.3 shard_map.89.rest_4_
  56.0 2.8 %collective-permute-start.16 = (bf16[208,128]{1,0:T(8,128)(2,1)S(1)}, bf16[208,128]{1,0:T(8,128)(2,1)S(1)}, u32[]{:S(2)}, u32[]{:S(2)}) collective-permute-start(bf16[208,128]{1,0:T(8,128)(2,1)S(1)} %shard_map.89.rest_4_), channel_id=1, source_target_pairs={{0,4},{4,0},{8,12},{12,8},{1,5},{5,1},{9,13},{13,9},{2,6},{6,2},{1... | collective-permute-start | bytes 159752 | tf_op jit(solution)/shard_map/ppermute | solution.py:428
  58.7 1.3 %collective-permute-start.17 = (bf16[208,128]{1,0:T(8,128)(2,1)S(1)}, bf16[208,128]{1,0:T(8,128)(2,1)S(1)}, u32[]{:S(2)}, u32[]{:S(2)}) collective-permute-start(bf16[208,128]{1,0:T(8,128)(2,1)S(1)} %shard_map.89.rest_4_), channel_id=1, source_target_pairs={{0,8},{4,12},{8,0},{12,4},{1,9},{5,13},{9,1},{13,5},{2,10},{6,14},... | collective-permute-start | bytes 159752 | tf_op jit(solution)/shard_map/ppermute | solution.py:428
  60.1 0.0 collective-permute-done.3.rest_1_
  60.1 1.4 %collective-permute-start.18 = (bf16[208,128]{1,0:T(8,128)(2,1)S(1)}, bf16[208,128]{1,0:T(8,128)(2,1)S(1)}, u32[]{:S(2)}, u32[]{:S(2)}) collective-permute-start(bf16[208,128]{1,0:T(8,128)(2,1)S(1)} %shard_map.89.rest_4_), channel_id=1, source_target_pairs={{0,12},{4,8},{8,4},{12,0},{1,13},{5,9},{9,5},{13,1},{2,14},{6,10},... | collective-permute-start | bytes 159752 | tf_op jit(solution)/shard_map/ppermute | solution.py:428
  61.4 0.6 shard_map.91.rest_9_.rest_2_
  62.0 0.6 shard_map.92.rest_10_.rest_3_
  62.6 0.0 collective-permute-done.4.rest_2_
  62.6 0.0 collective-permute-done.5.rest_3_
  62.6 0.0 collective-permute-done.16.rest_5_
  62.6 1.7 %collective-permute-done.17.rest_6_ = bf16[208,128]{1,0:T(8,128)(2,1)S(1)} collective-permute-done((bf16[208,128]{1,0:T(8,128)(2,1)S(1)}, bf16[208,128]{1,0:T(8,128)(2,1)S(1)}, u32[]{:S(2)}, u32[]{:S(2)}) %collective-permute-start.17) | collective-permute-done | bytes 53280 | tf_op jit(solution)/shard_map/ppermute | solution.py:428
  64.3 1.7 %collective-permute-done.18.rest_7_ = bf16[208,128]{1,0:T(8,128)(2,1)S(1)} collective-permute-done((bf16[208,128]{1,0:T(8,128)(2,1)S(1)}, bf16[208,128]{1,0:T(8,128)(2,1)S(1)}, u32[]{:S(2)}, u32[]{:S(2)}) %collective-permute-start.18) | collective-permute-done | bytes 53280 | tf_op jit(solution)/shard_map/ppermute | solution.py:428
  66.1 1.1 %shard_map.93 = (bf16[4,128,384]{2,1,0:T(8,128)(2,1)S(1)}, bf16[3,256,256]{2,1,0:T(8,128)(2,1)S(1)}) custom-call(s32[2]{0:T(128)S(1)} %pad_add_fusion.place, bf16[192,128]{1,0:T(8,128)(2,1)S(1)} %get-tuple-element.36.rest_0_, bf16[192,128]{1,0:T(8,128)(2,1)S(1)} %collective-permute-done.3.rest_1_, bf16[192,128]{1,0:T(8,128)(2,1)S(1)} %collective-permute-done.4.rest_2_, ...), custom_call_target="tpu_custom_call" | custom-call | flops 201326592 | bytes 1572864 | tf_op jit(solution)/shard_map/pallas_call | solution.py:57
  67.2 0.0 copy-start.2
  67.2 0.1 collective-permute-start.20
  67.3 0.9 %shard_map.94.rest_0_ = bf16[4,128,384]{2,1,0:T(8,128)(2,1)S(1)} custom-call(s32[2]{0:T(128)S(1)} %pad_add_fusion.place, bf16[3,256,256]{2,1,0:T(8,128)(2,1)S(1)} %get-tuple-element.55.rest_0_, bf16[4,3,128,256]{3,2,1,0:T(8,128)(2,1)S(1)} %shard_map.90.rest_8_.rest_1_, bf16[2,2,3,64,256]{4,3,2,1,0:T(8,128)(2,1)S(1)} %shard_map.91.rest_9_.rest_2_, ...), custom_call_target="tpu_custom_call" | custom-call | flops 201326592 | bytes 786432 | tf_op jit(solution)/shard_map/pallas_call | solution.py:57
  68.2 0.6 collective-permute-start.19
  68.7 0.6 shard_map.95.rest_2_
  69.3 0.0 collective-permute-done.20.rest_1_
  69.4 1.1 %shard_map.96.rest_3_ = bf16[4,128,384]{2,1,0:T(8,128)(2,1)S(1)} custom-call(s32[8]{0:T(128)S(1)} %copy-done.3, bf16[4,128,384]{2,1,0:T(8,128)(2,1)S(1)} %get-tuple-element.56.rest_0_, bf16[4,128,384]{2,1,0:T(8,128)(2,1)S(1)} %collective-permute-done.20.rest_1_, bf16[768,384]{1,0:T(8,128)(2,1)S(1)} %shard_map.95.rest_2_), custom_call_target="tpu_custom_call" | custom-call | flops 301989888 | bytes 786432 | tf_op jit(solution)/shard_map/pallas_call | solution.py:57
  70.5 0.0 collective-permute-done.19.rest_1_
  70.5 1.8 %shard_map.97 = bf16[8,128,384]{2,1,0:T(8,128)(2,1)} custom-call(s32[8]{0:T(128)S(1)} %copy-done.3, bf16[4,128,384]{2,1,0:T(8,128)(2,1)S(1)} %shard_map.94.rest_0_, bf16[4,128,384]{2,1,0:T(8,128)(2,1)S(1)} %collective-permute-done.19.rest_1_, bf16[768,384]{1,0:T(8,128)(2,1)S(1)} %shard_map.95.rest_2_, bf16[4,128,384]{2,1,0:T(8,128)(2,1)S(1)} %shard_map.96.rest_3_), custom_call_target="tpu_custom_call" | custom-call | flops 301989888 | bytes 1572864 | tf_op jit(solution)/shard_map/pallas_call | solution.py:57
  (13 shorter events, 0.0 us)
Async XLA Ops:
  0.0 14.2 %copy-start.5 = (f32[768]{0:T(1024)S(1)}, f32[768]{0:T(1024)}, u32[]{:S(2)}) copy-start(f32[768]{0:T(1024)} %param.9) | copy-start | bytes 9220
  0.0 22.3 %copy-start.4 = (bf16[768,384]{1,0:T(8,128)(2,1)S(1)}, bf16[768,384]{1,0:T(8,128)(2,1)}, u32[]{:S(2)}) copy-start(bf16[768,384]{1,0:T(8,128)(2,1)} %w_query.1) | copy-start | bytes 1769476
  0.0 22.3 %copy-start = (bf16[768,384]{1,0:T(8,128)(2,1)S(1)}, bf16[768,384]{1,0:T(8,128)(2,1)}, u32[]{:S(2)}) copy-start(bf16[768,384]{1,0:T(8,128)(2,1)} %w_key.9) | copy-start | bytes 1769476
  0.0 22.3 %copy-start.3 = (s32[8]{0:T(128)S(1)}, s32[8]{0:T(128)}, u32[]{:S(2)}) copy-start(s32[8]{0:T(128)} %live.5) | copy-start | bytes 100
  1.1 13.0 %collective-permute-start.7 = (bf16[256,768]{1,0:T(8,128)(2,1)S(1)}, bf16[256,768]{1,0:T(8,128)(2,1)S(1)}, u32[]{:S(2)}, u32[]{:S(2)}) collective-permute-start(bf16[256,768]{1,0:T(8,128)(2,1)S(1)} %bitcast.7), channel_id=1, source_target_pairs={{0,2},{2,0},{1,3},{3,1},{4,6},{6,4},{5,7},{7,5},{8,10},{10,8},{9,1... | collective-permute-start | bytes 1179656 | tf_op jit(solution)/shard_map/ppermute | solution.py:28
  6.5 15.7 %collective-permute-start.6 = (bf16[272,768]{1,0:T(8,128)(2,1)S(1)}, bf16[272,768]{1,0:T(8,128)(2,1)S(1)}, u32[]{:S(2)}, u32[]{:S(2)}) collective-permute-start(bf16[272,768]{1,0:T(8,128)(2,1)S(1)} %get-tuple-element.37), channel_id=1, source_target_pairs={{0,2},{2,0},{1,3},{3,1},{4,6},{6,4},{5,7},{7,5},{8,10},{10,8},{9,1... | collective-permute-start | bytes 1253384 | tf_op jit(solution)/shard_map/ppermute | solution.py:28
  14.1 17.1 %collective-permute-start.8 = (bf16[256,768]{1,0:T(8,128)(2,1)S(1)}, bf16[256,768]{1,0:T(8,128)(2,1)S(1)}, u32[]{:S(2)}, u32[]{:S(2)}) collective-permute-start(bf16[256,768]{1,0:T(8,128)(2,1)S(1)} %collective-permute-done.7.part), channel_id=1, source_target_pairs={{0,1},{1,0},{2,3},{3,2},{4,5},{5,4},{6,7},{7,6},{8,9},{9,8},{10,11... | collective-permute-start | bytes 1179656 | tf_op jit(solution)/shard_map/ppermute | solution.py:28
  22.3 22.6 %collective-permute-start.12 = (bf16[272,768]{1,0:T(8,128)(2,1)S(1)}, bf16[272,768]{1,0:T(8,128)(2,1)S(1)}, u32[]{:S(2)}, u32[]{:S(2)}) collective-permute-start(bf16[272,768]{1,0:T(8,128)(2,1)S(1)} %collective-permute-done.6.part), channel_id=1, source_target_pairs={{0,1},{1,0},{2,3},{3,2},{4,5},{5,4},{6,7},{7,6},{8,9},{9,8},{10,11... | collective-permute-start | bytes 1253384 | tf_op jit(solution)/shard_map/ppermute | solution.py:28
  22.3 7.4 %copy-start.6 = (s32[128]{0:T(128)S(1)}, s32[128]{0:T(128)}, u32[]{:S(2)}) copy-start(s32[128]{0:T(128)} %param.15) | copy-start | bytes 1540
  25.2 9.5 %collective-permute-start = (f32[200,128]{1,0:T(8,128)S(1)}, f32[200,128]{1,0:T(8,128)S(1)}, u32[]{:S(2)}, u32[]{:S(2)}) collective-permute-start(f32[200,128]{1,0:T(8,128)S(1)} %get-tuple-element.33), channel_id=1, source_target_pairs={{0,4},{4,0},{8,12},{12,8},{1,5},{5,1},{9,13},{13,9},{2,6},{6,2},{1... | collective-permute-start | bytes 307208 | tf_op jit(solution)/shard_map/ppermute | solution.py:428
  27.1 12.6 %collective-permute-start.1 = (f32[200,128]{1,0:T(8,128)S(1)}, f32[200,128]{1,0:T(8,128)S(1)}, u32[]{:S(2)}, u32[]{:S(2)}) collective-permute-start(f32[200,128]{1,0:T(8,128)S(1)} %get-tuple-element.34), channel_id=1, source_target_pairs={{0,8},{4,12},{8,0},{12,4},{1,9},{5,13},{9,1},{13,5},{2,10},{6,14},... | collective-permute-start | bytes 307208 | tf_op jit(solution)/shard_map/ppermute | solution.py:428
  29.7 10.0 %collective-permute-start.2 = (f32[200,128]{1,0:T(8,128)S(1)}, f32[200,128]{1,0:T(8,128)S(1)}, u32[]{:S(2)}, u32[]{:S(2)}) collective-permute-start(f32[200,128]{1,0:T(8,128)S(1)} %get-tuple-element.35), channel_id=1, source_target_pairs={{0,12},{4,8},{8,4},{12,0},{1,13},{5,9},{9,5},{13,1},{2,14},{6,10},... | collective-permute-start | bytes 307208 | tf_op jit(solution)/shard_map/ppermute | solution.py:428
  31.2 5.5 %copy-start.1 = (bf16[768,384]{1,0:T(8,128)(2,1)S(1)}, bf16[768,384]{1,0:T(8,128)(2,1)}, u32[]{:S(2)}) copy-start(bf16[768,384]{1,0:T(8,128)(2,1)} %refs_2_.3) | copy-start | bytes 1769476
  32.8 15.7 %collective-permute-start.10 = (f32[96,128]{1,0:T(8,128)S(1)}, f32[96,128]{1,0:T(8,128)S(1)}, u32[]{:S(2)}, u32[]{:S(2)}) collective-permute-start(f32[96,128]{1,0:T(8,128)S(1)} %get-tuple-element.43), channel_id=1, source_target_pairs={{0,8},{4,12},{8,0},{12,4},{1,9},{5,13},{9,1},{13,5},{2,10},{6,14},... | collective-permute-start | bytes 147464 | tf_op jit(solution)/shard_map/ppermute | solution.py:428
  34.7 14.9 %collective-permute-start.11 = (f32[96,128]{1,0:T(8,128)S(1)}, f32[96,128]{1,0:T(8,128)S(1)}, u32[]{:S(2)}, u32[]{:S(2)}) collective-permute-start(f32[96,128]{1,0:T(8,128)S(1)} %get-tuple-element.44), channel_id=1, source_target_pairs={{0,12},{4,8},{8,4},{12,0},{1,13},{5,9},{9,5},{13,1},{2,14},{6,10},... | collective-permute-start | bytes 147464 | tf_op jit(solution)/shard_map/ppermute | solution.py:428
  40.0 20.1 %collective-permute-start.3 = (bf16[192,128]{1,0:T(8,128)(2,1)S(1)}, bf16[192,128]{1,0:T(8,128)(2,1)S(1)}, u32[]{:S(2)}, u32[]{:S(2)}) collective-permute-start(bf16[192,128]{1,0:T(8,128)(2,1)S(1)} %get-tuple-element.36.rest_0_), channel_id=1, source_target_pairs={{0,4},{4,0},{8,12},{12,8},{1,5},{5,1},{9,13},{13,9},{2,6},{6,2},{1... | collective-permute-start | bytes 147464 | tf_op jit(solution)/shard_map/ppermute | solution.py:428
  44.8 6.3 %collective-permute-start.9 = (f32[96,128]{1,0:T(8,128)S(1)}, f32[96,128]{1,0:T(8,128)S(1)}, u32[]{:S(2)}, u32[]{:S(2)}) collective-permute-start(f32[96,128]{1,0:T(8,128)S(1)} %get-tuple-element.42), channel_id=1, source_target_pairs={{0,4},{4,0},{8,12},{12,8},{1,5},{5,1},{9,13},{13,9},{2,6},{6,2},{1... | collective-permute-start | bytes 147464 | tf_op jit(solution)/shard_map/ppermute | solution.py:428
  46.4 6.6 %collective-permute-start.13 = (f32[96,128]{1,0:T(8,128)S(1)}, f32[96,128]{1,0:T(8,128)S(1)}, u32[]{:S(2)}, u32[]{:S(2)}) collective-permute-start(f32[96,128]{1,0:T(8,128)S(1)} %get-tuple-element.47), channel_id=1, source_target_pairs={{0,4},{4,0},{8,12},{12,8},{1,5},{5,1},{9,13},{13,9},{2,6},{6,2},{1... | collective-permute-start | bytes 147464 | tf_op jit(solution)/shard_map/ppermute | solution.py:428
  48.5 7.2 %collective-permute-start.14 = (f32[96,128]{1,0:T(8,128)S(1)}, f32[96,128]{1,0:T(8,128)S(1)}, u32[]{:S(2)}, u32[]{:S(2)}) collective-permute-start(f32[96,128]{1,0:T(8,128)S(1)} %get-tuple-element.48), channel_id=1, source_target_pairs={{0,8},{4,12},{8,0},{12,4},{1,9},{5,13},{9,1},{13,5},{2,10},{6,14},... | collective-permute-start | bytes 147464 | tf_op jit(solution)/shard_map/ppermute | solution.py:428
  49.6 6.0 %collective-permute-start.15 = (f32[96,128]{1,0:T(8,128)S(1)}, f32[96,128]{1,0:T(8,128)S(1)}, u32[]{:S(2)}, u32[]{:S(2)}) collective-permute-start(f32[96,128]{1,0:T(8,128)S(1)} %get-tuple-element.49), channel_id=1, source_target_pairs={{0,12},{4,8},{8,4},{12,0},{1,13},{5,9},{9,5},{13,1},{2,14},{6,10},... | collective-permute-start | bytes 147464 | tf_op jit(solution)/shard_map/ppermute | solution.py:428
  51.1 11.5 %collective-permute-start.4 = (bf16[192,128]{1,0:T(8,128)(2,1)S(1)}, bf16[192,128]{1,0:T(8,128)(2,1)S(1)}, u32[]{:S(2)}, u32[]{:S(2)}) collective-permute-start(bf16[192,128]{1,0:T(8,128)(2,1)S(1)} %get-tuple-element.36.rest_0_), channel_id=1, source_target_pairs={{0,8},{4,12},{8,0},{12,4},{1,9},{5,13},{9,1},{13,5},{2,10},{6,14},... | collective-permute-start | bytes 147464 | tf_op jit(solution)/shard_map/ppermute | solution.py:428
  53.1 9.5 %collective-permute-start.5 = (bf16[192,128]{1,0:T(8,128)(2,1)S(1)}, bf16[192,128]{1,0:T(8,128)(2,1)S(1)}, u32[]{:S(2)}, u32[]{:S(2)}) collective-permute-start(bf16[192,128]{1,0:T(8,128)(2,1)S(1)} %get-tuple-element.36.rest_0_), channel_id=1, source_target_pairs={{0,12},{4,8},{8,4},{12,0},{1,13},{5,9},{9,5},{13,1},{2,14},{6,10},... | collective-permute-start | bytes 147464 | tf_op jit(solution)/shard_map/ppermute | solution.py:428
  56.0 6.6 %collective-permute-start.16 = (bf16[208,128]{1,0:T(8,128)(2,1)S(1)}, bf16[208,128]{1,0:T(8,128)(2,1)S(1)}, u32[]{:S(2)}, u32[]{:S(2)}) collective-permute-start(bf16[208,128]{1,0:T(8,128)(2,1)S(1)} %shard_map.89.rest_4_), channel_id=1, source_target_pairs={{0,4},{4,0},{8,12},{12,8},{1,5},{5,1},{9,13},{13,9},{2,6},{6,2},{1... | collective-permute-start | bytes 159752 | tf_op jit(solution)/shard_map/ppermute | solution.py:428
  58.7 5.6 %collective-permute-start.17 = (bf16[208,128]{1,0:T(8,128)(2,1)S(1)}, bf16[208,128]{1,0:T(8,128)(2,1)S(1)}, u32[]{:S(2)}, u32[]{:S(2)}) collective-permute-start(bf16[208,128]{1,0:T(8,128)(2,1)S(1)} %shard_map.89.rest_4_), channel_id=1, source_target_pairs={{0,8},{4,12},{8,0},{12,4},{1,9},{5,13},{9,1},{13,5},{2,10},{6,14},... | collective-permute-start | bytes 159752 | tf_op jit(solution)/shard_map/ppermute | solution.py:428
  60.1 6.0 %collective-permute-start.18 = (bf16[208,128]{1,0:T(8,128)(2,1)S(1)}, bf16[208,128]{1,0:T(8,128)(2,1)S(1)}, u32[]{:S(2)}, u32[]{:S(2)}) collective-permute-start(bf16[208,128]{1,0:T(8,128)(2,1)S(1)} %shard_map.89.rest_4_), channel_id=1, source_target_pairs={{0,12},{4,8},{8,4},{12,0},{1,13},{5,9},{9,5},{13,1},{2,14},{6,10},... | collective-permute-start | bytes 159752 | tf_op jit(solution)/shard_map/ppermute | solution.py:428
  67.2 1.6 %copy-start.2 = (bf16[768,384]{1,0:T(8,128)(2,1)S(1)}, bf16[768,384]{1,0:T(8,128)(2,1)}, u32[]{:S(2)}) copy-start(bf16[768,384]{1,0:T(8,128)(2,1)} %w_out.1) | copy-start | bytes 1769476
  67.2 2.2 %collective-permute-start.20 = (bf16[4,128,384]{2,1,0:T(8,128)(2,1)S(1)}, bf16[4,128,384]{2,1,0:T(8,128)(2,1)S(1)}, u32[]{:S(2)}, u32[]{:S(2)}) collective-permute-start(bf16[4,128,384]{2,1,0:T(8,128)(2,1)S(1)} %get-tuple-element.56.rest_0_), channel_id=1, source_target_pairs={{0,1},{1,0},{2,3},{3,2},{4,5},{5,4},{6,7},{7,6},{8,9},{9,8},{10,11... | collective-permute-start | bytes 1179656 | tf_op jit(solution)/shard_map/ppermute | solution.py:28
  68.2 2.3 %collective-permute-start.19 = (bf16[4,128,384]{2,1,0:T(8,128)(2,1)S(1)}, bf16[4,128,384]{2,1,0:T(8,128)(2,1)S(1)}, u32[]{:S(2)}, u32[]{:S(2)}) collective-permute-start(bf16[4,128,384]{2,1,0:T(8,128)(2,1)S(1)} %shard_map.94.rest_0_), channel_id=1, source_target_pairs={{0,1},{1,0},{2,3},{3,2},{4,5},{5,4},{6,7},{7,6},{8,9},{9,8},{10,11... | collective-permute-start | bytes 1179656 | tf_op jit(solution)/shard_map/ppermute | solution.py:28

commit v3 on v2

v3 whole, which is shorter than its diff:
```python
import functools

import jax
import jax.numpy as jnp
from jax import lax
from jax.experimental import pallas as pl
from jax.experimental.pallas import tpu as pltpu
from jax.sharding import PartitionSpec as P

HEADS = 12
LANES = 128
CHUNKS = 2
SIZE = 2
LIMIT = 16 << 20
LOWEST = -1e30
PAD = 16


VMEM = pltpu.VMEM
SMEM = pltpu.SMEM
HBM = pltpu.HBM
BF16 = jnp.bfloat16
F32 = jnp.float32


def from_behind(value, axis, steps):
    count = lax.axis_size(axis)
    return lax.ppermute(value, axis, [(s, (s + steps) % count) for s in range(count)])


def spec(space=VMEM):
    return pl.BlockSpec(memory_space=space)


def call(kernel, out_shape, in_specs, scratch=(), flops=0, space=VMEM):
    single = not isinstance(out_shape, (list, tuple))
    shapes = [out_shape] if single else list(out_shape)
    nbytes = sum(s.size * s.dtype.itemsize for s in shapes)
    shapes = [space(s.shape, s.dtype) for s in shapes]
    fn = pl.pallas_call(
        kernel,
        out_shape=shapes,
        in_specs=in_specs,
        out_specs=[spec(space) for _ in shapes],
        scratch_shapes=list(scratch),
        compiler_params=pltpu.CompilerParams(vmem_limit_bytes=LIMIT),
        cost_estimate=pl.CostEstimate(flops=flops, transcendentals=0, bytes_accessed=2 * nbytes),
    )

    def run(*args):
        args = [
            arg
            if block.memory_space == SMEM
            else pltpu.with_memory_space_constraint(arg, block.memory_space)
            for arg, block in zip(args, in_specs, strict=True)
        ]
        out = fn(*args)
        return out[0] if single else out

    return run


def dot(left, right):
    return jnp.dot(left, right, preferred_element_type=F32)


def dot_t(left, right):
    return lax.dot_general(left, right, (((1,), (1,)), ((), ())), preferred_element_type=F32)


def normed_rows(rows, gain):
    values_f = rows.astype(F32)
    average = jnp.mean(values_f, axis=-1, keepdims=True)
    centred = values_f - average
    spread = jnp.mean(centred * centred, axis=-1, keepdims=True)
    return (centred * lax.rsqrt(spread + 1e-05) * gain).astype(BF16)


def load_kernel(valid, rows_in, resident, *rest, part_cols):
    lasts, flags, sems = rest[:-2], rest[-2], rest[-1]
    rows_here, cols, _ = resident.shape
    some = lasts[-1].shape[0] // part_cols
    begin = lax.axis_index("heads") * some * len(lasts)
    first = pltpu.make_async_copy(valid, flags, sems.at[rows_here + some * len(lasts)])
    first.start()
    copies = []
    for r in range(some * len(lasts)):
        source = rows_in.at[begin + r, pl.ds(cols - part_cols, part_cols), :]
        target = lasts[r // some].at[pl.ds(r % some * part_cols, part_cols)]
        copies.append(pltpu.make_async_copy(source, target, sems.at[rows_here + r]))
    for r in range(rows_here):
        copies.append(pltpu.make_async_copy(rows_in.at[r], resident.at[r], sems.at[r]))
    for copy in copies:
        copy.start()
    first.wait()
    tail = some * part_cols
    lasts[0][tail:, :] = jnp.zeros((PAD, lasts[0].shape[1]), BF16)
    lasts[0][tail:, 0:cols] = jnp.broadcast_to(flags[...].astype(F32), (PAD, cols)).astype(BF16)
    for copy in copies:
        copy.wait()


def side_by_side(block, first, cols, pair):
    at = slice(pair * LANES, (pair + 1) * LANES)
    pieces = [block[(first + r) * cols : (first + r + 1) * cols, at] for r in range(SIZE)]
    return jnp.concatenate(pieces, axis=1)


def write_shards(total, shards, depth_index):
    slots, cols, _ = total.shape
    count = len(shards)
    part = cols // count
    for k, shard in enumerate(shards):
        begin = pl.multiple_of(lax.bitwise_xor(depth_index, k) * part, part)
        for slot in range(slots):
            rows = total[slot, pl.ds(begin, part), :]
            shard[slot * part : (slot + 1) * part, :] = rows


def own_kernel(live, rows_in, gain, w_query, w_key, *rest, shards):
    normed_out, query_out = rest[0], rest[1]
    outs = rest[2 : 2 + shards]
    keys, total = rest[2 + shards :]
    groups, pairs = query_out.shape[0], query_out.shape[1]
    _, cols, width = rows_in.shape
    low = lax.broadcasted_iota(jnp.int32, (cols, LANES), 1) < LANES // 2
    zero = jnp.zeros((cols, LANES), BF16)
    local = w_query.shape[1]
    weights = jnp.concatenate([w_query[...], w_key[...]], axis=1)
    for g in range(groups):
        rows = rows_in[g * SIZE : (g + 1) * SIZE].reshape(SIZE * cols, width)
        normed = normed_rows(rows, gain[...])
        normed_out[g] = normed
        both_sides = dot(normed, weights)
        query, key = both_sides[:, :local], both_sides[:, local:].astype(BF16)
        for r in range(SIZE):
            scale = live[g * SIZE + r : g * SIZE + r + 1, :]
            for p in range(pairs):
                both = query[r * cols : (r + 1) * cols, p * LANES : (p + 1) * LANES]
                both = (both * scale).astype(BF16)
                at = slice(r * LANES, (r + 1) * LANES)
                query_out[g, p, 0:cols, at] = jnp.where(low, both, zero)
                query_out[g, p, cols : 2 * cols, at] = jnp.where(low, zero, both)
        for p in range(pairs):
            keys[g, p] = side_by_side(key, 0, cols, p)
    for p in range(pairs):
        score = dot_t(query_out[0, p], keys[0, p])
        for g in range(1, groups):
            score = score + dot_t(query_out[g, p], keys[g, p])
        total[2 * p] = score[:cols]
        total[2 * p + 1] = score[cols:]
    write_shards(total, outs, lax.axis_index("depth"))
    real = jnp.sum(live[...], axis=0, keepdims=True)
    for out in outs:
        out[out.shape[0] - 8 :, :] = jnp.broadcast_to(real, (8, LANES))


def value_kernel(*refs, cores, cols):
    parts = len(refs) - 2
    normed, w_value, values = refs[:parts], refs[parts], refs[parts + 1]
    _, inner, pairs, _, _ = values.shape
    each = inner * cores // parts
    for n in range(parts):
        value = dot(normed[n][...], w_value[...]).astype(BF16)
        for g in range(each):
            for p in range(pairs):
                block = side_by_side(value, g * SIZE, cols, p)
                values[n % cores, n // cores * each + g, p] = block


def own_value_kernel(normed, w_value, values, *, cols):
    for g in range(values.shape[0]):
        value = dot(normed[g], w_value[...]).astype(BF16)
        for p in range(values.shape[1]):
            values[g, p] = side_by_side(value, 0, cols, p)


def remote_kernel(part, gain, w_key, query, *rest, step, steps, chunk, part_cols, cores, shards):
    if step > 0:
        before, rest = rest[0], rest[1:]
    normed_out, rest = rest[0], rest[1:]
    last = step + 1 == steps
    used = normed_out.shape[0]
    rows, cols = used // part_cols, part_cols
    pairs, full = query.shape[1], query.shape[2] // 2
    normed = normed_rows(part[0:used, :], gain[...])
    normed_out[...] = normed
    key = dot(normed, w_key[...]).astype(BF16)
    total = rest[shards] if last else rest[0]
    inner = rows // SIZE
    source = lax.rem(lax.axis_index("heads") + cores - step % cores, cores)
    base = source * (steps // cores) * inner + step // cores * inner
    low = lax.broadcasted_iota(jnp.int32, (full, LANES), 1) < LANES // 2
    for p in range(pairs):
        score = before[p] if step > 0 else None
        whole = None
        for g in range(inner):
            one = side_by_side(key, g * SIZE, cols, p)
            twice = jnp.concatenate([one, one], axis=0)
            extra = dot_t(query[base + g, p], twice)
            whole = extra if whole is None else whole + extra
        left, right = whole[:full], whole[full:]
        if chunk % 2 == 1:
            left, right = right, left
        packed = jnp.where(low, left, right)
        total[p] = packed if score is None else score + packed
    if last:
        write_shards(total, rest[:shards], lax.axis_index("depth"))


def added(pieces):
    total = pieces[0][...]
    for piece in pieces[1:]:
        total = total + piece[...]
    return total


def diagonal(rows):
    row = lax.broadcasted_iota(jnp.int32, (rows, LANES), 0)
    return row == lax.broadcasted_iota(jnp.int32, (rows, LANES), 1)


def low_lanes(rows):
    return lax.broadcasted_iota(jnp.int32, (rows, LANES), 1) < LANES // 2


def half_mask(valid, half, rows):
    flags = valid[...]
    turned = pltpu.roll(flags, LANES // 2, 1)
    low = low_lanes(1)
    both = jnp.where(low, flags, turned) if half == 0 else jnp.where(low, turned, flags)
    return jnp.broadcast_to(both > 0.5, (rows, LANES))


def row_max(block):
    return jnp.max(block, axis=-1, keepdims=True)


def row_sum(block):
    return jnp.sum(block, axis=-1, keepdims=True)


def own_soft_kernel(*rest, shards, offsets, heads, head_width):
    valid, rest = rest[: 1 + offsets], rest[1 + offsets :]
    probs, stats = rest[-2:]
    sums = [added(rest[t * shards : (t + 1) * shards]) for t in range(1 + offsets)]
    rows = stats.shape[1]
    part = rows // heads
    factor = lax.rsqrt(F32(head_width) * sums[0][rows : rows + 1, 0:1])
    mask = jnp.broadcast_to(valid[0][...] > 0.5, (part, LANES))
    halves = [half_mask(valid[1 + o], 0, part) for o in range(offsets)]
    low = low_lanes(part)
    for p in range(heads // 2):
        at = slice(p * part, (p + 1) * part)
        near = []
        for o in range(offsets):
            near.append(jnp.where(halves[o], sums[1 + o][at] * factor, LOWEST))
        highest = functools.reduce(jnp.maximum, near)
        tops, wholes = [], []
        for h in (2 * p, 2 * p + 1):
            mine = slice(h * part, (h + 1) * part)
            side = low if h % 2 == 0 else jnp.logical_not(low)
            scaled = jnp.where(mask, sums[0][mine] * factor, LOWEST)
            top = row_max(jnp.maximum(scaled, jnp.where(side, highest, LOWEST)))
            expo = jnp.where(mask, jnp.exp(scaled - top), 0.0)
            probs[mine, :] = expo.astype(BF16)
            tops.append(top)
            wholes.append(expo)
        top = jnp.where(low, tops[0], tops[1])
        mass = jnp.zeros((part, LANES), F32)
        for o in range(offsets):
            expo = jnp.where(halves[o], jnp.exp(near[o] - top), 0.0)
            begin = rows + (o * heads // 2 + p) * part
            probs[begin : begin + part, :] = expo.astype(BF16)
            mass = mass + expo
        for h in (2 * p, 2 * p + 1):
            mine = slice(h * part, (h + 1) * part)
            side = low if h % 2 == 0 else jnp.logical_not(low)
            whole = row_sum(wholes[h % 2] + jnp.where(side, mass, 0.0))
            stats[0, mine, :] = jnp.broadcast_to(tops[h % 2], (part, LANES))
            stats[1, mine, :] = jnp.broadcast_to(whole, (part, LANES))
            stats[2, mine, :] = jnp.broadcast_to(factor, (part, LANES))


def last_soft_kernel(*rest, shards, offsets, heads):
    valid, stats, probs = rest[:offsets], rest[offsets], rest[-1]
    rest = rest[offsets + 1 : -1]
    sums = [added(rest[t * shards : (t + 1) * shards]) for t in range(offsets)]
    part = stats.shape[1] // heads
    low = low_lanes(part)
    halves = [half_mask(valid[o], 1, part) for o in range(offsets)]
    kept = diagonal(part)
    lines = []
    for p in range(heads // 2):
        at = slice(p * part, (p + 1) * part)
        factor = stats[2, 2 * p * part : (2 * p + 1) * part, :]
        far = [jnp.where(halves[o], sums[o][at] * factor, LOWEST) for o in range(offsets)]
        highest = functools.reduce(jnp.maximum, far)
        tops, shifts = [], []
        for h in (2 * p, 2 * p + 1):
            old = stats[0, h * part : (h + 1) * part, :]
            side = jnp.logical_not(low) if h % 2 == 0 else low
            top = jnp.maximum(old, row_max(jnp.where(side, highest, LOWEST)))
            tops.append(top)
            shifts.append(jnp.exp(old - top))
        top = jnp.where(low, tops[1], tops[0])
        expo = [jnp.where(halves[o], jnp.exp(far[o] - top), 0.0) for o in range(offsets)]
        mass = functools.reduce(jnp.add, expo)
        wholes = []
        for h in (2 * p, 2 * p + 1):
            side = jnp.logical_not(low) if h % 2 == 0 else low
            own = stats[1, h * part : (h + 1) * part, :]
            whole = shifts[h % 2] * own + row_sum(jnp.where(side, mass, 0.0))
            wholes.append(whole)
            block = jnp.where(kept, shifts[h % 2] / whole, 0.0)
            lines.append(jnp.sum(block, axis=0, keepdims=True))
        whole = jnp.where(low, wholes[1], wholes[0])
        for o in range(offsets):
            begin = (o * heads // 2 + p) * part
            probs[begin : begin + part, :] = (expo[o] / whole).astype(BF16)
    lines = jnp.concatenate(lines + [jnp.zeros((8 - heads, LANES), F32)], axis=0)
    coarse = lines.astype(BF16).astype(F32)
    tail = jnp.concatenate([coarse, lines - coarse], axis=0)
    probs[probs.shape[0] - PAD :, :] = tail.astype(BF16)


def collect(owns, others, probs, heads):
    blocks = probs.shape[2] // LANES
    cols = probs.shape[1] // 2
    part = (others[0].shape[0] - PAD) // ((blocks - 1) * heads // 2)
    kept = diagonal(part)
    low = low_lanes(part)
    for k in range(len(owns)):
        begin = lax.bitwise_xor(lax.axis_index("depth"), k) * part
        tail = others[k][others[k].shape[0] - PAD :, :].astype(F32)
        lines = tail[0:8] + tail[8:16]
        for head in range(heads):
            at = pl.ds(pl.multiple_of(head % 2 * cols + begin, part), part)
            line = jnp.where(kept, jnp.broadcast_to(lines[head : head + 1], (part, LANES)), 0.0)
            scale = row_sum(line)
            own = owns[k][head * part : (head + 1) * part, :].astype(F32) * scale
            probs[head // 2, at, 0:LANES] = own.astype(BF16)
            for o in range(blocks - 1):
                first = (o * heads // 2 + head // 2) * part
                near = owns[k][heads * part + first : heads * part + first + part, :]
                near = near.astype(F32) * scale
                far = others[k][first : first + part, :].astype(F32)
                if head % 2 == 0:
                    both = jnp.where(low, near, far)
                else:
                    both = pltpu.roll(jnp.where(low, far, near), LANES // 2, 1)
                probs[head // 2, at, (1 + o) * LANES : (2 + o) * LANES] = both.astype(BF16)


def mix_kernel(*rest, side, cores, tiles, shards, heads):
    if shards:
        rest, probs = rest[:-1], rest[-1]
        collect(rest[:shards], rest[shards : 2 * shards], probs, heads)
        rest = rest[2 * shards :]
    else:
        probs, rest = rest[0], rest[1:]
    own, remote, out = rest[0], rest[1 : 1 + tiles], rest[1 + tiles]
    _, pairs, cols, lanes = own.shape
    inner = own.shape[0] // cores
    low = jnp.concatenate([low_lanes(cols)] * (lanes // LANES), axis=1)
    step = lax.rem(lax.axis_index("heads") + cores - side, cores)
    for g in range(inner):
        for p in range(pairs):
            blocks = [own[side * inner + g, p]]
            blocks += [block[step, g, p] for block in remote]
            mixed = dot(probs[p], jnp.concatenate(blocks, axis=0))
            picked = jnp.where(low, mixed[:cols], mixed[cols:]).astype(BF16)
            for r in range(SIZE):
                at = slice(r * LANES, (r + 1) * LANES)
                out[g * SIZE + r, :, p * LANES : (p + 1) * LANES] = picked[:, at]


def order_kernel(w_out, ordered, *, cores):
    local = w_out.shape[0] // cores
    for k in range(cores):
        source = lax.rem(lax.axis_index("heads") + cores - k, cores)
        rows = w_out[pl.ds(pl.multiple_of(source * local, local), local), :]
        ordered[k * local : (k + 1) * local, :] = rows


def projected(live, parts, weights, first):
    size, cols, local = parts[0].shape
    blocks = [part[...].reshape(size * cols, local) for part in parts]
    total = dot(jnp.concatenate(blocks, axis=1), weights[...])
    results = []
    for r in range(size):
        scale = live[first + r : first + r + 1, :]
        scale = jnp.concatenate([scale] * (total.shape[1] // LANES), axis=1)
        results.append((total[r * cols : (r + 1) * cols] * scale).astype(BF16))
    return results


def project_kernel(live, *rest, cores, first):
    parts, weights, out = rest[:cores], rest[cores], rest[cores + 1]
    for r, rows in enumerate(projected(live, parts, weights, first)):
        out[r] = rows


def finish_kernel(live, *rest, cores):
    parts, weights, ready = rest[:cores], rest[cores], rest[cores + 1 : -3]
    out, buffer, sems = rest[-3:]
    size = buffer.shape[0]
    copies = []
    for k, done in enumerate(ready):
        copies.append(pltpu.make_async_copy(done, out.at[pl.ds(k * size, size)], sems.at[k]))
        copies[-1].start()
    first = len(ready) * size
    for r, rows in enumerate(projected(live, parts, weights, first)):
        buffer[r] = rows
        at = out.at[first + r]
        copies.append(pltpu.make_async_copy(buffer.at[r], at, sems.at[len(ready) + r]))
        copies[-1].start()
    for copy in copies:
        copy.wait()


def on_device(alignment, norm_gain, w_query, w_key, w_value, w_out, row_mask, col_valid):
    rows_here, cols_here, width = alignment.shape
    local_width = w_query.shape[1]
    head_width = width // HEADS
    local_heads = local_width // head_width
    pairs = local_heads // 2
    offsets = lax.axis_size("cols") - 1
    depth = lax.axis_size("depth")
    cores = lax.axis_size("heads")
    core = lax.axis_index("heads")
    part_rows = rows_here // cores
    inner = part_rows // SIZE
    groups = rows_here // SIZE
    part_cols = cols_here // CHUNKS
    direct = depth in (2, 4, 8) and cols_here % (16 * depth) == 0
    shards = depth if direct else 1
    part = cols_here // shards
    lanes = SIZE * LANES
    total_cols = (1 + offsets) * cols_here
    shape = jax.ShapeDtypeStruct
    gain = norm_gain[None, :]
    live = jnp.broadcast_to(row_mask.astype(F32)[:, None], (rows_here, LANES))

    first = lax.dynamic_slice(
        alignment, (core * part_rows, 0, 0), (part_rows, cols_here - part_cols, width)
    )
    sent = {(0, 0): first.reshape(part_rows * part_cols, width)}
    spans = [1] * CHUNKS
    some = part_rows // spans[-1] * part_cols
    resident, *lasts = call(
        functools.partial(load_kernel, part_cols=part_cols),
        [shape((rows_here, cols_here, width), BF16), shape((some + PAD, width), BF16)]
        + [shape((some, width), BF16)] * (spans[-1] - 1),
        [spec(HBM), spec(HBM)],
        [
            pltpu.VMEM((1, cols_here), jnp.int32),
            pltpu.SemaphoreType.DMA((part_rows + rows_here + 1,)),
        ],
    )(col_valid[None, :], alignment)
    for m, block in enumerate(lasts):
        sent[CHUNKS - 1, m] = block
    arrived = {}
    for offset in range(1, offsets + 1):
        for (c, m), block in sent.items():
            mine = from_behind(block, "cols", offset)
            arrived[offset, c, m] = [mine] + [
                from_behind(mine, "heads", k) for k in range(1, cores)
            ]

    def exchange(values):
        received = [values[0]]
        for k in range(1, shards):
            swapped = [(source, source ^ k) for source in range(depth)]
            received.append(lax.ppermute(values[k], "depth", swapped))
        return received

    own = call(
        functools.partial(own_kernel, shards=shards),
        [
            shape((groups, SIZE * cols_here, width), BF16),
            shape((groups, pairs, 2 * cols_here, lanes), BF16),
        ]
        + [shape((local_heads * part + 8, cols_here), F32)] * shards,
        [spec()] * 5,
        [
            pltpu.VMEM((groups, pairs, cols_here, lanes), BF16),
            pltpu.VMEM((local_heads, cols_here, cols_here), F32),
        ],
        flops=4 * rows_here * cols_here * width * local_width,
    )(live, resident, gain, w_query, w_key)
    normed, query, own_sums = own[0], own[1], exchange(own[2:])

    own_values = call(
        functools.partial(own_value_kernel, cols=cols_here),
        shape((groups, pairs, cols_here, lanes), BF16),
        [spec()] * 2,
        flops=2 * rows_here * cols_here * width * local_width,
    )(normed, w_value)
    ordered = call(
        functools.partial(order_kernel, cores=cores), shape(w_out.shape, BF16), [spec()]
    )(w_out)

    tiles, remote_values = [], []
    for offset in range(1, offsets + 1):
        for c in range(CHUNKS):
            before, rows_of = [], []
            steps = spans[c] * cores
            used = part_rows // spans[c] * part_cols
            for n in range(steps):
                m, k = divmod(n, cores)
                outs = [shape((used, width), BF16)]
                scratch = []
                if n + 1 == steps:
                    outs += [shape((pairs * part, LANES), F32)] * shards
                    scratch = [pltpu.VMEM((pairs, cols_here, LANES), F32)]
                else:
                    outs += [shape((pairs, cols_here, LANES), F32)]
                result = call(
                    functools.partial(
                        remote_kernel,
                        step=n,
                        steps=steps,
                        chunk=c,
                        part_cols=part_cols,
                        cores=cores,
                        shards=shards,
                    ),
                    outs,
                    [spec()] * (4 + len(before)),
                    scratch,
                    flops=2 * used * width * local_width,
                )(arrived[offset, c, m][k], gain, w_key, query, *before)
                rows_of.append(result[0])
                before = [result[1]]
            tiles.append(exchange(result[1:]))
            remote_values.append(
                call(
                    functools.partial(value_kernel, cores=cores, cols=part_cols),
                    shape((cores, inner, pairs, part_cols, lanes), BF16),
                    [spec()] * (steps + 1),
                    flops=2 * cores * part_rows * part_cols * width * local_width,
                )(*rows_of, w_value)
            )

    valid_tiles = [col_valid.astype(BF16)[None, :]]
    for offset in range(1, offsets + 1):
        valid_tiles.append(arrived[offset, CHUNKS - 1, 0][0][-PAD : 1 - PAD, :cols_here])
    if direct:
        valid = [tile.astype(F32) for tile in valid_tiles]
        rows = local_heads * part
        far_rows = offsets * pairs * part
        early = [piece for tile in tiles[0::CHUNKS] for piece in tile]
        late = [piece for tile in tiles[1::CHUNKS] for piece in tile]
        own_probs, stats = call(
            functools.partial(
                own_soft_kernel,
                shards=shards,
                offsets=offsets,
                heads=local_heads,
                head_width=head_width,
            ),
            [shape((rows + far_rows, LANES), BF16), shape((3, rows, LANES), F32)],
            [spec()] * ((1 + offsets) * (1 + shards)),
            flops=1000000,
        )(*valid, *own_sums, *early)
        own_probs = exchange([own_probs] * shards)
        probs = call(
            functools.partial(
                last_soft_kernel, shards=shards, offsets=offsets, heads=local_heads
            ),
            shape((far_rows + PAD, LANES), BF16),
            [spec()] * (1 + offsets * (1 + shards)),
            flops=1000000,
        )(*valid[1:], stats, *late)
        probs = exchange([probs] * shards)
        probs = own_probs + probs
    else:
        count = lax.psum(jnp.sum(row_mask.astype(F32)), "depth")
        own_part = own_sums[0][: local_heads * cols_here]
        blocks = [own_part.reshape(local_heads, cols_here, cols_here)]
        for index, tile in enumerate(tiles):
            packed = tile[0].reshape(pairs, cols_here, 2, part_cols)
            packed = packed[:, :, ::-1] if index % CHUNKS % 2 == 1 else packed
            packed = jnp.transpose(packed, (0, 2, 1, 3))
            blocks.append(packed.reshape(local_heads, cols_here, part_cols))
        logits = jnp.concatenate(blocks, axis=2)
        share = lax.psum_scatter(logits, "depth", scatter_dimension=1, tiled=True)
        mask = jnp.concatenate(valid_tiles, axis=1)[None] > 0.5
        scaled = jnp.where(mask, share * lax.rsqrt(F32(head_width) * count), LOWEST)
        expo = jnp.where(mask, jnp.exp(scaled - jnp.max(scaled, axis=-1, keepdims=True)), 0.0)
        probs = (expo / jnp.sum(expo, axis=-1, keepdims=True)).astype(BF16)
        probs = lax.all_gather(probs, "depth", axis=1, tiled=True)
        probs = [probs.reshape(pairs, 2 * cols_here, total_cols)]

    finished = []
    piece = shape((part_rows, cols_here, local_width), BF16)
    for side in range(cores):
        gathers = len(probs) // 2
        outs = [piece]
        if gathers:
            outs.append(shape((pairs, 2 * cols_here, total_cols), BF16))
        mixed = call(
            functools.partial(
                mix_kernel,
                side=side,
                cores=cores,
                tiles=len(tiles),
                shards=gathers,
                heads=local_heads,
            ),
            outs,
            [spec()] * (len(probs) + 1 + len(remote_values)),
            flops=4 * SIZE * cols_here * total_cols * local_width,
        )(*probs, own_values, *remote_values)
        mine, probs = mixed[0], mixed[1:] if gathers else probs
        parts = [mine] + [from_behind(mine, "heads", k) for k in range(1, cores)]
        if side + 1 < cores:
            finished.append(
                call(
                    functools.partial(project_kernel, cores=cores, first=side * part_rows),
                    piece,
                    [spec()] * (cores + 2),
                    flops=2 * SIZE * cols_here * width * local_width,
                )(live, *parts, ordered)
            )
    return call(
        functools.partial(finish_kernel, cores=cores),
        shape((rows_here, cols_here, local_width), BF16),
        [spec()] * (2 * cores + 1),
        [
            pltpu.VMEM((part_rows, cols_here, local_width), BF16),
            pltpu.SemaphoreType.DMA((cores - 1 + part_rows,)),
        ],
        flops=2 * SIZE * cols_here * width * local_width,
        space=HBM,
    )(live, *parts, ordered, *finished)


def solution(mesh):
    in_specs = (
        P(("groups", "depth"), "cols", None),
        P(),
        P(None, "heads"),
        P(None, "heads"),
        P(None, "heads"),
        P(None, "heads"),
        P(("groups", "depth")),
        P(("groups", "cols")),
    )
    out_specs = P(("groups", "depth"), "cols", "heads")

    return jax.shard_map(
        on_device, mesh=mesh, in_specs=in_specs, out_specs=out_specs, check_vma=False
    )
```

time: 72.5 us -> 70.6 us (0.974)
  waiting for transfers between devices: 22.5 us -> 30.6 us
  starting transfers between devices: 29 us -> 23.9 us
  Pallas kernels: 19.3 us -> 14.5 us
    ppermute x15, waiting for transfers between devices: 6.83 us -> 12.7 us  [exchange(): received.append(lax.ppermute(values[k], 'depth', swapped))]
    ppermute x15, starting transfers between devices: 25.3 us -> 20.1 us  [exchange(): received.append(lax.ppermute(values[k], 'depth', swapped))]
    pallas_call x16, Pallas kernels: 19.3 us -> 14.5 us  [run(): out = fn(*args)]
    ppermute x6, waiting for transfers between devices: 15.7 us -> 17.8 us  [from_behind(): lax.ppermute(value, axis, [(s, (s + steps) % count) for s in range(count)])]
  transfers between devices with their start and end apart: 21 -> 21, of which waited for: 6 -> 10; matrix products, arithmetic and copies ran while one was open for 0% -> 2% of each run, Pallas kernels for 23% -> 14%
where the time goes in v3:
time: 70.6 us; the launch traced here: 70.4 us
  waiting for transfers between devices  30.6 us (43%)
  starting transfers between devices  23.9 us (34%)
  Pallas kernels  14.5 us (21%)
  local copies, waits for them, and re-layouts  1.15 us (2%)
    ppermute x15, starting transfers between devices, exchange(): received.append(lax.ppermute(values[k], 'depth', swapped))  20.1 us
    ppermute x6, waiting for transfers between devices, from_behind(): lax.ppermute(value, axis, [(s, (s + steps) % count) for s in range(count)])  17.8 us
    pallas_call x16, Pallas kernels, run(): out = fn(*args)  14.5 us
    ppermute x15, waiting for transfers between devices, exchange(): received.append(lax.ppermute(values[k], 'depth', swapped))  12.7 us
    ppermute x6, starting transfers between devices, from_behind(): lax.ppermute(value, axis, [(s, (s + steps) % count) for s in range(count)])  3.77 us
  transfers between devices with their start and end apart: 21, of which 10 were waited for; matrix products, arithmetic and copies ran while one was open for 2% of the time, Pallas kernels for 14%

profile of v3, /device:TPU:0, one launch (start us, length us, event | category | flops | bytes accessed | tf_op | source)
XLA Modules:
  0.0 70.4 jit_solution(6120118476878498876)
XLA Ops:
  0.0 2.5 %shard_map.82 = (bf16[8,128,768]{2,1,0:T(8,128)(2,1)S(1)}, bf16[272,768]{1,0:T(8,128)(2,1)}) custom-call(s32[1,128]{1,0:T(1,128)} %bitcast.6, bf16[8,128,768]{2,1,0:T(8,128)(2,1)} %rows_in.1), custom_call_target="tpu_custom_call" | custom-call | bytes 3981312 | tf_op jit(solution)/shard_map/pallas_call | solution.py:57
  2.6 3.0 %collective-permute-start = (bf16[272,768]{1,0:T(8,128)(2,1)}, bf16[272,768]{1,0:T(8,128)(2,1)S(1)}, u32[]{:S(2)}, u32[]{:S(2)}) collective-permute-start(bf16[272,768]{1,0:T(8,128)(2,1)} %get-tuple-element.31), channel_id=1, source_target_pairs={{0,2},{2,0},{1,3},{3,1},{4,6},{6,4},{5,7},{7,5},{8,10},{10,8},{9,1... | collective-permute-start | bytes 1253384 | tf_op jit(solution)/shard_map/ppermute | solution.py:28
  5.6 1.0 %constant_dynamic-slice_fusion = bf16[4,64,768]{2,1,0:T(8,128)(2,1)S(1)} fusion(bf16[8,128,768]{2,1,0:T(8,128)(2,1)} %rows_in.1, s32[]{:T(128)S(6)} %select_n.3), kind=kLoop, calls=%fused_computation.2 | loop fusion | bytes 786436 | tf_op jit(solution)/shard_map/dynamic_slice | solution.py:445
  6.6 0.1 collective-permute-start.4
  6.7 9.6 %collective-permute-done.part = bf16[272,768]{1,0:T(8,128)(2,1)S(1)} collective-permute-done((bf16[272,768]{1,0:T(8,128)(2,1)}, bf16[272,768]{1,0:T(8,128)(2,1)S(1)}, u32[]{:S(2)}, u32[]{:S(2)}) %collective-permute-start) | collective-permute-done | bytes 417824 | tf_op jit(solution)/shard_map/ppermute | solution.py:28
  16.3 0.0 collective-permute-start.12
  16.3 7.6 %collective-permute-done.4.part = bf16[256,768]{1,0:T(8,128)(2,1)S(1)} collective-permute-done((bf16[256,768]{1,0:T(8,128)(2,1)S(1)}, bf16[256,768]{1,0:T(8,128)(2,1)S(1)}, u32[]{:S(2)}, u32[]{:S(2)}) %collective-permute-start.4) | collective-permute-done | bytes 393248 | tf_op jit(solution)/shard_map/ppermute | solution.py:28
  23.9 0.0 collective-permute-start.5
  23.9 0.0 copy-done.4
  23.9 0.0 copy-done.6
  23.9 0.1 broadcast_in_dim.6.live
  24.0 2.4 %shard_map.83 = (bf16[4,256,768]{2,1,0:T(8,128)(2,1)S(1)}, bf16[4,3,256,256]{3,2,1,0:T(8,128)(2,1)S(1)}, f32[200,128]{1,0:T(8,128)S(1)}, f32[200,128]{1,0:T(8,12...) custom-call(f32[8,128]{1,0:T(8,128)S(1)} %broadcast_in_dim.6.live, ...), custom_call_target="tpu_custom_call" | custom-call | flops 1207959552 | bytes 7110656 | tf_op jit(solution)/shard_map/pallas_call | solution.py:57
  26.4 1.9 %collective-permute-start.1 = (f32[200,128]{1,0:T(8,128)S(1)}, f32[200,128]{1,0:T(8,128)S(1)}, u32[]{:S(2)}, u32[]{:S(2)}) collective-permute-start(f32[200,128]{1,0:T(8,128)S(1)} %get-tuple-element.34), channel_id=1, source_target_pairs={{0,4},{4,0},{8,12},{12,8},{1,5},{5,1},{9,13},{13,9},{2,6},{6,2},{1... | collective-permute-start | bytes 307208 | tf_op jit(solution)/shard_map/ppermute | solution.py:475
  28.3 2.6 %collective-permute-start.2 = (f32[200,128]{1,0:T(8,128)S(1)}, f32[200,128]{1,0:T(8,128)S(1)}, u32[]{:S(2)}, u32[]{:S(2)}) collective-permute-start(f32[200,128]{1,0:T(8,128)S(1)} %get-tuple-element.35), channel_id=1, source_target_pairs={{0,8},{4,12},{8,0},{12,4},{1,9},{5,13},{9,1},{13,5},{2,10},{6,14},... | collective-permute-start | bytes 307208 | tf_op jit(solution)/shard_map/ppermute | solution.py:475
  30.9 0.0 collective-permute-start.3
  30.9 1.0 %shard_map.84 = (bf16[256,768]{1,0:T(8,128)(2,1)S(1)}, f32[3,128,128]{2,1,0:T(8,128)S(1)}) custom-call(bf16[256,768]{1,0:T(8,128)(2,1)S(1)} %collective-permute-done.4.part, f32[1,768]{1,0:T(1,128)S(1)} %broadcast_in_dim.15.gain, bf16[768,384]{1,0:T(8,128)(2,1)S(1)} %copy-done, bf16[4,3,256,256]{3,2,1,0:T(8,128)(2,1)S(1)} %get-tuple-element.37.query), custom_call_target="tpu_custom_call" | custom-call | flops 150994944 | bytes 1179648 | tf_op jit(solution)/shard_map/pallas_call | solution.py:57
  31.9 1.0 %shard_map.87 = (bf16[256,768]{1,0:T(8,128)(2,1)S(1)}, f32[3,128,128]{2,1,0:T(8,128)S(1)}) custom-call(bf16[272,768]{1,0:T(8,128)(2,1)S(1)} %collective-permute-done.part, f32[1,768]{1,0:T(1,128)S(1)} %broadcast_in_dim.15.gain, bf16[768,384]{1,0:T(8,128)(2,1)S(1)} %copy-done, bf16[4,3,256,256]{3,2,1,0:T(8,128)(2,1)S(1)} %get-tuple-element.37.query), custom_call_target="tpu_custom_call" | custom-call | flops 150994944 | bytes 1179648 | tf_op jit(solution)/shard_map/pallas_call | solution.py:57
  32.9 0.0 collective-permute-done.5.part
  32.9 1.0 %shard_map.85 = (bf16[256,768]{1,0:T(8,128)(2,1)S(1)}, f32[96,128]{1,0:T(8,128)S(1)}, f32[96,128]{1,0:T(8,128)S(1)}, f32[96,128]{1,0:T(8,128)S(1)}, f32[96,128]{1,0:T(8,128)S(1)}) custom-call(bf16[256,768]{1,0:T(8,128)(2,1)S(1)} %collective-permute-done.5.part, f32[1,768]{1,0:T(1,128)S(1)} %broadcast_in_dim.15.gain, bf16[768,384]{1,0:T(8,128)(2,1)S(1)} %copy-done, ...), custom_call_target="tpu_custom_call" | custom-call | flops 150994944 | bytes 1179648 | tf_op jit(solution)/shard_map/pallas_call | solution.py:57
  33.9 1.0 %collective-permute-start.6 = (f32[96,128]{1,0:T(8,128)S(1)}, f32[96,128]{1,0:T(8,128)S(1)}, u32[]{:S(2)}, u32[]{:S(2)}) collective-permute-start(f32[96,128]{1,0:T(8,128)S(1)} %get-tuple-element.40), channel_id=1, source_target_pairs={{0,4},{4,0},{8,12},{12,8},{1,5},{5,1},{9,13},{13,9},{2,6},{6,2},{1... | collective-permute-start | bytes 147464 | tf_op jit(solution)/shard_map/ppermute | solution.py:475
  34.8 0.0 collective-permute-done.12.part
  34.8 3.5 %collective-permute-start.7 = (f32[96,128]{1,0:T(8,128)S(1)}, f32[96,128]{1,0:T(8,128)S(1)}, u32[]{:S(2)}, u32[]{:S(2)}) collective-permute-start(f32[96,128]{1,0:T(8,128)S(1)} %get-tuple-element.41), channel_id=1, source_target_pairs={{0,8},{4,12},{8,0},{12,4},{1,9},{5,13},{9,1},{13,5},{2,10},{6,14},... | collective-permute-start | bytes 147464 | tf_op jit(solution)/shard_map/ppermute | solution.py:475
  38.3 1.0 %shard_map.88 = (bf16[256,768]{1,0:T(8,128)(2,1)S(1)}, f32[96,128]{1,0:T(8,128)S(1)}, f32[96,128]{1,0:T(8,128)S(1)}, f32[96,128]{1,0:T(8,128)S(1)}, f32[96,128]{1,0:T(8,128)S(1)}) custom-call(bf16[272,768]{1,0:T(8,128)(2,1)S(1)} %collective-permute-done.12.part, f32[1,768]{1,0:T(1,128)S(1)} %broadcast_in_dim.15.gain, bf16[768,384]{1,0:T(8,128)(2,1)S(1)} %copy-done, ...), custom_call_target="tpu_custom_call" | custom-call | flops 150994944 | bytes 1179648 | tf_op jit(solution)/shard_map/pallas_call | solution.py:57
  39.3 0.0 collective-permute-done.1.rest_3_
  39.3 0.1 collective-permute-start.8
  39.4 0.5 collective-permute-done.2.rest_4_
  39.9 0.1 collective-permute-start.13
  40.0 0.0 collective-permute-done.3.rest_5_
  40.0 0.0 collective-permute-done.6.rest_7_
  40.0 4.0 %collective-permute-done.7.rest_8_ = f32[96,128]{1,0:T(8,128)S(1)} collective-permute-done((f32[96,128]{1,0:T(8,128)S(1)}, f32[96,128]{1,0:T(8,128)S(1)}, u32[]{:S(2)}, u32[]{:S(2)}) %collective-permute-start.7) | collective-permute-done | bytes 49184 | tf_op jit(solution)/shard_map/ppermute | solution.py:475
  44.0 1.3 %collective-permute-done.8.rest_9_ = f32[96,128]{1,0:T(8,128)S(1)} collective-permute-done((f32[96,128]{1,0:T(8,128)S(1)}, f32[96,128]{1,0:T(8,128)S(1)}, u32[]{:S(2)}, u32[]{:S(2)}) %collective-permute-start.8) | collective-permute-done | bytes 49184 | tf_op jit(solution)/shard_map/ppermute | solution.py:475
  45.3 0.3 shard_map.86
  45.6 1.4 %collective-permute-start.10 = (bf16[288,128]{1,0:T(8,128)(2,1)S(1)}, bf16[288,128]{1,0:T(8,128)(2,1)S(1)}, u32[]{:S(2)}, u32[]{:S(2)}) collective-permute-start(bf16[288,128]{1,0:T(8,128)(2,1)S(1)} %get-tuple-element.43.rest_0_), channel_id=1, source_target_pairs={{0,8},{4,12},{8,0},{12,4},{1,9},{5,13},{9,1},{13,5},{2,10},{6,14},... | collective-permute-start | bytes 221192 | tf_op jit(solution)/shard_map/ppermute | solution.py:475
  47.0 0.8 %collective-permute-start.11 = (bf16[288,128]{1,0:T(8,128)(2,1)S(1)}, bf16[288,128]{1,0:T(8,128)(2,1)S(1)}, u32[]{:S(2)}, u32[]{:S(2)}) collective-permute-start(bf16[288,128]{1,0:T(8,128)(2,1)S(1)} %get-tuple-element.43.rest_0_), channel_id=1, source_target_pairs={{0,12},{4,8},{8,4},{12,0},{1,13},{5,9},{9,5},{13,1},{2,14},{6,10},... | collective-permute-start | bytes 221192 | tf_op jit(solution)/shard_map/ppermute | solution.py:475
  47.8 1.3 %collective-permute-start.9 = (bf16[288,128]{1,0:T(8,128)(2,1)S(1)}, bf16[288,128]{1,0:T(8,128)(2,1)S(1)}, u32[]{:S(2)}, u32[]{:S(2)}) collective-permute-start(bf16[288,128]{1,0:T(8,128)(2,1)S(1)} %get-tuple-element.43.rest_0_), channel_id=1, source_target_pairs={{0,4},{4,0},{8,12},{12,8},{1,5},{5,1},{9,13},{13,9},{2,6},{6,2},{1... | collective-permute-start | bytes 221192 | tf_op jit(solution)/shard_map/ppermute | solution.py:475
  49.1 2.2 %collective-permute-start.14 = (f32[96,128]{1,0:T(8,128)S(1)}, f32[96,128]{1,0:T(8,128)S(1)}, u32[]{:S(2)}, u32[]{:S(2)}) collective-permute-start(f32[96,128]{1,0:T(8,128)S(1)} %get-tuple-element.48), channel_id=1, source_target_pairs={{0,8},{4,12},{8,0},{12,4},{1,9},{5,13},{9,1},{13,5},{2,10},{6,14},... | collective-permute-start | bytes 147464 | tf_op jit(solution)/shard_map/ppermute | solution.py:475
  51.4 0.0 collective-permute-done.13.rest_3_
  51.4 0.8 %collective-permute-start.15 = (f32[96,128]{1,0:T(8,128)S(1)}, f32[96,128]{1,0:T(8,128)S(1)}, u32[]{:S(2)}, u32[]{:S(2)}) collective-permute-start(f32[96,128]{1,0:T(8,128)S(1)} %get-tuple-element.49), channel_id=1, source_target_pairs={{0,12},{4,8},{8,4},{12,0},{1,13},{5,9},{9,5},{13,1},{2,14},{6,10},... | collective-permute-start | bytes 147464 | tf_op jit(solution)/shard_map/ppermute | solution.py:475
  52.2 1.0 %shard_map.90.rest_8_.rest_1_ = bf16[4,3,128,256]{3,2,1,0:T(8,128)(2,1)S(1)} custom-call(bf16[4,256,768]{2,1,0:T(8,128)(2,1)S(1)} %get-tuple-element.50.normed, bf16[768,384]{1,0:T(8,128)(2,1)S(1)} %copy-done.1), custom_call_target="tpu_custom_call" | custom-call | flops 603979776 | bytes 1572864 | tf_op jit(solution)/shard_map/pallas_call | solution.py:57
  53.2 3.5 %collective-permute-done.14.rest_4_ = f32[96,128]{1,0:T(8,128)S(1)} collective-permute-done((f32[96,128]{1,0:T(8,128)S(1)}, f32[96,128]{1,0:T(8,128)S(1)}, u32[]{:S(2)}, u32[]{:S(2)}) %collective-permute-start.14) | collective-permute-done | bytes 49184 | tf_op jit(solution)/shard_map/ppermute | solution.py:475
  56.7 0.7 collective-permute-done.15.rest_5_
  57.4 0.3 shard_map.89.rest_4_
  57.6 1.0 %collective-permute-start.16 = (bf16[112,128]{1,0:T(8,128)(2,1)S(1)}, bf16[112,128]{1,0:T(8,128)(2,1)S(1)}, u32[]{:S(2)}, u32[]{:S(2)}) collective-permute-start(bf16[112,128]{1,0:T(8,128)(2,1)S(1)} %shard_map.89.rest_4_), channel_id=1, source_target_pairs={{0,4},{4,0},{8,12},{12,8},{1,5},{5,1},{9,13},{13,9},{2,6},{6,2},{1... | collective-permute-start | bytes 86024 | tf_op jit(solution)/shard_map/ppermute | solution.py:475
  58.6 1.7 %collective-permute-start.17 = (bf16[112,128]{1,0:T(8,128)(2,1)S(1)}, bf16[112,128]{1,0:T(8,128)(2,1)S(1)}, u32[]{:S(2)}, u32[]{:S(2)}) collective-permute-start(bf16[112,128]{1,0:T(8,128)(2,1)S(1)} %shard_map.89.rest_4_), channel_id=1, source_target_pairs={{0,8},{4,12},{8,0},{12,4},{1,9},{5,13},{9,1},{13,5},{2,10},{6,14},... | collective-permute-start | bytes 86024 | tf_op jit(solution)/shard_map/ppermute | solution.py:475
  60.3 0.0 collective-permute-done.10.rest_2_
  60.3 1.8 %collective-permute-start.18 = (bf16[112,128]{1,0:T(8,128)(2,1)S(1)}, bf16[112,128]{1,0:T(8,128)(2,1)S(1)}, u32[]{:S(2)}, u32[]{:S(2)}) collective-permute-start(bf16[112,128]{1,0:T(8,128)(2,1)S(1)} %shard_map.89.rest_4_), channel_id=1, source_target_pairs={{0,12},{4,8},{8,4},{12,0},{1,13},{5,9},{9,5},{13,1},{2,14},{6,10},... | collective-permute-start | bytes 86024 | tf_op jit(solution)/shard_map/ppermute | solution.py:475
  62.1 0.6 shard_map.91.rest_9_.rest_2_
  62.7 0.6 shard_map.92.rest_10_.rest_3_
  63.2 0.0 collective-permute-done.11.rest_3_
  63.3 0.0 collective-permute-done.9.rest_1_
  63.3 0.0 collective-permute-done.16.rest_5_
  63.3 0.1 collective-permute-done.17.rest_6_
  63.4 2.6 %collective-permute-done.18.rest_7_ = bf16[112,128]{1,0:T(8,128)(2,1)S(1)} collective-permute-done((bf16[112,128]{1,0:T(8,128)(2,1)S(1)}, bf16[112,128]{1,0:T(8,128)(2,1)S(1)}, u32[]{:S(2)}, u32[]{:S(2)}) %collective-permute-start.18) | collective-permute-done | bytes 28704 | tf_op jit(solution)/shard_map/ppermute | solution.py:475
  66.0 0.7 %shard_map.93 = (bf16[4,128,384]{2,1,0:T(8,128)(2,1)S(1)}, bf16[3,256,256]{2,1,0:T(8,128)(2,1)S(1)}) custom-call(bf16[288,128]{1,0:T(8,128)(2,1)S(1)} %get-tuple-element.43.rest_0_, bf16[288,128]{1,0:T(8,128)(2,1)S(1)} %collective-permute-done.9.rest_1_, bf16[288,128]{1,0:T(8,128)(2,1)S(1)} %collective-permute-done.10.rest_2_, ...), custom_call_target="tpu_custom_call" | custom-call | flops 100663296 | bytes 1572864 | tf_op jit(solution)/shard_map/pallas_call | solution.py:57
  66.7 0.0 copy-start.2
  66.7 0.1 collective-permute-start.20
  66.8 0.4 shard_map.94.rest_0_
  67.2 0.6 collective-permute-start.19
  67.7 0.0 copy-done.2
  67.8 0.1 shard_map.95.rest_2_
  67.8 0.7 collective-permute-done.20.rest_1_
  68.5 0.6 shard_map.96.rest_3_
  69.1 0.0 collective-permute-done.19.rest_1_
  69.1 1.3 %shard_map.97 = bf16[8,128,384]{2,1,0:T(8,128)(2,1)} custom-call(f32[8,128]{1,0:T(8,128)S(1)} %broadcast_in_dim.6.live, bf16[4,128,384]{2,1,0:T(8,128)(2,1)S(1)} %shard_map.94.rest_0_, bf16[4,128,384]{2,1,0:T(8,128)(2,1)S(1)} %collective-permute-done.19.rest_1_, bf16[768,384]{1,0:T(8,128)(2,1)S(1)} %shard_map.95.rest_2_, ...), custom_call_target="tpu_custom_call" | custom-call | flops 150994944 | bytes 1572864 | tf_op jit(solution)/shard_map/pallas_call | solution.py:57
  (14 shorter events, 0.0 us)
Async XLA Ops:
  0.0 23.9 %copy-start.4 = (f32[768]{0:T(1024)S(1)}, f32[768]{0:T(1024)}, u32[]{:S(2)}) copy-start(f32[768]{0:T(1024)} %param.9) | copy-start | bytes 9220
  0.0 23.9 %copy-start.6 = (s32[8]{0:T(128)S(1)}, s32[8]{0:T(128)}, u32[]{:S(2)}) copy-start(s32[8]{0:T(128)} %param.14) | copy-start | bytes 100
  0.0 24.0 %copy-start.3 = (bf16[768,384]{1,0:T(8,128)(2,1)S(1)}, bf16[768,384]{1,0:T(8,128)(2,1)}, u32[]{:S(2)}) copy-start(bf16[768,384]{1,0:T(8,128)(2,1)} %w_query.1) | copy-start | bytes 1769476
  0.0 24.0 %copy-start = (bf16[768,384]{1,0:T(8,128)(2,1)S(1)}, bf16[768,384]{1,0:T(8,128)(2,1)}, u32[]{:S(2)}) copy-start(bf16[768,384]{1,0:T(8,128)(2,1)} %w_key.9) | copy-start | bytes 1769476
  2.6 13.7 %collective-permute-start = (bf16[272,768]{1,0:T(8,128)(2,1)}, bf16[272,768]{1,0:T(8,128)(2,1)S(1)}, u32[]{:S(2)}, u32[]{:S(2)}) collective-permute-start(bf16[272,768]{1,0:T(8,128)(2,1)} %get-tuple-element.31), channel_id=1, source_target_pairs={{0,2},{2,0},{1,3},{3,1},{4,6},{6,4},{5,7},{7,5},{8,10},{10,8},{9,1... | collective-permute-start | bytes 1253384 | tf_op jit(solution)/shard_map/ppermute | solution.py:28
  6.6 17.3 %collective-permute-start.4 = (bf16[256,768]{1,0:T(8,128)(2,1)S(1)}, bf16[256,768]{1,0:T(8,128)(2,1)S(1)}, u32[]{:S(2)}, u32[]{:S(2)}) collective-permute-start(bf16[256,768]{1,0:T(8,128)(2,1)S(1)} %bitcast.5), channel_id=1, source_target_pairs={{0,2},{2,0},{1,3},{3,1},{4,6},{6,4},{5,7},{7,5},{8,10},{10,8},{9,1... | collective-permute-start | bytes 1179656 | tf_op jit(solution)/shard_map/ppermute | solution.py:28
  16.3 18.5 %collective-permute-start.12 = (bf16[272,768]{1,0:T(8,128)(2,1)S(1)}, bf16[272,768]{1,0:T(8,128)(2,1)S(1)}, u32[]{:S(2)}, u32[]{:S(2)}) collective-permute-start(bf16[272,768]{1,0:T(8,128)(2,1)S(1)} %collective-permute-done.part), channel_id=1, source_target_pairs={{0,1},{1,0},{2,3},{3,2},{4,5},{5,4},{6,7},{7,6},{8,9},{9,8},{10,11... | collective-permute-start | bytes 1253384 | tf_op jit(solution)/shard_map/ppermute | solution.py:28
  23.9 9.0 %collective-permute-start.5 = (bf16[256,768]{1,0:T(8,128)(2,1)S(1)}, bf16[256,768]{1,0:T(8,128)(2,1)S(1)}, u32[]{:S(2)}, u32[]{:S(2)}) collective-permute-start(bf16[256,768]{1,0:T(8,128)(2,1)S(1)} %collective-permute-done.4.part), channel_id=1, source_target_pairs={{0,1},{1,0},{2,3},{3,2},{4,5},{5,4},{6,7},{7,6},{8,9},{9,8},{10,11... | collective-permute-start | bytes 1179656 | tf_op jit(solution)/shard_map/ppermute | solution.py:28
  24.0 6.9 %copy-start.5 = (s32[128]{0:T(128)S(1)}, s32[128]{0:T(128)}, u32[]{:S(2)}) copy-start(s32[128]{0:T(128)} %param.15) | copy-start | bytes 1540
  26.4 12.9 %collective-permute-start.1 = (f32[200,128]{1,0:T(8,128)S(1)}, f32[200,128]{1,0:T(8,128)S(1)}, u32[]{:S(2)}, u32[]{:S(2)}) collective-permute-start(f32[200,128]{1,0:T(8,128)S(1)} %get-tuple-element.34), channel_id=1, source_target_pairs={{0,4},{4,0},{8,12},{12,8},{1,5},{5,1},{9,13},{13,9},{2,6},{6,2},{1... | collective-permute-start | bytes 307208 | tf_op jit(solution)/shard_map/ppermute | solution.py:475
  28.3 11.6 %collective-permute-start.2 = (f32[200,128]{1,0:T(8,128)S(1)}, f32[200,128]{1,0:T(8,128)S(1)}, u32[]{:S(2)}, u32[]{:S(2)}) collective-permute-start(f32[200,128]{1,0:T(8,128)S(1)} %get-tuple-element.35), channel_id=1, source_target_pairs={{0,8},{4,12},{8,0},{12,4},{1,9},{5,13},{9,1},{13,5},{2,10},{6,14},... | collective-permute-start | bytes 307208 | tf_op jit(solution)/shard_map/ppermute | solution.py:475
  30.9 9.1 %collective-permute-start.3 = (f32[200,128]{1,0:T(8,128)S(1)}, f32[200,128]{1,0:T(8,128)S(1)}, u32[]{:S(2)}, u32[]{:S(2)}) collective-permute-start(f32[200,128]{1,0:T(8,128)S(1)} %get-tuple-element.36), channel_id=1, source_target_pairs={{0,12},{4,8},{8,4},{12,0},{1,13},{5,9},{9,5},{13,1},{2,14},{6,10},... | collective-permute-start | bytes 307208 | tf_op jit(solution)/shard_map/ppermute | solution.py:475
  33.9 6.1 %collective-permute-start.6 = (f32[96,128]{1,0:T(8,128)S(1)}, f32[96,128]{1,0:T(8,128)S(1)}, u32[]{:S(2)}, u32[]{:S(2)}) collective-permute-start(f32[96,128]{1,0:T(8,128)S(1)} %get-tuple-element.40), channel_id=1, source_target_pairs={{0,4},{4,0},{8,12},{12,8},{1,5},{5,1},{9,13},{13,9},{2,6},{6,2},{1... | collective-permute-start | bytes 147464 | tf_op jit(solution)/shard_map/ppermute | solution.py:475
  34.8 9.2 %collective-permute-start.7 = (f32[96,128]{1,0:T(8,128)S(1)}, f32[96,128]{1,0:T(8,128)S(1)}, u32[]{:S(2)}, u32[]{:S(2)}) collective-permute-start(f32[96,128]{1,0:T(8,128)S(1)} %get-tuple-element.41), channel_id=1, source_target_pairs={{0,8},{4,12},{8,0},{12,4},{1,9},{5,13},{9,1},{13,5},{2,10},{6,14},... | collective-permute-start | bytes 147464 | tf_op jit(solution)/shard_map/ppermute | solution.py:475
  38.3 13.9 %copy-start.1 = (bf16[768,384]{1,0:T(8,128)(2,1)S(1)}, bf16[768,384]{1,0:T(8,128)(2,1)}, u32[]{:S(2)}) copy-start(bf16[768,384]{1,0:T(8,128)(2,1)} %refs_2_.3) | copy-start | bytes 1769476
  39.3 6.0 %collective-permute-start.8 = (f32[96,128]{1,0:T(8,128)S(1)}, f32[96,128]{1,0:T(8,128)S(1)}, u32[]{:S(2)}, u32[]{:S(2)}) collective-permute-start(f32[96,128]{1,0:T(8,128)S(1)} %get-tuple-element.42), channel_id=1, source_target_pairs={{0,12},{4,8},{8,4},{12,0},{1,13},{5,9},{9,5},{13,1},{2,14},{6,10},... | collective-permute-start | bytes 147464 | tf_op jit(solution)/shard_map/ppermute | solution.py:475
  39.9 11.4 %collective-permute-start.13 = (f32[96,128]{1,0:T(8,128)S(1)}, f32[96,128]{1,0:T(8,128)S(1)}, u32[]{:S(2)}, u32[]{:S(2)}) collective-permute-start(f32[96,128]{1,0:T(8,128)S(1)} %get-tuple-element.47), channel_id=1, source_target_pairs={{0,4},{4,0},{8,12},{12,8},{1,5},{5,1},{9,13},{13,9},{2,6},{6,2},{1... | collective-permute-start | bytes 147464 | tf_op jit(solution)/shard_map/ppermute | solution.py:475
  45.6 14.8 %collective-permute-start.10 = (bf16[288,128]{1,0:T(8,128)(2,1)S(1)}, bf16[288,128]{1,0:T(8,128)(2,1)S(1)}, u32[]{:S(2)}, u32[]{:S(2)}) collective-permute-start(bf16[288,128]{1,0:T(8,128)(2,1)S(1)} %get-tuple-element.43.rest_0_), channel_id=1, source_target_pairs={{0,8},{4,12},{8,0},{12,4},{1,9},{5,13},{9,1},{13,5},{2,10},{6,14},... | collective-permute-start | bytes 221192 | tf_op jit(solution)/shard_map/ppermute | solution.py:475
  47.0 16.3 %collective-permute-start.11 = (bf16[288,128]{1,0:T(8,128)(2,1)S(1)}, bf16[288,128]{1,0:T(8,128)(2,1)S(1)}, u32[]{:S(2)}, u32[]{:S(2)}) collective-permute-start(bf16[288,128]{1,0:T(8,128)(2,1)S(1)} %get-tuple-element.43.rest_0_), channel_id=1, source_target_pairs={{0,12},{4,8},{8,4},{12,0},{1,13},{5,9},{9,5},{13,1},{2,14},{6,10},... | collective-permute-start | bytes 221192 | tf_op jit(solution)/shard_map/ppermute | solution.py:475
  47.8 15.5 %collective-permute-start.9 = (bf16[288,128]{1,0:T(8,128)(2,1)S(1)}, bf16[288,128]{1,0:T(8,128)(2,1)S(1)}, u32[]{:S(2)}, u32[]{:S(2)}) collective-permute-start(bf16[288,128]{1,0:T(8,128)(2,1)S(1)} %get-tuple-element.43.rest_0_), channel_id=1, source_target_pairs={{0,4},{4,0},{8,12},{12,8},{1,5},{5,1},{9,13},{13,9},{2,6},{6,2},{1... | collective-permute-start | bytes 221192 | tf_op jit(solution)/shard_map/ppermute | solution.py:475
  49.1 7.6 %collective-permute-start.14 = (f32[96,128]{1,0:T(8,128)S(1)}, f32[96,128]{1,0:T(8,128)S(1)}, u32[]{:S(2)}, u32[]{:S(2)}) collective-permute-start(f32[96,128]{1,0:T(8,128)S(1)} %get-tuple-element.48), channel_id=1, source_target_pairs={{0,8},{4,12},{8,0},{12,4},{1,9},{5,13},{9,1},{13,5},{2,10},{6,14},... | collective-permute-start | bytes 147464 | tf_op jit(solution)/shard_map/ppermute | solution.py:475
  51.4 6.0 %collective-permute-start.15 = (f32[96,128]{1,0:T(8,128)S(1)}, f32[96,128]{1,0:T(8,128)S(1)}, u32[]{:S(2)}, u32[]{:S(2)}) collective-permute-start(f32[96,128]{1,0:T(8,128)S(1)} %get-tuple-element.49), channel_id=1, source_target_pairs={{0,12},{4,8},{8,4},{12,0},{1,13},{5,9},{9,5},{13,1},{2,14},{6,10},... | collective-permute-start | bytes 147464 | tf_op jit(solution)/shard_map/ppermute | solution.py:475
  57.6 5.6 %collective-permute-start.16 = (bf16[112,128]{1,0:T(8,128)(2,1)S(1)}, bf16[112,128]{1,0:T(8,128)(2,1)S(1)}, u32[]{:S(2)}, u32[]{:S(2)}) collective-permute-start(bf16[112,128]{1,0:T(8,128)(2,1)S(1)} %shard_map.89.rest_4_), channel_id=1, source_target_pairs={{0,4},{4,0},{8,12},{12,8},{1,5},{5,1},{9,13},{13,9},{2,6},{6,2},{1... | collective-permute-start | bytes 86024 | tf_op jit(solution)/shard_map/ppermute | solution.py:475
  58.6 4.8 %collective-permute-start.17 = (bf16[112,128]{1,0:T(8,128)(2,1)S(1)}, bf16[112,128]{1,0:T(8,128)(2,1)S(1)}, u32[]{:S(2)}, u32[]{:S(2)}) collective-permute-start(bf16[112,128]{1,0:T(8,128)(2,1)S(1)} %shard_map.89.rest_4_), channel_id=1, source_target_pairs={{0,8},{4,12},{8,0},{12,4},{1,9},{5,13},{9,1},{13,5},{2,10},{6,14},... | collective-permute-start | bytes 86024 | tf_op jit(solution)/shard_map/ppermute | solution.py:475
  60.3 5.7 %collective-permute-start.18 = (bf16[112,128]{1,0:T(8,128)(2,1)S(1)}, bf16[112,128]{1,0:T(8,128)(2,1)S(1)}, u32[]{:S(2)}, u32[]{:S(2)}) collective-permute-start(bf16[112,128]{1,0:T(8,128)(2,1)S(1)} %shard_map.89.rest_4_), channel_id=1, source_target_pairs={{0,12},{4,8},{8,4},{12,0},{1,13},{5,9},{9,5},{13,1},{2,14},{6,10},... | collective-permute-start | bytes 86024 | tf_op jit(solution)/shard_map/ppermute | solution.py:475
  66.7 1.1 %copy-start.2 = (bf16[768,384]{1,0:T(8,128)(2,1)S(1)}, bf16[768,384]{1,0:T(8,128)(2,1)}, u32[]{:S(2)}) copy-start(bf16[768,384]{1,0:T(8,128)(2,1)} %w_out.1) | copy-start | bytes 1769476
  66.7 1.8 %collective-permute-start.20 = (bf16[4,128,384]{2,1,0:T(8,128)(2,1)S(1)}, bf16[4,128,384]{2,1,0:T(8,128)(2,1)S(1)}, u32[]{:S(2)}, u32[]{:S(2)}) collective-permute-start(bf16[4,128,384]{2,1,0:T(8,128)(2,1)S(1)} %get-tuple-element.56.rest_0_), channel_id=1, source_target_pairs={{0,1},{1,0},{2,3},{3,2},{4,5},{5,4},{6,7},{7,6},{8,9},{9,8},{10,11... | collective-permute-start | bytes 1179656 | tf_op jit(solution)/shard_map/ppermute | solution.py:28
  67.2 1.9 %collective-permute-start.19 = (bf16[4,128,384]{2,1,0:T(8,128)(2,1)S(1)}, bf16[4,128,384]{2,1,0:T(8,128)(2,1)S(1)}, u32[]{:S(2)}, u32[]{:S(2)}) collective-permute-start(bf16[4,128,384]{2,1,0:T(8,128)(2,1)S(1)} %shard_map.94.rest_0_), channel_id=1, source_target_pairs={{0,1},{1,0},{2,3},{3,2},{4,5},{5,4},{6,7},{7,6},{8,9},{9,8},{10,11... | collective-permute-start | bytes 1179656 | tf_op jit(solution)/shard_map/ppermute | solution.py:28

commit v4 on v3

--- a/solution.py
+++ b/solution.py
@@ -111,9 +111,9 @@
     count = len(shards)
     part = cols // count
     for k, shard in enumerate(shards):
-        begin = pl.multiple_of(lax.bitwise_xor(depth_index, k) * part, part)
+        begin = lax.bitwise_xor(depth_index, k) * part if count > 1 else 0
         for slot in range(slots):
-            rows = total[slot, pl.ds(begin, part), :]
+            rows = total[slot, pl.ds(pl.multiple_of(begin, part), part), :]
             shard[slot * part : (slot + 1) * part, :] = rows
 
 
@@ -383,26 +383,38 @@
         ordered[k * local : (k + 1) * local, :] = rows
 
 
-def projected(live, parts, weights, first):
+def mine_kernel(*rest):
+    parts, weights, out = rest[:-2], rest[-2], rest[-1]
     size, cols, local = parts[0].shape
-    blocks = [part[...].reshape(size * cols, local) for part in parts]
-    total = dot(jnp.concatenate(blocks, axis=1), weights[...])
+    for side, part in enumerate(parts):
+        rows = part[...].reshape(size * cols, local)
+        total = dot(rows, weights[0:local, :])
+        out[side * size : (side + 1) * size] = total.reshape(size, cols, local)
+
+
+def projected(live, half, parts, weights, begin, first):
+    cols, local = parts[0].shape[1], parts[0].shape[2]
+    blocks = [part[begin : begin + SIZE].reshape(SIZE * cols, local) for part in parts]
+    block = jnp.concatenate(blocks, axis=1) if len(blocks) > 1 else blocks[0]
+    at = first + begin
+    total = dot(block, weights[local:, :]) + half[at : at + SIZE].reshape(SIZE * cols, local)
     results = []
-    for r in range(size):
-        scale = live[first + r : first + r + 1, :]
-        scale = jnp.concatenate([scale] * (total.shape[1] // LANES), axis=1)
+    for r in range(SIZE):
+        scale = live[at + r : at + r + 1, :]
+        scale = jnp.concatenate([scale] * (local // LANES), axis=1)
         results.append((total[r * cols : (r + 1) * cols] * scale).astype(BF16))
     return results
 
 
-def project_kernel(live, *rest, cores, first):
-    parts, weights, out = rest[:cores], rest[cores], rest[cores + 1]
-    for r, rows in enumerate(projected(live, parts, weights, first)):
-        out[r] = rows
-
-
-def finish_kernel(live, *rest, cores):
-    parts, weights, ready = rest[:cores], rest[cores], rest[cores + 1 : -3]
+def project_kernel(live, half, *rest, first):
+    parts, weights, out = rest[:-2], rest[-2], rest[-1]
+    for begin in range(0, out.shape[0], SIZE):
+        for r, rows in enumerate(projected(live, half, parts, weights, begin, first)):
+            out[begin + r] = rows
+
+
+def finish_kernel(live, half, *rest, cores):
+    parts, weights, ready = rest[: cores - 1], rest[cores - 1], rest[cores:-3]
     out, buffer, sems = rest[-3:]
     size = buffer.shape[0]
     copies = []
@@ -410,11 +422,13 @@
         copies.append(pltpu.make_async_copy(done, out.at[pl.ds(k * size, size)], sems.at[k]))
         copies[-1].start()
     first = len(ready) * size
-    for r, rows in enumerate(projected(live, parts, weights, first)):
-        buffer[r] = rows
-        at = out.at[first + r]
-        copies.append(pltpu.make_async_copy(buffer.at[r], at, sems.at[len(ready) + r]))
-        copies[-1].start()
+    for begin in range(0, size, SIZE):
+        for r, rows in enumerate(projected(live, half, parts, weights, begin, first)):
+            row = begin + r
+            buffer[row] = rows
+            target = out.at[first + row]
+            copies.append(pltpu.make_async_copy(buffer.at[row], target, sems.at[len(ready) + row]))
+            copies[-1].start()
     for copy in copies:
         copy.wait()
 
@@ -593,8 +607,8 @@
         probs = lax.all_gather(probs, "depth", axis=1, tiled=True)
         probs = [probs.reshape(pairs, 2 * cols_here, total_cols)]
 
-    finished = []
     piece = shape((part_rows, cols_here, local_width), BF16)
+    mines, others = [], []
     for side in range(cores):
         gathers = len(probs) // 2
         outs = [piece]
@@ -611,19 +625,27 @@
             ),
             outs,
             [spec()] * (len(probs) + 1 + len(remote_values)),
-            flops=4 * SIZE * cols_here * total_cols * local_width,
+            flops=4 * part_rows * cols_here * total_cols * local_width,
         )(*probs, own_values, *remote_values)
-        mine, probs = mixed[0], mixed[1:] if gathers else probs
-        parts = [mine] + [from_behind(mine, "heads", k) for k in range(1, cores)]
-        if side + 1 < cores:
-            finished.append(
-                call(
-                    functools.partial(project_kernel, cores=cores, first=side * part_rows),
-                    piece,
-                    [spec()] * (cores + 2),
-                    flops=2 * SIZE * cols_here * width * local_width,
-                )(live, *parts, ordered)
-            )
+        mines.append(mixed[0])
+        probs = mixed[1:] if gathers else probs
+        others.append([from_behind(mixed[0], "heads", k) for k in range(1, cores)])
+    half = call(
+        mine_kernel,
+        shape((rows_here, cols_here, local_width), F32),
+        [spec()] * (cores + 1),
+        flops=2 * rows_here * cols_here * local_width * local_width,
+    )(*mines, ordered)
+    finished = []
+    for side in range(cores - 1):
+        finished.append(
+            call(
+                functools.partial(project_kernel, first=side * part_rows),
+                piece,
+                [spec()] * (cores + 2),
+                flops=2 * part_rows * cols_here * width * local_width,
+            )(live, half, *others[side], ordered)
+        )
     return call(
         functools.partial(finish_kernel, cores=cores),
         shape((rows_here, cols_here, local_width), BF16),
@@ -632,9 +654,9 @@
             pltpu.VMEM((part_rows, cols_here, local_width), BF16),
             pltpu.SemaphoreType.DMA((cores - 1 + part_rows,)),
         ],
-        flops=2 * SIZE * cols_here * width * local_width,
+        flops=2 * part_rows * cols_here * width * local_width,
         space=HBM,
-    )(live, *parts, ordered, *finished)
+    )(live, half, *others[cores - 1], ordered, *finished)
 
 
 def solution(mesh):

time: 70.6 us -> 70.4 us (level)
    pallas_call x16 -> x17, Pallas kernels: 14.5 us -> 14.8 us  [run(): out = fn(*args)]
  transfers between devices with their start and end apart: 21 -> 21, of which waited for: 10 -> 10; matrix products, arithmetic and copies ran while one was open for 2% -> 2% of each run, Pallas kernels for 14% -> 15%
where the time goes in v4:
time: 70.4 us; the launch traced here: 70.2 us
  waiting for transfers between devices  30.1 us (43%)
  starting transfers between devices  23.9 us (34%)
  Pallas kernels  14.8 us (21%)
  local copies, waits for them, and re-layouts  1.15 us (2%)
    ppermute x15, starting transfers between devices, exchange(): received.append(lax.ppermute(values[k], 'depth', swapped))  20.1 us
    ppermute x6, waiting for transfers between devices, from_behind(): lax.ppermute(value, axis, [(s, (s + steps) % count) for s in range(count)])  17.4 us
    pallas_call x17, Pallas kernels, run(): out = fn(*args)  14.8 us
    ppermute x15, waiting for transfers between devices, exchange(): received.append(lax.ppermute(values[k], 'depth', swapped))  12.7 us
    ppermute x6, starting transfers between devices, from_behind(): lax.ppermute(value, axis, [(s, (s + steps) % count) for s in range(count)])  3.77 us
  transfers between devices with their start and end apart: 21, of which 10 were waited for; matrix products, arithmetic and copies ran while one was open for 2% of the time, Pallas kernels for 15%

profile of v4, /device:TPU:0, one launch (start us, length us, event | category | flops | bytes accessed | tf_op | source)
XLA Modules:
  0.0 70.2 jit_solution(1288902647452217465)
XLA Ops:
  0.0 2.5 %shard_map.82 = (bf16[8,128,768]{2,1,0:T(8,128)(2,1)S(1)}, bf16[272,768]{1,0:T(8,128)(2,1)}) custom-call(s32[1,128]{1,0:T(1,128)} %bitcast.6, bf16[8,128,768]{2,1,0:T(8,128)(2,1)} %rows_in.1), custom_call_target="tpu_custom_call" | custom-call | bytes 3981312 | tf_op jit(solution)/shard_map/pallas_call | solution.py:57
  2.6 3.0 %collective-permute-start = (bf16[272,768]{1,0:T(8,128)(2,1)}, bf16[272,768]{1,0:T(8,128)(2,1)S(1)}, u32[]{:S(2)}, u32[]{:S(2)}) collective-permute-start(bf16[272,768]{1,0:T(8,128)(2,1)} %get-tuple-element.31), channel_id=1, source_target_pairs={{0,2},{2,0},{1,3},{3,1},{4,6},{6,4},{5,7},{7,5},{8,10},{10,8},{9,1... | collective-permute-start | bytes 1253384 | tf_op jit(solution)/shard_map/ppermute | solution.py:28
  5.6 1.0 %constant_dynamic-slice_fusion = bf16[4,64,768]{2,1,0:T(8,128)(2,1)S(1)} fusion(bf16[8,128,768]{2,1,0:T(8,128)(2,1)} %rows_in.1, s32[]{:T(128)S(6)} %select_n.3), kind=kLoop, calls=%fused_computation.2 | loop fusion | bytes 786436 | tf_op jit(solution)/shard_map/dynamic_slice | solution.py:459
  6.6 0.1 collective-permute-start.4
  6.7 9.6 %collective-permute-done.part = bf16[272,768]{1,0:T(8,128)(2,1)S(1)} collective-permute-done((bf16[272,768]{1,0:T(8,128)(2,1)}, bf16[272,768]{1,0:T(8,128)(2,1)S(1)}, u32[]{:S(2)}, u32[]{:S(2)}) %collective-permute-start) | collective-permute-done | bytes 417824 | tf_op jit(solution)/shard_map/ppermute | solution.py:28
  16.3 0.0 collective-permute-start.12
  16.3 7.6 %collective-permute-done.4.part = bf16[256,768]{1,0:T(8,128)(2,1)S(1)} collective-permute-done((bf16[256,768]{1,0:T(8,128)(2,1)S(1)}, bf16[256,768]{1,0:T(8,128)(2,1)S(1)}, u32[]{:S(2)}, u32[]{:S(2)}) %collective-permute-start.4) | collective-permute-done | bytes 393248 | tf_op jit(solution)/shard_map/ppermute | solution.py:28
  23.9 0.0 collective-permute-start.5
  23.9 0.0 copy-done.6
  23.9 0.1 broadcast_in_dim.6.live
  24.0 2.4 %shard_map.83 = (bf16[4,256,768]{2,1,0:T(8,128)(2,1)S(1)}, bf16[4,3,256,256]{3,2,1,0:T(8,128)(2,1)S(1)}, f32[200,128]{1,0:T(8,128)S(1)}, f32[200,128]{1,0:T(8,12...) custom-call(f32[8,128]{1,0:T(8,128)S(1)} %broadcast_in_dim.6.live, ...), custom_call_target="tpu_custom_call" | custom-call | flops 1207959552 | bytes 7110656 | tf_op jit(solution)/shard_map/pallas_call | solution.py:57
  26.4 1.9 %collective-permute-start.1 = (f32[200,128]{1,0:T(8,128)S(1)}, f32[200,128]{1,0:T(8,128)S(1)}, u32[]{:S(2)}, u32[]{:S(2)}) collective-permute-start(f32[200,128]{1,0:T(8,128)S(1)} %get-tuple-element.34), channel_id=1, source_target_pairs={{0,4},{4,0},{8,12},{12,8},{1,5},{5,1},{9,13},{13,9},{2,6},{6,2},{1... | collective-permute-start | bytes 307208 | tf_op jit(solution)/shard_map/ppermute | solution.py:489
  28.3 2.6 %collective-permute-start.2 = (f32[200,128]{1,0:T(8,128)S(1)}, f32[200,128]{1,0:T(8,128)S(1)}, u32[]{:S(2)}, u32[]{:S(2)}) collective-permute-start(f32[200,128]{1,0:T(8,128)S(1)} %get-tuple-element.35), channel_id=1, source_target_pairs={{0,8},{4,12},{8,0},{12,4},{1,9},{5,13},{9,1},{13,5},{2,10},{6,14},... | collective-permute-start | bytes 307208 | tf_op jit(solution)/shard_map/ppermute | solution.py:489
  30.9 0.0 collective-permute-start.3
  30.9 1.0 %shard_map.84 = (bf16[256,768]{1,0:T(8,128)(2,1)S(1)}, f32[3,128,128]{2,1,0:T(8,128)S(1)}) custom-call(bf16[256,768]{1,0:T(8,128)(2,1)S(1)} %collective-permute-done.4.part, f32[1,768]{1,0:T(1,128)S(1)} %broadcast_in_dim.15.gain, bf16[768,384]{1,0:T(8,128)(2,1)S(1)} %copy-done, bf16[4,3,256,256]{3,2,1,0:T(8,128)(2,1)S(1)} %get-tuple-element.37.query), custom_call_target="tpu_custom_call" | custom-call | flops 150994944 | bytes 1179648 | tf_op jit(solution)/shard_map/pallas_call | solution.py:57
  31.9 1.0 %shard_map.87 = (bf16[256,768]{1,0:T(8,128)(2,1)S(1)}, f32[3,128,128]{2,1,0:T(8,128)S(1)}) custom-call(bf16[272,768]{1,0:T(8,128)(2,1)S(1)} %collective-permute-done.part, f32[1,768]{1,0:T(1,128)S(1)} %broadcast_in_dim.15.gain, bf16[768,384]{1,0:T(8,128)(2,1)S(1)} %copy-done, bf16[4,3,256,256]{3,2,1,0:T(8,128)(2,1)S(1)} %get-tuple-element.37.query), custom_call_target="tpu_custom_call" | custom-call | flops 150994944 | bytes 1179648 | tf_op jit(solution)/shard_map/pallas_call | solution.py:57
  32.9 0.0 collective-permute-done.5.part
  32.9 1.0 %shard_map.85 = (bf16[256,768]{1,0:T(8,128)(2,1)S(1)}, f32[96,128]{1,0:T(8,128)S(1)}, f32[96,128]{1,0:T(8,128)S(1)}, f32[96,128]{1,0:T(8,128)S(1)}, f32[96,128]{1,0:T(8,128)S(1)}) custom-call(bf16[256,768]{1,0:T(8,128)(2,1)S(1)} %collective-permute-done.5.part, f32[1,768]{1,0:T(1,128)S(1)} %broadcast_in_dim.15.gain, bf16[768,384]{1,0:T(8,128)(2,1)S(1)} %copy-done, ...), custom_call_target="tpu_custom_call" | custom-call | flops 150994944 | bytes 1179648 | tf_op jit(solution)/shard_map/pallas_call | solution.py:57
  33.9 0.9 %collective-permute-start.6 = (f32[96,128]{1,0:T(8,128)S(1)}, f32[96,128]{1,0:T(8,128)S(1)}, u32[]{:S(2)}, u32[]{:S(2)}) collective-permute-start(f32[96,128]{1,0:T(8,128)S(1)} %get-tuple-element.40), channel_id=1, source_target_pairs={{0,4},{4,0},{8,12},{12,8},{1,5},{5,1},{9,13},{13,9},{2,6},{6,2},{1... | collective-permute-start | bytes 147464 | tf_op jit(solution)/shard_map/ppermute | solution.py:489
  34.8 0.0 collective-permute-done.12.part
  34.8 3.5 %collective-permute-start.7 = (f32[96,128]{1,0:T(8,128)S(1)}, f32[96,128]{1,0:T(8,128)S(1)}, u32[]{:S(2)}, u32[]{:S(2)}) collective-permute-start(f32[96,128]{1,0:T(8,128)S(1)} %get-tuple-element.41), channel_id=1, source_target_pairs={{0,8},{4,12},{8,0},{12,4},{1,9},{5,13},{9,1},{13,5},{2,10},{6,14},... | collective-permute-start | bytes 147464 | tf_op jit(solution)/shard_map/ppermute | solution.py:489
  38.3 1.0 %shard_map.88 = (bf16[256,768]{1,0:T(8,128)(2,1)S(1)}, f32[96,128]{1,0:T(8,128)S(1)}, f32[96,128]{1,0:T(8,128)S(1)}, f32[96,128]{1,0:T(8,128)S(1)}, f32[96,128]{1,0:T(8,128)S(1)}) custom-call(bf16[272,768]{1,0:T(8,128)(2,1)S(1)} %collective-permute-done.12.part, f32[1,768]{1,0:T(1,128)S(1)} %broadcast_in_dim.15.gain, bf16[768,384]{1,0:T(8,128)(2,1)S(1)} %copy-done, ...), custom_call_target="tpu_custom_call" | custom-call | flops 150994944 | bytes 1179648 | tf_op jit(solution)/shard_map/pallas_call | solution.py:57
  39.3 0.0 collective-permute-done.1.rest_3_
  39.3 0.1 collective-permute-start.8
  39.4 0.5 collective-permute-done.2.rest_4_
  39.9 0.0 collective-permute-start.13
  40.0 0.0 collective-permute-done.3.rest_5_
  40.0 0.0 collective-permute-done.6.rest_7_
  40.0 4.0 %collective-permute-done.7.rest_8_ = f32[96,128]{1,0:T(8,128)S(1)} collective-permute-done((f32[96,128]{1,0:T(8,128)S(1)}, f32[96,128]{1,0:T(8,128)S(1)}, u32[]{:S(2)}, u32[]{:S(2)}) %collective-permute-start.7) | collective-permute-done | bytes 49184 | tf_op jit(solution)/shard_map/ppermute | solution.py:489
  44.0 1.3 %collective-permute-done.8.rest_9_ = f32[96,128]{1,0:T(8,128)S(1)} collective-permute-done((f32[96,128]{1,0:T(8,128)S(1)}, f32[96,128]{1,0:T(8,128)S(1)}, u32[]{:S(2)}, u32[]{:S(2)}) %collective-permute-start.8) | collective-permute-done | bytes 49184 | tf_op jit(solution)/shard_map/ppermute | solution.py:489
  45.3 0.3 shard_map.86
  45.5 1.4 %collective-permute-start.10 = (bf16[288,128]{1,0:T(8,128)(2,1)S(1)}, bf16[288,128]{1,0:T(8,128)(2,1)S(1)}, u32[]{:S(2)}, u32[]{:S(2)}) collective-permute-start(bf16[288,128]{1,0:T(8,128)(2,1)S(1)} %get-tuple-element.43.rest_0_), channel_id=1, source_target_pairs={{0,8},{4,12},{8,0},{12,4},{1,9},{5,13},{9,1},{13,5},{2,10},{6,14},... | collective-permute-start | bytes 221192 | tf_op jit(solution)/shard_map/ppermute | solution.py:489
  47.0 0.8 %collective-permute-start.11 = (bf16[288,128]{1,0:T(8,128)(2,1)S(1)}, bf16[288,128]{1,0:T(8,128)(2,1)S(1)}, u32[]{:S(2)}, u32[]{:S(2)}) collective-permute-start(bf16[288,128]{1,0:T(8,128)(2,1)S(1)} %get-tuple-element.43.rest_0_), channel_id=1, source_target_pairs={{0,12},{4,8},{8,4},{12,0},{1,13},{5,9},{9,5},{13,1},{2,14},{6,10},... | collective-permute-start | bytes 221192 | tf_op jit(solution)/shard_map/ppermute | solution.py:489
  47.8 1.3 %collective-permute-start.9 = (bf16[288,128]{1,0:T(8,128)(2,1)S(1)}, bf16[288,128]{1,0:T(8,128)(2,1)S(1)}, u32[]{:S(2)}, u32[]{:S(2)}) collective-permute-start(bf16[288,128]{1,0:T(8,128)(2,1)S(1)} %get-tuple-element.43.rest_0_), channel_id=1, source_target_pairs={{0,4},{4,0},{8,12},{12,8},{1,5},{5,1},{9,13},{13,9},{2,6},{6,2},{1... | collective-permute-start | bytes 221192 | tf_op jit(solution)/shard_map/ppermute | solution.py:489
  49.1 2.2 %collective-permute-start.14 = (f32[96,128]{1,0:T(8,128)S(1)}, f32[96,128]{1,0:T(8,128)S(1)}, u32[]{:S(2)}, u32[]{:S(2)}) collective-permute-start(f32[96,128]{1,0:T(8,128)S(1)} %get-tuple-element.48), channel_id=1, source_target_pairs={{0,8},{4,12},{8,0},{12,4},{1,9},{5,13},{9,1},{13,5},{2,10},{6,14},... | collective-permute-start | bytes 147464 | tf_op jit(solution)/shard_map/ppermute | solution.py:489
  51.3 0.0 collective-permute-done.13.rest_3_
  51.3 0.8 %collective-permute-start.15 = (f32[96,128]{1,0:T(8,128)S(1)}, f32[96,128]{1,0:T(8,128)S(1)}, u32[]{:S(2)}, u32[]{:S(2)}) collective-permute-start(f32[96,128]{1,0:T(8,128)S(1)} %get-tuple-element.49), channel_id=1, source_target_pairs={{0,12},{4,8},{8,4},{12,0},{1,13},{5,9},{9,5},{13,1},{2,14},{6,10},... | collective-permute-start | bytes 147464 | tf_op jit(solution)/shard_map/ppermute | solution.py:489
  52.2 1.0 %shard_map.90.rest_8_.rest_1_ = bf16[4,3,128,256]{3,2,1,0:T(8,128)(2,1)S(1)} custom-call(bf16[4,256,768]{2,1,0:T(8,128)(2,1)S(1)} %get-tuple-element.50.normed, bf16[768,384]{1,0:T(8,128)(2,1)S(1)} %copy-done.1), custom_call_target="tpu_custom_call" | custom-call | flops 603979776 | bytes 1572864 | tf_op jit(solution)/shard_map/pallas_call | solution.py:57
  53.2 3.5 %collective-permute-done.14.rest_4_ = f32[96,128]{1,0:T(8,128)S(1)} collective-permute-done((f32[96,128]{1,0:T(8,128)S(1)}, f32[96,128]{1,0:T(8,128)S(1)}, u32[]{:S(2)}, u32[]{:S(2)}) %collective-permute-start.14) | collective-permute-done | bytes 49184 | tf_op jit(solution)/shard_map/ppermute | solution.py:489
  56.7 0.7 collective-permute-done.15.rest_5_
  57.3 0.3 shard_map.89.rest_4_
  57.6 1.0 %collective-permute-start.16 = (bf16[112,128]{1,0:T(8,128)(2,1)S(1)}, bf16[112,128]{1,0:T(8,128)(2,1)S(1)}, u32[]{:S(2)}, u32[]{:S(2)}) collective-permute-start(bf16[112,128]{1,0:T(8,128)(2,1)S(1)} %shard_map.89.rest_4_), channel_id=1, source_target_pairs={{0,4},{4,0},{8,12},{12,8},{1,5},{5,1},{9,13},{13,9},{2,6},{6,2},{1... | collective-permute-start | bytes 86024 | tf_op jit(solution)/shard_map/ppermute | solution.py:489
  58.6 1.7 %collective-permute-start.17 = (bf16[112,128]{1,0:T(8,128)(2,1)S(1)}, bf16[112,128]{1,0:T(8,128)(2,1)S(1)}, u32[]{:S(2)}, u32[]{:S(2)}) collective-permute-start(bf16[112,128]{1,0:T(8,128)(2,1)S(1)} %shard_map.89.rest_4_), channel_id=1, source_target_pairs={{0,8},{4,12},{8,0},{12,4},{1,9},{5,13},{9,1},{13,5},{2,10},{6,14},... | collective-permute-start | bytes 86024 | tf_op jit(solution)/shard_map/ppermute | solution.py:489
  60.3 0.0 collective-permute-done.10.rest_2_
  60.3 1.8 %collective-permute-start.18 = (bf16[112,128]{1,0:T(8,128)(2,1)S(1)}, bf16[112,128]{1,0:T(8,128)(2,1)S(1)}, u32[]{:S(2)}, u32[]{:S(2)}) collective-permute-start(bf16[112,128]{1,0:T(8,128)(2,1)S(1)} %shard_map.89.rest_4_), channel_id=1, source_target_pairs={{0,12},{4,8},{8,4},{12,0},{1,13},{5,9},{9,5},{13,1},{2,14},{6,10},... | collective-permute-start | bytes 86024 | tf_op jit(solution)/shard_map/ppermute | solution.py:489
  62.1 0.6 shard_map.91.rest_9_.rest_2_
  62.7 0.6 shard_map.92.rest_10_.rest_3_
  63.2 0.0 collective-permute-done.11.rest_3_
  63.2 0.0 collective-permute-done.9.rest_1_
  63.2 0.0 collective-permute-done.16.rest_5_
  63.3 0.1 collective-permute-done.17.rest_6_
  63.4 2.6 %collective-permute-done.18.rest_7_ = bf16[112,128]{1,0:T(8,128)(2,1)S(1)} collective-permute-done((bf16[112,128]{1,0:T(8,128)(2,1)S(1)}, bf16[112,128]{1,0:T(8,128)(2,1)S(1)}, u32[]{:S(2)}, u32[]{:S(2)}) %collective-permute-start.18) | collective-permute-done | bytes 28704 | tf_op jit(solution)/shard_map/ppermute | solution.py:489
  66.0 0.7 %shard_map.93 = (bf16[4,128,384]{2,1,0:T(8,128)(2,1)S(1)}, bf16[3,256,256]{2,1,0:T(8,128)(2,1)S(1)}) custom-call(bf16[288,128]{1,0:T(8,128)(2,1)S(1)} %get-tuple-element.43.rest_0_, bf16[288,128]{1,0:T(8,128)(2,1)S(1)} %collective-permute-done.9.rest_1_, bf16[288,128]{1,0:T(8,128)(2,1)S(1)} %collective-permute-done.10.rest_2_, ...), custom_call_target="tpu_custom_call" | custom-call | flops 201326592 | bytes 1572864 | tf_op jit(solution)/shard_map/pallas_call | solution.py:57
  66.7 0.0 copy-start.2
  66.7 0.1 collective-permute-start.20
  66.8 0.4 shard_map.94.rest_1_
  67.2 0.6 collective-permute-start.19
  67.7 0.0 copy-done.2
  67.8 0.1 shard_map.95.rest_2_.rest_1_
  67.8 0.6 shard_map.96.half
  68.5 0.0 collective-permute-done.20.rest_0_
  68.5 0.4 shard_map.97.rest_2_
  68.9 0.2 collective-permute-done.19.rest_0_
  69.1 1.1 %shard_map.98 = bf16[8,128,384]{2,1,0:T(8,128)(2,1)} custom-call(f32[8,128]{1,0:T(8,128)S(1)} %broadcast_in_dim.6.live, f32[8,128,384]{2,1,0:T(8,128)S(1)} %shard_map.96.half, bf16[4,128,384]{2,1,0:T(8,128)(2,1)S(1)} %collective-permute-done.19.rest_0_, bf16[768,384]{1,0:T(8,128)(2,1)S(1)} %shard_map.95.rest_2_.rest_1_, ...), custom_call_target="tpu_custom_call" | custom-call | flops 301989888 | bytes 1572864 | tf_op jit(solution)/shard_map/pallas_call | solution.py:57
  (15 shorter events, 0.0 us)
Async XLA Ops:
  0.0 23.9 %copy-start.4 = (f32[768]{0:T(1024)S(1)}, f32[768]{0:T(1024)}, u32[]{:S(2)}) copy-start(f32[768]{0:T(1024)} %param.9) | copy-start | bytes 9220
  0.0 23.9 %copy-start.6 = (s32[8]{0:T(128)S(1)}, s32[8]{0:T(128)}, u32[]{:S(2)}) copy-start(s32[8]{0:T(128)} %param.14) | copy-start | bytes 100
  0.0 24.0 %copy-start.3 = (bf16[768,384]{1,0:T(8,128)(2,1)S(1)}, bf16[768,384]{1,0:T(8,128)(2,1)}, u32[]{:S(2)}) copy-start(bf16[768,384]{1,0:T(8,128)(2,1)} %w_query.1) | copy-start | bytes 1769476
  0.0 24.0 %copy-start = (bf16[768,384]{1,0:T(8,128)(2,1)S(1)}, bf16[768,384]{1,0:T(8,128)(2,1)}, u32[]{:S(2)}) copy-start(bf16[768,384]{1,0:T(8,128)(2,1)} %w_key.9) | copy-start | bytes 1769476
  2.6 13.7 %collective-permute-start = (bf16[272,768]{1,0:T(8,128)(2,1)}, bf16[272,768]{1,0:T(8,128)(2,1)S(1)}, u32[]{:S(2)}, u32[]{:S(2)}) collective-permute-start(bf16[272,768]{1,0:T(8,128)(2,1)} %get-tuple-element.31), channel_id=1, source_target_pairs={{0,2},{2,0},{1,3},{3,1},{4,6},{6,4},{5,7},{7,5},{8,10},{10,8},{9,1... | collective-permute-start | bytes 1253384 | tf_op jit(solution)/shard_map/ppermute | solution.py:28
  6.6 17.3 %collective-permute-start.4 = (bf16[256,768]{1,0:T(8,128)(2,1)S(1)}, bf16[256,768]{1,0:T(8,128)(2,1)S(1)}, u32[]{:S(2)}, u32[]{:S(2)}) collective-permute-start(bf16[256,768]{1,0:T(8,128)(2,1)S(1)} %bitcast.5), channel_id=1, source_target_pairs={{0,2},{2,0},{1,3},{3,1},{4,6},{6,4},{5,7},{7,5},{8,10},{10,8},{9,1... | collective-permute-start | bytes 1179656 | tf_op jit(solution)/shard_map/ppermute | solution.py:28
  16.3 18.5 %collective-permute-start.12 = (bf16[272,768]{1,0:T(8,128)(2,1)S(1)}, bf16[272,768]{1,0:T(8,128)(2,1)S(1)}, u32[]{:S(2)}, u32[]{:S(2)}) collective-permute-start(bf16[272,768]{1,0:T(8,128)(2,1)S(1)} %collective-permute-done.part), channel_id=1, source_target_pairs={{0,1},{1,0},{2,3},{3,2},{4,5},{5,4},{6,7},{7,6},{8,9},{9,8},{10,11... | collective-permute-start | bytes 1253384 | tf_op jit(solution)/shard_map/ppermute | solution.py:28
  23.9 9.0 %collective-permute-start.5 = (bf16[256,768]{1,0:T(8,128)(2,1)S(1)}, bf16[256,768]{1,0:T(8,128)(2,1)S(1)}, u32[]{:S(2)}, u32[]{:S(2)}) collective-permute-start(bf16[256,768]{1,0:T(8,128)(2,1)S(1)} %collective-permute-done.4.part), channel_id=1, source_target_pairs={{0,1},{1,0},{2,3},{3,2},{4,5},{5,4},{6,7},{7,6},{8,9},{9,8},{10,11... | collective-permute-start | bytes 1179656 | tf_op jit(solution)/shard_map/ppermute | solution.py:28
  24.0 6.9 %copy-start.5 = (s32[128]{0:T(128)S(1)}, s32[128]{0:T(128)}, u32[]{:S(2)}) copy-start(s32[128]{0:T(128)} %param.15) | copy-start | bytes 1540
  26.4 12.9 %collective-permute-start.1 = (f32[200,128]{1,0:T(8,128)S(1)}, f32[200,128]{1,0:T(8,128)S(1)}, u32[]{:S(2)}, u32[]{:S(2)}) collective-permute-start(f32[200,128]{1,0:T(8,128)S(1)} %get-tuple-element.34), channel_id=1, source_target_pairs={{0,4},{4,0},{8,12},{12,8},{1,5},{5,1},{9,13},{13,9},{2,6},{6,2},{1... | collective-permute-start | bytes 307208 | tf_op jit(solution)/shard_map/ppermute | solution.py:489
  28.3 11.6 %collective-permute-start.2 = (f32[200,128]{1,0:T(8,128)S(1)}, f32[200,128]{1,0:T(8,128)S(1)}, u32[]{:S(2)}, u32[]{:S(2)}) collective-permute-start(f32[200,128]{1,0:T(8,128)S(1)} %get-tuple-element.35), channel_id=1, source_target_pairs={{0,8},{4,12},{8,0},{12,4},{1,9},{5,13},{9,1},{13,5},{2,10},{6,14},... | collective-permute-start | bytes 307208 | tf_op jit(solution)/shard_map/ppermute | solution.py:489
  30.9 9.1 %collective-permute-start.3 = (f32[200,128]{1,0:T(8,128)S(1)}, f32[200,128]{1,0:T(8,128)S(1)}, u32[]{:S(2)}, u32[]{:S(2)}) collective-permute-start(f32[200,128]{1,0:T(8,128)S(1)} %get-tuple-element.36), channel_id=1, source_target_pairs={{0,12},{4,8},{8,4},{12,0},{1,13},{5,9},{9,5},{13,1},{2,14},{6,10},... | collective-permute-start | bytes 307208 | tf_op jit(solution)/shard_map/ppermute | solution.py:489
  33.9 6.1 %collective-permute-start.6 = (f32[96,128]{1,0:T(8,128)S(1)}, f32[96,128]{1,0:T(8,128)S(1)}, u32[]{:S(2)}, u32[]{:S(2)}) collective-permute-start(f32[96,128]{1,0:T(8,128)S(1)} %get-tuple-element.40), channel_id=1, source_target_pairs={{0,4},{4,0},{8,12},{12,8},{1,5},{5,1},{9,13},{13,9},{2,6},{6,2},{1... | collective-permute-start | bytes 147464 | tf_op jit(solution)/shard_map/ppermute | solution.py:489
  34.8 9.2 %collective-permute-start.7 = (f32[96,128]{1,0:T(8,128)S(1)}, f32[96,128]{1,0:T(8,128)S(1)}, u32[]{:S(2)}, u32[]{:S(2)}) collective-permute-start(f32[96,128]{1,0:T(8,128)S(1)} %get-tuple-element.41), channel_id=1, source_target_pairs={{0,8},{4,12},{8,0},{12,4},{1,9},{5,13},{9,1},{13,5},{2,10},{6,14},... | collective-permute-start | bytes 147464 | tf_op jit(solution)/shard_map/ppermute | solution.py:489
  38.3 13.8 %copy-start.1 = (bf16[768,384]{1,0:T(8,128)(2,1)S(1)}, bf16[768,384]{1,0:T(8,128)(2,1)}, u32[]{:S(2)}) copy-start(bf16[768,384]{1,0:T(8,128)(2,1)} %refs_2_.3) | copy-start | bytes 1769476
  39.3 6.0 %collective-permute-start.8 = (f32[96,128]{1,0:T(8,128)S(1)}, f32[96,128]{1,0:T(8,128)S(1)}, u32[]{:S(2)}, u32[]{:S(2)}) collective-permute-start(f32[96,128]{1,0:T(8,128)S(1)} %get-tuple-element.42), channel_id=1, source_target_pairs={{0,12},{4,8},{8,4},{12,0},{1,13},{5,9},{9,5},{13,1},{2,14},{6,10},... | collective-permute-start | bytes 147464 | tf_op jit(solution)/shard_map/ppermute | solution.py:489
  39.9 11.4 %collective-permute-start.13 = (f32[96,128]{1,0:T(8,128)S(1)}, f32[96,128]{1,0:T(8,128)S(1)}, u32[]{:S(2)}, u32[]{:S(2)}) collective-permute-start(f32[96,128]{1,0:T(8,128)S(1)} %get-tuple-element.47), channel_id=1, source_target_pairs={{0,4},{4,0},{8,12},{12,8},{1,5},{5,1},{9,13},{13,9},{2,6},{6,2},{1... | collective-permute-start | bytes 147464 | tf_op jit(solution)/shard_map/ppermute | solution.py:489
  45.5 14.8 %collective-permute-start.10 = (bf16[288,128]{1,0:T(8,128)(2,1)S(1)}, bf16[288,128]{1,0:T(8,128)(2,1)S(1)}, u32[]{:S(2)}, u32[]{:S(2)}) collective-permute-start(bf16[288,128]{1,0:T(8,128)(2,1)S(1)} %get-tuple-element.43.rest_0_), channel_id=1, source_target_pairs={{0,8},{4,12},{8,0},{12,4},{1,9},{5,13},{9,1},{13,5},{2,10},{6,14},... | collective-permute-start | bytes 221192 | tf_op jit(solution)/shard_map/ppermute | solution.py:489
  47.0 16.3 %collective-permute-start.11 = (bf16[288,128]{1,0:T(8,128)(2,1)S(1)}, bf16[288,128]{1,0:T(8,128)(2,1)S(1)}, u32[]{:S(2)}, u32[]{:S(2)}) collective-permute-start(bf16[288,128]{1,0:T(8,128)(2,1)S(1)} %get-tuple-element.43.rest_0_), channel_id=1, source_target_pairs={{0,12},{4,8},{8,4},{12,0},{1,13},{5,9},{9,5},{13,1},{2,14},{6,10},... | collective-permute-start | bytes 221192 | tf_op jit(solution)/shard_map/ppermute | solution.py:489
  47.8 15.5 %collective-permute-start.9 = (bf16[288,128]{1,0:T(8,128)(2,1)S(1)}, bf16[288,128]{1,0:T(8,128)(2,1)S(1)}, u32[]{:S(2)}, u32[]{:S(2)}) collective-permute-start(bf16[288,128]{1,0:T(8,128)(2,1)S(1)} %get-tuple-element.43.rest_0_), channel_id=1, source_target_pairs={{0,4},{4,0},{8,12},{12,8},{1,5},{5,1},{9,13},{13,9},{2,6},{6,2},{1... | collective-permute-start | bytes 221192 | tf_op jit(solution)/shard_map/ppermute | solution.py:489
  49.1 7.6 %collective-permute-start.14 = (f32[96,128]{1,0:T(8,128)S(1)}, f32[96,128]{1,0:T(8,128)S(1)}, u32[]{:S(2)}, u32[]{:S(2)}) collective-permute-start(f32[96,128]{1,0:T(8,128)S(1)} %get-tuple-element.48), channel_id=1, source_target_pairs={{0,8},{4,12},{8,0},{12,4},{1,9},{5,13},{9,1},{13,5},{2,10},{6,14},... | collective-permute-start | bytes 147464 | tf_op jit(solution)/shard_map/ppermute | solution.py:489
  51.3 6.0 %collective-permute-start.15 = (f32[96,128]{1,0:T(8,128)S(1)}, f32[96,128]{1,0:T(8,128)S(1)}, u32[]{:S(2)}, u32[]{:S(2)}) collective-permute-start(f32[96,128]{1,0:T(8,128)S(1)} %get-tuple-element.49), channel_id=1, source_target_pairs={{0,12},{4,8},{8,4},{12,0},{1,13},{5,9},{9,5},{13,1},{2,14},{6,10},... | collective-permute-start | bytes 147464 | tf_op jit(solution)/shard_map/ppermute | solution.py:489
  57.6 5.6 %collective-permute-start.16 = (bf16[112,128]{1,0:T(8,128)(2,1)S(1)}, bf16[112,128]{1,0:T(8,128)(2,1)S(1)}, u32[]{:S(2)}, u32[]{:S(2)}) collective-permute-start(bf16[112,128]{1,0:T(8,128)(2,1)S(1)} %shard_map.89.rest_4_), channel_id=1, source_target_pairs={{0,4},{4,0},{8,12},{12,8},{1,5},{5,1},{9,13},{13,9},{2,6},{6,2},{1... | collective-permute-start | bytes 86024 | tf_op jit(solution)/shard_map/ppermute | solution.py:489
  58.6 4.8 %collective-permute-start.17 = (bf16[112,128]{1,0:T(8,128)(2,1)S(1)}, bf16[112,128]{1,0:T(8,128)(2,1)S(1)}, u32[]{:S(2)}, u32[]{:S(2)}) collective-permute-start(bf16[112,128]{1,0:T(8,128)(2,1)S(1)} %shard_map.89.rest_4_), channel_id=1, source_target_pairs={{0,8},{4,12},{8,0},{12,4},{1,9},{5,13},{9,1},{13,5},{2,10},{6,14},... | collective-permute-start | bytes 86024 | tf_op jit(solution)/shard_map/ppermute | solution.py:489
  60.3 5.7 %collective-permute-start.18 = (bf16[112,128]{1,0:T(8,128)(2,1)S(1)}, bf16[112,128]{1,0:T(8,128)(2,1)S(1)}, u32[]{:S(2)}, u32[]{:S(2)}) collective-permute-start(bf16[112,128]{1,0:T(8,128)(2,1)S(1)} %shard_map.89.rest_4_), channel_id=1, source_target_pairs={{0,12},{4,8},{8,4},{12,0},{1,13},{5,9},{9,5},{13,1},{2,14},{6,10},... | collective-permute-start | bytes 86024 | tf_op jit(solution)/shard_map/ppermute | solution.py:489
  66.7 1.1 %copy-start.2 = (bf16[768,384]{1,0:T(8,128)(2,1)S(1)}, bf16[768,384]{1,0:T(8,128)(2,1)}, u32[]{:S(2)}) copy-start(bf16[768,384]{1,0:T(8,128)(2,1)} %w_out.1) | copy-start | bytes 1769476
  66.7 1.8 %collective-permute-start.20 = (bf16[4,128,384]{2,1,0:T(8,128)(2,1)S(1)}, bf16[4,128,384]{2,1,0:T(8,128)(2,1)S(1)}, u32[]{:S(2)}, u32[]{:S(2)}) collective-permute-start(bf16[4,128,384]{2,1,0:T(8,128)(2,1)S(1)} %get-tuple-element.55.rest_0_), channel_id=1, source_target_pairs={{0,1},{1,0},{2,3},{3,2},{4,5},{5,4},{6,7},{7,6},{8,9},{9,8},{10,11... | collective-permute-start | bytes 1179656 | tf_op jit(solution)/shard_map/ppermute | solution.py:28
  67.2 1.9 %collective-permute-start.19 = (bf16[4,128,384]{2,1,0:T(8,128)(2,1)S(1)}, bf16[4,128,384]{2,1,0:T(8,128)(2,1)S(1)}, u32[]{:S(2)}, u32[]{:S(2)}) collective-permute-start(bf16[4,128,384]{2,1,0:T(8,128)(2,1)S(1)} %shard_map.94.rest_1_), channel_id=1, source_target_pairs={{0,1},{1,0},{2,3},{3,2},{4,5},{5,4},{6,7},{7,6},{8,9},{9,8},{10,11... | collective-permute-start | bytes 1179656 | tf_op jit(solution)/shard_map/ppermute | solution.py:28

commit v5 on v4

--- a/solution.py
+++ b/solution.py
@@ -74,6 +74,19 @@
     centred = values_f - average
     spread = jnp.mean(centred * centred, axis=-1, keepdims=True)
     return (centred * lax.rsqrt(spread + 1e-05) * gain).astype(BF16)
+
+
+def first_kernel(rows_in, chunk, sems, *, part_cols):
+    part_rows = chunk.shape[0] // part_cols
+    begin = lax.axis_index("heads") * part_rows
+    copies = []
+    for r in range(part_rows):
+        source = rows_in.at[begin + r, pl.ds(0, part_cols), :]
+        target = chunk.at[pl.ds(r * part_cols, part_cols)]
+        copies.append(pltpu.make_async_copy(source, target, sems.at[r]))
+        copies[-1].start()
+    for copy in copies:
+        copy.wait()
 
 
 def load_kernel(valid, rows_in, resident, *rest, part_cols):
@@ -419,15 +432,17 @@
     size = buffer.shape[0]
     copies = []
     for k, done in enumerate(ready):
-        copies.append(pltpu.make_async_copy(done, out.at[pl.ds(k * size, size)], sems.at[k]))
-        copies[-1].start()
+        for r in range(size):
+            target, sem = out.at[k * size + r], sems.at[k * size + r]
+            copies.append(pltpu.make_async_copy(done.at[r], target, sem))
+            copies[-1].start()
     first = len(ready) * size
     for begin in range(0, size, SIZE):
         for r, rows in enumerate(projected(live, half, parts, weights, begin, first)):
             row = begin + r
             buffer[row] = rows
             target = out.at[first + row]
-            copies.append(pltpu.make_async_copy(buffer.at[row], target, sems.at[len(ready) + row]))
+            copies.append(pltpu.make_async_copy(buffer.at[row], target, sems.at[first + row]))
             copies[-1].start()
     for copy in copies:
         copy.wait()
@@ -442,7 +457,6 @@
     offsets = lax.axis_size("cols") - 1
     depth = lax.axis_size("depth")
     cores = lax.axis_size("heads")
-    core = lax.axis_index("heads")
     part_rows = rows_here // cores
     inner = part_rows // SIZE
     groups = rows_here // SIZE
@@ -456,10 +470,13 @@
     gain = norm_gain[None, :]
     live = jnp.broadcast_to(row_mask.astype(F32)[:, None], (rows_here, LANES))
 
-    first = lax.dynamic_slice(
-        alignment, (core * part_rows, 0, 0), (part_rows, cols_here - part_cols, width)
-    )
-    sent = {(0, 0): first.reshape(part_rows * part_cols, width)}
+    first = call(
+        functools.partial(first_kernel, part_cols=part_cols),
+        shape((part_rows * part_cols, width), BF16),
+        [spec(HBM)],
+        [pltpu.SemaphoreType.DMA((part_rows,))],
+    )(alignment)
+    sent = {(0, 0): first}
     spans = [1] * CHUNKS
     some = part_rows // spans[-1] * part_cols
     resident, *lasts = call(
@@ -652,7 +669,7 @@
         [spec()] * (2 * cores + 1),
         [
             pltpu.VMEM((part_rows, cols_here, local_width), BF16),
-            pltpu.SemaphoreType.DMA((cores - 1 + part_rows,)),
+            pltpu.SemaphoreType.DMA((rows_here,)),
         ],
         flops=2 * part_rows * cols_here * width * local_width,
         space=HBM,

time: 70.4 us -> 69.4 us (0.986)
  local copies, waits for them, and re-layouts: 1.15 us -> 0.14 us
    dynamic_slice x1 -> x0, local copies, waits for them, and re-layouts: 1.02 us -> none  [on_device(): lax.dynamic_slice(alignment, (core * part_rows, 0, 0), (part_rows, cols_h...]
    pallas_call x17 -> x18, Pallas kernels: 14.8 us -> 15.1 us  [run(): out = fn(*args)]
  transfers between devices with their start and end apart: 21 -> 21, of which waited for: 10 -> 10; matrix products, arithmetic and copies ran while one was open for 2% -> 0% of each run, Pallas kernels for 15% -> 17%
where the time goes in v5:
time: 69.4 us; the launch traced here: 69.2 us
  waiting for transfers between devices  29.8 us (43%)
  starting transfers between devices  23.9 us (34%)
  Pallas kernels  15.1 us (22%)
    ppermute x15, starting transfers between devices, exchange(): received.append(lax.ppermute(values[k], 'depth', swapped))  20.1 us
    ppermute x6, waiting for transfers between devices, from_behind(): lax.ppermute(value, axis, [(s, (s + steps) % count) for s in range(count)])  17.1 us
    pallas_call x18, Pallas kernels, run(): out = fn(*args)  15.1 us
    ppermute x15, waiting for transfers between devices, exchange(): received.append(lax.ppermute(values[k], 'depth', swapped))  12.7 us
    ppermute x6, starting transfers between devices, from_behind(): lax.ppermute(value, axis, [(s, (s + steps) % count) for s in range(count)])  3.77 us
  transfers between devices with their start and end apart: 21, of which 10 were waited for; matrix products, arithmetic and copies ran while one was open for 0% of the time, Pallas kernels for 17%

profile of v5, /device:TPU:0, one launch (start us, length us, event | category | flops | bytes accessed | tf_op | source)
XLA Modules:
  0.0 69.2 jit_solution(4735123983856349734)
XLA Ops:
  0.0 1.8 %shard_map.82 = (bf16[8,128,768]{2,1,0:T(8,128)(2,1)S(1)}, bf16[272,768]{1,0:T(8,128)(2,1)S(1)}) custom-call(s32[1,128]{1,0:T(1,128)} %bitcast.4, bf16[8,128,768]{2,1,0:T(8,128)(2,1)} %rows_in.3), custom_call_target="tpu_custom_call" | custom-call | bytes 3981312 | tf_op jit(solution)/shard_map/pallas_call | solution.py:57
  1.8 3.0 %collective-permute-start = (bf16[272,768]{1,0:T(8,128)(2,1)S(1)}, bf16[272,768]{1,0:T(8,128)(2,1)S(1)}, u32[]{:S(2)}, u32[]{:S(2)}) collective-permute-start(bf16[272,768]{1,0:T(8,128)(2,1)S(1)} %get-tuple-element.31), channel_id=1, source_target_pairs={{0,2},{2,0},{1,3},{3,1},{4,6},{6,4},{5,7},{7,5},{8,10},{10,8},{9,1... | collective-permute-start | bytes 1253384 | tf_op jit(solution)/shard_map/ppermute | solution.py:28
  4.9 1.1 %shard_map.84 = bf16[256,768]{1,0:T(8,128)(2,1)S(1)} custom-call(bf16[8,128,768]{2,1,0:T(8,128)(2,1)} %rows_in.3), custom_call_target="tpu_custom_call" | custom-call | bytes 786432 | tf_op jit(solution)/shard_map/pallas_call | solution.py:57
  5.9 0.1 collective-permute-start.4
  6.0 9.3 %collective-permute-done.part = bf16[272,768]{1,0:T(8,128)(2,1)S(1)} collective-permute-done((bf16[272,768]{1,0:T(8,128)(2,1)S(1)}, bf16[272,768]{1,0:T(8,128)(2,1)S(1)}, u32[]{:S(2)}, u32[]{:S(2)}) %collective-permute-start) | collective-permute-done | bytes 417824 | tf_op jit(solution)/shard_map/ppermute | solution.py:28
  15.3 0.0 collective-permute-start.12
  15.3 7.6 %collective-permute-done.4.part = bf16[256,768]{1,0:T(8,128)(2,1)S(1)} collective-permute-done((bf16[256,768]{1,0:T(8,128)(2,1)S(1)}, bf16[256,768]{1,0:T(8,128)(2,1)S(1)}, u32[]{:S(2)}, u32[]{:S(2)}) %collective-permute-start.4) | collective-permute-done | bytes 393248 | tf_op jit(solution)/shard_map/ppermute | solution.py:28
  22.9 0.0 collective-permute-start.5
  23.0 0.1 broadcast_in_dim.6.live
  23.0 2.4 %shard_map.83 = (bf16[4,256,768]{2,1,0:T(8,128)(2,1)S(1)}, bf16[4,3,256,256]{3,2,1,0:T(8,128)(2,1)S(1)}, f32[200,128]{1,0:T(8,128)S(1)}, f32[200,128]{1,0:T(8,12...) custom-call(f32[8,128]{1,0:T(8,128)S(1)} %broadcast_in_dim.6.live, ...), custom_call_target="tpu_custom_call" | custom-call | flops 1207959552 | bytes 7110656 | tf_op jit(solution)/shard_map/pallas_call | solution.py:57
  25.5 1.9 %collective-permute-start.1 = (f32[200,128]{1,0:T(8,128)S(1)}, f32[200,128]{1,0:T(8,128)S(1)}, u32[]{:S(2)}, u32[]{:S(2)}) collective-permute-start(f32[200,128]{1,0:T(8,128)S(1)} %get-tuple-element.34), channel_id=1, source_target_pairs={{0,4},{4,0},{8,12},{12,8},{1,5},{5,1},{9,13},{13,9},{2,6},{6,2},{1... | collective-permute-start | bytes 307208 | tf_op jit(solution)/shard_map/ppermute | solution.py:506
  27.3 2.6 %collective-permute-start.2 = (f32[200,128]{1,0:T(8,128)S(1)}, f32[200,128]{1,0:T(8,128)S(1)}, u32[]{:S(2)}, u32[]{:S(2)}) collective-permute-start(f32[200,128]{1,0:T(8,128)S(1)} %get-tuple-element.35), channel_id=1, source_target_pairs={{0,8},{4,12},{8,0},{12,4},{1,9},{5,13},{9,1},{13,5},{2,10},{6,14},... | collective-permute-start | bytes 307208 | tf_op jit(solution)/shard_map/ppermute | solution.py:506
  29.9 0.0 collective-permute-start.3
  30.0 1.0 %shard_map.85 = (bf16[256,768]{1,0:T(8,128)(2,1)S(1)}, f32[3,128,128]{2,1,0:T(8,128)S(1)}) custom-call(bf16[256,768]{1,0:T(8,128)(2,1)S(1)} %collective-permute-done.4.part, f32[1,768]{1,0:T(1,128)S(1)} %broadcast_in_dim.15.gain, bf16[768,384]{1,0:T(8,128)(2,1)S(1)} %copy-done, bf16[4,3,256,256]{3,2,1,0:T(8,128)(2,1)S(1)} %get-tuple-element.37.query), custom_call_target="tpu_custom_call" | custom-call | flops 150994944 | bytes 1179648 | tf_op jit(solution)/shard_map/pallas_call | solution.py:57
  30.9 1.0 %shard_map.88 = (bf16[256,768]{1,0:T(8,128)(2,1)S(1)}, f32[3,128,128]{2,1,0:T(8,128)S(1)}) custom-call(bf16[272,768]{1,0:T(8,128)(2,1)S(1)} %collective-permute-done.part, f32[1,768]{1,0:T(1,128)S(1)} %broadcast_in_dim.15.gain, bf16[768,384]{1,0:T(8,128)(2,1)S(1)} %copy-done, bf16[4,3,256,256]{3,2,1,0:T(8,128)(2,1)S(1)} %get-tuple-element.37.query), custom_call_target="tpu_custom_call" | custom-call | flops 150994944 | bytes 1179648 | tf_op jit(solution)/shard_map/pallas_call | solution.py:57
  31.9 0.0 collective-permute-done.5.part
  31.9 1.0 %shard_map.86 = (bf16[256,768]{1,0:T(8,128)(2,1)S(1)}, f32[96,128]{1,0:T(8,128)S(1)}, f32[96,128]{1,0:T(8,128)S(1)}, f32[96,128]{1,0:T(8,128)S(1)}, f32[96,128]{1,0:T(8,128)S(1)}) custom-call(bf16[256,768]{1,0:T(8,128)(2,1)S(1)} %collective-permute-done.5.part, f32[1,768]{1,0:T(1,128)S(1)} %broadcast_in_dim.15.gain, bf16[768,384]{1,0:T(8,128)(2,1)S(1)} %copy-done, ...), custom_call_target="tpu_custom_call" | custom-call | flops 150994944 | bytes 1179648 | tf_op jit(solution)/shard_map/pallas_call | solution.py:57
  32.9 1.0 %collective-permute-start.6 = (f32[96,128]{1,0:T(8,128)S(1)}, f32[96,128]{1,0:T(8,128)S(1)}, u32[]{:S(2)}, u32[]{:S(2)}) collective-permute-start(f32[96,128]{1,0:T(8,128)S(1)} %get-tuple-element.40), channel_id=1, source_target_pairs={{0,4},{4,0},{8,12},{12,8},{1,5},{5,1},{9,13},{13,9},{2,6},{6,2},{1... | collective-permute-start | bytes 147464 | tf_op jit(solution)/shard_map/ppermute | solution.py:506
  33.9 0.0 collective-permute-done.12.part
  33.9 3.5 %collective-permute-start.7 = (f32[96,128]{1,0:T(8,128)S(1)}, f32[96,128]{1,0:T(8,128)S(1)}, u32[]{:S(2)}, u32[]{:S(2)}) collective-permute-start(f32[96,128]{1,0:T(8,128)S(1)} %get-tuple-element.41), channel_id=1, source_target_pairs={{0,8},{4,12},{8,0},{12,4},{1,9},{5,13},{9,1},{13,5},{2,10},{6,14},... | collective-permute-start | bytes 147464 | tf_op jit(solution)/shard_map/ppermute | solution.py:506
  37.4 1.0 %shard_map.89 = (bf16[256,768]{1,0:T(8,128)(2,1)S(1)}, f32[96,128]{1,0:T(8,128)S(1)}, f32[96,128]{1,0:T(8,128)S(1)}, f32[96,128]{1,0:T(8,128)S(1)}, f32[96,128]{1,0:T(8,128)S(1)}) custom-call(bf16[272,768]{1,0:T(8,128)(2,1)S(1)} %collective-permute-done.12.part, f32[1,768]{1,0:T(1,128)S(1)} %broadcast_in_dim.15.gain, bf16[768,384]{1,0:T(8,128)(2,1)S(1)} %copy-done, ...), custom_call_target="tpu_custom_call" | custom-call | flops 150994944 | bytes 1179648 | tf_op jit(solution)/shard_map/pallas_call | solution.py:57
  38.4 0.0 collective-permute-done.1.rest_3_
  38.4 0.1 collective-permute-start.8
  38.4 0.5 collective-permute-done.2.rest_4_
  39.0 0.1 collective-permute-start.13
  39.0 0.0 collective-permute-done.3.rest_5_
  39.0 0.0 collective-permute-done.6.rest_7_
  39.0 4.0 %collective-permute-done.7.rest_8_ = f32[96,128]{1,0:T(8,128)S(1)} collective-permute-done((f32[96,128]{1,0:T(8,128)S(1)}, f32[96,128]{1,0:T(8,128)S(1)}, u32[]{:S(2)}, u32[]{:S(2)}) %collective-permute-start.7) | collective-permute-done | bytes 49184 | tf_op jit(solution)/shard_map/ppermute | solution.py:506
  43.0 1.3 %collective-permute-done.8.rest_9_ = f32[96,128]{1,0:T(8,128)S(1)} collective-permute-done((f32[96,128]{1,0:T(8,128)S(1)}, f32[96,128]{1,0:T(8,128)S(1)}, u32[]{:S(2)}, u32[]{:S(2)}) %collective-permute-start.8) | collective-permute-done | bytes 49184 | tf_op jit(solution)/shard_map/ppermute | solution.py:506
  44.3 0.3 shard_map.87
  44.6 1.4 %collective-permute-start.10 = (bf16[288,128]{1,0:T(8,128)(2,1)S(1)}, bf16[288,128]{1,0:T(8,128)(2,1)S(1)}, u32[]{:S(2)}, u32[]{:S(2)}) collective-permute-start(bf16[288,128]{1,0:T(8,128)(2,1)S(1)} %get-tuple-element.43.rest_0_), channel_id=1, source_target_pairs={{0,8},{4,12},{8,0},{12,4},{1,9},{5,13},{9,1},{13,5},{2,10},{6,14},... | collective-permute-start | bytes 221192 | tf_op jit(solution)/shard_map/ppermute | solution.py:506
  46.0 0.8 %collective-permute-start.11 = (bf16[288,128]{1,0:T(8,128)(2,1)S(1)}, bf16[288,128]{1,0:T(8,128)(2,1)S(1)}, u32[]{:S(2)}, u32[]{:S(2)}) collective-permute-start(bf16[288,128]{1,0:T(8,128)(2,1)S(1)} %get-tuple-element.43.rest_0_), channel_id=1, source_target_pairs={{0,12},{4,8},{8,4},{12,0},{1,13},{5,9},{9,5},{13,1},{2,14},{6,10},... | collective-permute-start | bytes 221192 | tf_op jit(solution)/shard_map/ppermute | solution.py:506
  46.8 1.3 %collective-permute-start.9 = (bf16[288,128]{1,0:T(8,128)(2,1)S(1)}, bf16[288,128]{1,0:T(8,128)(2,1)S(1)}, u32[]{:S(2)}, u32[]{:S(2)}) collective-permute-start(bf16[288,128]{1,0:T(8,128)(2,1)S(1)} %get-tuple-element.43.rest_0_), channel_id=1, source_target_pairs={{0,4},{4,0},{8,12},{12,8},{1,5},{5,1},{9,13},{13,9},{2,6},{6,2},{1... | collective-permute-start | bytes 221192 | tf_op jit(solution)/shard_map/ppermute | solution.py:506
  48.1 2.2 %collective-permute-start.14 = (f32[96,128]{1,0:T(8,128)S(1)}, f32[96,128]{1,0:T(8,128)S(1)}, u32[]{:S(2)}, u32[]{:S(2)}) collective-permute-start(f32[96,128]{1,0:T(8,128)S(1)} %get-tuple-element.48), channel_id=1, source_target_pairs={{0,8},{4,12},{8,0},{12,4},{1,9},{5,13},{9,1},{13,5},{2,10},{6,14},... | collective-permute-start | bytes 147464 | tf_op jit(solution)/shard_map/ppermute | solution.py:506
  50.4 0.0 collective-permute-done.13.rest_3_
  50.4 0.8 %collective-permute-start.15 = (f32[96,128]{1,0:T(8,128)S(1)}, f32[96,128]{1,0:T(8,128)S(1)}, u32[]{:S(2)}, u32[]{:S(2)}) collective-permute-start(f32[96,128]{1,0:T(8,128)S(1)} %get-tuple-element.49), channel_id=1, source_target_pairs={{0,12},{4,8},{8,4},{12,0},{1,13},{5,9},{9,5},{13,1},{2,14},{6,10},... | collective-permute-start | bytes 147464 | tf_op jit(solution)/shard_map/ppermute | solution.py:506
  51.2 0.0 copy-done.1
  51.2 1.0 %shard_map.91.rest_8_.rest_1_ = bf16[4,3,128,256]{3,2,1,0:T(8,128)(2,1)S(1)} custom-call(bf16[4,256,768]{2,1,0:T(8,128)(2,1)S(1)} %get-tuple-element.50.normed, bf16[768,384]{1,0:T(8,128)(2,1)S(1)} %copy-done.1), custom_call_target="tpu_custom_call" | custom-call | flops 603979776 | bytes 1572864 | tf_op jit(solution)/shard_map/pallas_call | solution.py:57
  52.2 3.5 %collective-permute-done.14.rest_4_ = f32[96,128]{1,0:T(8,128)S(1)} collective-permute-done((f32[96,128]{1,0:T(8,128)S(1)}, f32[96,128]{1,0:T(8,128)S(1)}, u32[]{:S(2)}, u32[]{:S(2)}) %collective-permute-start.14) | collective-permute-done | bytes 49184 | tf_op jit(solution)/shard_map/ppermute | solution.py:506
  55.7 0.7 collective-permute-done.15.rest_5_
  56.4 0.3 shard_map.90.rest_4_
  56.7 1.0 %collective-permute-start.16 = (bf16[112,128]{1,0:T(8,128)(2,1)S(1)}, bf16[112,128]{1,0:T(8,128)(2,1)S(1)}, u32[]{:S(2)}, u32[]{:S(2)}) collective-permute-start(bf16[112,128]{1,0:T(8,128)(2,1)S(1)} %shard_map.90.rest_4_), channel_id=1, source_target_pairs={{0,4},{4,0},{8,12},{12,8},{1,5},{5,1},{9,13},{13,9},{2,6},{6,2},{1... | collective-permute-start | bytes 86024 | tf_op jit(solution)/shard_map/ppermute | solution.py:506
  57.7 1.7 %collective-permute-start.17 = (bf16[112,128]{1,0:T(8,128)(2,1)S(1)}, bf16[112,128]{1,0:T(8,128)(2,1)S(1)}, u32[]{:S(2)}, u32[]{:S(2)}) collective-permute-start(bf16[112,128]{1,0:T(8,128)(2,1)S(1)} %shard_map.90.rest_4_), channel_id=1, source_target_pairs={{0,8},{4,12},{8,0},{12,4},{1,9},{5,13},{9,1},{13,5},{2,10},{6,14},... | collective-permute-start | bytes 86024 | tf_op jit(solution)/shard_map/ppermute | solution.py:506
  59.4 0.0 collective-permute-done.10.rest_2_
  59.4 1.8 %collective-permute-start.18 = (bf16[112,128]{1,0:T(8,128)(2,1)S(1)}, bf16[112,128]{1,0:T(8,128)(2,1)S(1)}, u32[]{:S(2)}, u32[]{:S(2)}) collective-permute-start(bf16[112,128]{1,0:T(8,128)(2,1)S(1)} %shard_map.90.rest_4_), channel_id=1, source_target_pairs={{0,12},{4,8},{8,4},{12,0},{1,13},{5,9},{9,5},{13,1},{2,14},{6,10},... | collective-permute-start | bytes 86024 | tf_op jit(solution)/shard_map/ppermute | solution.py:506
  61.1 0.6 shard_map.92.rest_9_.rest_2_
  61.7 0.6 shard_map.93.rest_10_.rest_3_
  62.3 0.0 collective-permute-done.11.rest_3_
  62.3 0.0 collective-permute-done.9.rest_1_
  62.3 0.0 collective-permute-done.16.rest_5_
  62.3 0.1 collective-permute-done.17.rest_6_
  62.4 2.6 %collective-permute-done.18.rest_7_ = bf16[112,128]{1,0:T(8,128)(2,1)S(1)} collective-permute-done((bf16[112,128]{1,0:T(8,128)(2,1)S(1)}, bf16[112,128]{1,0:T(8,128)(2,1)S(1)}, u32[]{:S(2)}, u32[]{:S(2)}) %collective-permute-start.18) | collective-permute-done | bytes 28704 | tf_op jit(solution)/shard_map/ppermute | solution.py:506
  65.0 0.7 %shard_map.94 = (bf16[4,128,384]{2,1,0:T(8,128)(2,1)S(1)}, bf16[3,256,256]{2,1,0:T(8,128)(2,1)S(1)}) custom-call(bf16[288,128]{1,0:T(8,128)(2,1)S(1)} %get-tuple-element.43.rest_0_, bf16[288,128]{1,0:T(8,128)(2,1)S(1)} %collective-permute-done.9.rest_1_, bf16[288,128]{1,0:T(8,128)(2,1)S(1)} %collective-permute-done.10.rest_2_, ...), custom_call_target="tpu_custom_call" | custom-call | flops 201326592 | bytes 1572864 | tf_op jit(solution)/shard_map/pallas_call | solution.py:57
  65.7 0.0 copy-start.2
  65.8 0.1 collective-permute-start.20
  65.8 0.4 shard_map.95.rest_1_
  66.2 0.6 collective-permute-start.19
  66.8 0.0 copy-done.2
  66.8 0.1 shard_map.96.rest_2_.rest_1_
  66.9 0.6 shard_map.97.half
  67.5 0.0 collective-permute-done.20.rest_0_
  67.5 0.4 shard_map.98.rest_2_
  67.9 0.2 collective-permute-done.19.rest_0_
  68.1 1.1 %shard_map.99 = bf16[8,128,384]{2,1,0:T(8,128)(2,1)} custom-call(f32[8,128]{1,0:T(8,128)S(1)} %broadcast_in_dim.6.live, f32[8,128,384]{2,1,0:T(8,128)S(1)} %shard_map.97.half, bf16[4,128,384]{2,1,0:T(8,128)(2,1)S(1)} %collective-permute-done.19.rest_0_, bf16[768,384]{1,0:T(8,128)(2,1)S(1)} %shard_map.96.rest_2_.rest_1_, ...), custom_call_target="tpu_custom_call" | custom-call | flops 301989888 | bytes 1572864 | tf_op jit(solution)/shard_map/pallas_call | solution.py:57
  (15 shorter events, 0.0 us)
Async XLA Ops:
  0.0 22.9 %copy-start.4 = (f32[768]{0:T(1024)S(1)}, f32[768]{0:T(1024)}, u32[]{:S(2)}) copy-start(f32[768]{0:T(1024)} %param.9) | copy-start | bytes 9220
  0.0 22.9 %copy-start.6 = (s32[8]{0:T(128)S(1)}, s32[8]{0:T(128)}, u32[]{:S(2)}) copy-start(s32[8]{0:T(128)} %param.14) | copy-start | bytes 100
  0.0 23.0 %copy-start = (bf16[768,384]{1,0:T(8,128)(2,1)S(1)}, bf16[768,384]{1,0:T(8,128)(2,1)}, u32[]{:S(2)}) copy-start(bf16[768,384]{1,0:T(8,128)(2,1)} %w_key.9) | copy-start | bytes 1769476
  0.0 23.0 %copy-start.3 = (bf16[768,384]{1,0:T(8,128)(2,1)S(1)}, bf16[768,384]{1,0:T(8,128)(2,1)}, u32[]{:S(2)}) copy-start(bf16[768,384]{1,0:T(8,128)(2,1)} %w_query.1) | copy-start | bytes 1769476
  1.8 13.5 %collective-permute-start = (bf16[272,768]{1,0:T(8,128)(2,1)S(1)}, bf16[272,768]{1,0:T(8,128)(2,1)S(1)}, u32[]{:S(2)}, u32[]{:S(2)}) collective-permute-start(bf16[272,768]{1,0:T(8,128)(2,1)S(1)} %get-tuple-element.31), channel_id=1, source_target_pairs={{0,2},{2,0},{1,3},{3,1},{4,6},{6,4},{5,7},{7,5},{8,10},{10,8},{9,1... | collective-permute-start | bytes 1253384 | tf_op jit(solution)/shard_map/ppermute | solution.py:28
  5.9 17.0 %collective-permute-start.4 = (bf16[256,768]{1,0:T(8,128)(2,1)S(1)}, bf16[256,768]{1,0:T(8,128)(2,1)S(1)}, u32[]{:S(2)}, u32[]{:S(2)}) collective-permute-start(bf16[256,768]{1,0:T(8,128)(2,1)S(1)} %shard_map.84), channel_id=1, source_target_pairs={{0,2},{2,0},{1,3},{3,1},{4,6},{6,4},{5,7},{7,5},{8,10},{10,8},{9,1... | collective-permute-start | bytes 1179656 | tf_op jit(solution)/shard_map/ppermute | solution.py:28
  15.3 18.5 %collective-permute-start.12 = (bf16[272,768]{1,0:T(8,128)(2,1)S(1)}, bf16[272,768]{1,0:T(8,128)(2,1)S(1)}, u32[]{:S(2)}, u32[]{:S(2)}) collective-permute-start(bf16[272,768]{1,0:T(8,128)(2,1)S(1)} %collective-permute-done.part), channel_id=1, source_target_pairs={{0,1},{1,0},{2,3},{3,2},{4,5},{5,4},{6,7},{7,6},{8,9},{9,8},{10,11... | collective-permute-start | bytes 1253384 | tf_op jit(solution)/shard_map/ppermute | solution.py:28
  22.9 9.0 %collective-permute-start.5 = (bf16[256,768]{1,0:T(8,128)(2,1)S(1)}, bf16[256,768]{1,0:T(8,128)(2,1)S(1)}, u32[]{:S(2)}, u32[]{:S(2)}) collective-permute-start(bf16[256,768]{1,0:T(8,128)(2,1)S(1)} %collective-permute-done.4.part), channel_id=1, source_target_pairs={{0,1},{1,0},{2,3},{3,2},{4,5},{5,4},{6,7},{7,6},{8,9},{9,8},{10,11... | collective-permute-start | bytes 1179656 | tf_op jit(solution)/shard_map/ppermute | solution.py:28
  23.0 6.9 %copy-start.5 = (s32[128]{0:T(128)S(1)}, s32[128]{0:T(128)}, u32[]{:S(2)}) copy-start(s32[128]{0:T(128)} %param.15) | copy-start | bytes 1540
  25.5 12.9 %collective-permute-start.1 = (f32[200,128]{1,0:T(8,128)S(1)}, f32[200,128]{1,0:T(8,128)S(1)}, u32[]{:S(2)}, u32[]{:S(2)}) collective-permute-start(f32[200,128]{1,0:T(8,128)S(1)} %get-tuple-element.34), channel_id=1, source_target_pairs={{0,4},{4,0},{8,12},{12,8},{1,5},{5,1},{9,13},{13,9},{2,6},{6,2},{1... | collective-permute-start | bytes 307208 | tf_op jit(solution)/shard_map/ppermute | solution.py:506
  27.3 11.6 %collective-permute-start.2 = (f32[200,128]{1,0:T(8,128)S(1)}, f32[200,128]{1,0:T(8,128)S(1)}, u32[]{:S(2)}, u32[]{:S(2)}) collective-permute-start(f32[200,128]{1,0:T(8,128)S(1)} %get-tuple-element.35), channel_id=1, source_target_pairs={{0,8},{4,12},{8,0},{12,4},{1,9},{5,13},{9,1},{13,5},{2,10},{6,14},... | collective-permute-start | bytes 307208 | tf_op jit(solution)/shard_map/ppermute | solution.py:506
  29.9 9.1 %collective-permute-start.3 = (f32[200,128]{1,0:T(8,128)S(1)}, f32[200,128]{1,0:T(8,128)S(1)}, u32[]{:S(2)}, u32[]{:S(2)}) collective-permute-start(f32[200,128]{1,0:T(8,128)S(1)} %get-tuple-element.36), channel_id=1, source_target_pairs={{0,12},{4,8},{8,4},{12,0},{1,13},{5,9},{9,5},{13,1},{2,14},{6,10},... | collective-permute-start | bytes 307208 | tf_op jit(solution)/shard_map/ppermute | solution.py:506
  32.9 6.1 %collective-permute-start.6 = (f32[96,128]{1,0:T(8,128)S(1)}, f32[96,128]{1,0:T(8,128)S(1)}, u32[]{:S(2)}, u32[]{:S(2)}) collective-permute-start(f32[96,128]{1,0:T(8,128)S(1)} %get-tuple-element.40), channel_id=1, source_target_pairs={{0,4},{4,0},{8,12},{12,8},{1,5},{5,1},{9,13},{13,9},{2,6},{6,2},{1... | collective-permute-start | bytes 147464 | tf_op jit(solution)/shard_map/ppermute | solution.py:506
  33.9 9.2 %collective-permute-start.7 = (f32[96,128]{1,0:T(8,128)S(1)}, f32[96,128]{1,0:T(8,128)S(1)}, u32[]{:S(2)}, u32[]{:S(2)}) collective-permute-start(f32[96,128]{1,0:T(8,128)S(1)} %get-tuple-element.41), channel_id=1, source_target_pairs={{0,8},{4,12},{8,0},{12,4},{1,9},{5,13},{9,1},{13,5},{2,10},{6,14},... | collective-permute-start | bytes 147464 | tf_op jit(solution)/shard_map/ppermute | solution.py:506
  37.4 13.8 %copy-start.1 = (bf16[768,384]{1,0:T(8,128)(2,1)S(1)}, bf16[768,384]{1,0:T(8,128)(2,1)}, u32[]{:S(2)}) copy-start(bf16[768,384]{1,0:T(8,128)(2,1)} %refs_2_.3) | copy-start | bytes 1769476
  38.4 6.0 %collective-permute-start.8 = (f32[96,128]{1,0:T(8,128)S(1)}, f32[96,128]{1,0:T(8,128)S(1)}, u32[]{:S(2)}, u32[]{:S(2)}) collective-permute-start(f32[96,128]{1,0:T(8,128)S(1)} %get-tuple-element.42), channel_id=1, source_target_pairs={{0,12},{4,8},{8,4},{12,0},{1,13},{5,9},{9,5},{13,1},{2,14},{6,10},... | collective-permute-start | bytes 147464 | tf_op jit(solution)/shard_map/ppermute | solution.py:506
  39.0 11.4 %collective-permute-start.13 = (f32[96,128]{1,0:T(8,128)S(1)}, f32[96,128]{1,0:T(8,128)S(1)}, u32[]{:S(2)}, u32[]{:S(2)}) collective-permute-start(f32[96,128]{1,0:T(8,128)S(1)} %get-tuple-element.47), channel_id=1, source_target_pairs={{0,4},{4,0},{8,12},{12,8},{1,5},{5,1},{9,13},{13,9},{2,6},{6,2},{1... | collective-permute-start | bytes 147464 | tf_op jit(solution)/shard_map/ppermute | solution.py:506
  44.6 14.8 %collective-permute-start.10 = (bf16[288,128]{1,0:T(8,128)(2,1)S(1)}, bf16[288,128]{1,0:T(8,128)(2,1)S(1)}, u32[]{:S(2)}, u32[]{:S(2)}) collective-permute-start(bf16[288,128]{1,0:T(8,128)(2,1)S(1)} %get-tuple-element.43.rest_0_), channel_id=1, source_target_pairs={{0,8},{4,12},{8,0},{12,4},{1,9},{5,13},{9,1},{13,5},{2,10},{6,14},... | collective-permute-start | bytes 221192 | tf_op jit(solution)/shard_map/ppermute | solution.py:506
  46.0 16.3 %collective-permute-start.11 = (bf16[288,128]{1,0:T(8,128)(2,1)S(1)}, bf16[288,128]{1,0:T(8,128)(2,1)S(1)}, u32[]{:S(2)}, u32[]{:S(2)}) collective-permute-start(bf16[288,128]{1,0:T(8,128)(2,1)S(1)} %get-tuple-element.43.rest_0_), channel_id=1, source_target_pairs={{0,12},{4,8},{8,4},{12,0},{1,13},{5,9},{9,5},{13,1},{2,14},{6,10},... | collective-permute-start | bytes 221192 | tf_op jit(solution)/shard_map/ppermute | solution.py:506
  46.8 15.5 %collective-permute-start.9 = (bf16[288,128]{1,0:T(8,128)(2,1)S(1)}, bf16[288,128]{1,0:T(8,128)(2,1)S(1)}, u32[]{:S(2)}, u32[]{:S(2)}) collective-permute-start(bf16[288,128]{1,0:T(8,128)(2,1)S(1)} %get-tuple-element.43.rest_0_), channel_id=1, source_target_pairs={{0,4},{4,0},{8,12},{12,8},{1,5},{5,1},{9,13},{13,9},{2,6},{6,2},{1... | collective-permute-start | bytes 221192 | tf_op jit(solution)/shard_map/ppermute | solution.py:506
  48.1 7.6 %collective-permute-start.14 = (f32[96,128]{1,0:T(8,128)S(1)}, f32[96,128]{1,0:T(8,128)S(1)}, u32[]{:S(2)}, u32[]{:S(2)}) collective-permute-start(f32[96,128]{1,0:T(8,128)S(1)} %get-tuple-element.48), channel_id=1, source_target_pairs={{0,8},{4,12},{8,0},{12,4},{1,9},{5,13},{9,1},{13,5},{2,10},{6,14},... | collective-permute-start | bytes 147464 | tf_op jit(solution)/shard_map/ppermute | solution.py:506
  50.4 6.0 %collective-permute-start.15 = (f32[96,128]{1,0:T(8,128)S(1)}, f32[96,128]{1,0:T(8,128)S(1)}, u32[]{:S(2)}, u32[]{:S(2)}) collective-permute-start(f32[96,128]{1,0:T(8,128)S(1)} %get-tuple-element.49), channel_id=1, source_target_pairs={{0,12},{4,8},{8,4},{12,0},{1,13},{5,9},{9,5},{13,1},{2,14},{6,10},... | collective-permute-start | bytes 147464 | tf_op jit(solution)/shard_map/ppermute | solution.py:506
  56.7 5.6 %collective-permute-start.16 = (bf16[112,128]{1,0:T(8,128)(2,1)S(1)}, bf16[112,128]{1,0:T(8,128)(2,1)S(1)}, u32[]{:S(2)}, u32[]{:S(2)}) collective-permute-start(bf16[112,128]{1,0:T(8,128)(2,1)S(1)} %shard_map.90.rest_4_), channel_id=1, source_target_pairs={{0,4},{4,0},{8,12},{12,8},{1,5},{5,1},{9,13},{13,9},{2,6},{6,2},{1... | collective-permute-start | bytes 86024 | tf_op jit(solution)/shard_map/ppermute | solution.py:506
  57.7 4.8 %collective-permute-start.17 = (bf16[112,128]{1,0:T(8,128)(2,1)S(1)}, bf16[112,128]{1,0:T(8,128)(2,1)S(1)}, u32[]{:S(2)}, u32[]{:S(2)}) collective-permute-start(bf16[112,128]{1,0:T(8,128)(2,1)S(1)} %shard_map.90.rest_4_), channel_id=1, source_target_pairs={{0,8},{4,12},{8,0},{12,4},{1,9},{5,13},{9,1},{13,5},{2,10},{6,14},... | collective-permute-start | bytes 86024 | tf_op jit(solution)/shard_map/ppermute | solution.py:506
  59.4 5.7 %collective-permute-start.18 = (bf16[112,128]{1,0:T(8,128)(2,1)S(1)}, bf16[112,128]{1,0:T(8,128)(2,1)S(1)}, u32[]{:S(2)}, u32[]{:S(2)}) collective-permute-start(bf16[112,128]{1,0:T(8,128)(2,1)S(1)} %shard_map.90.rest_4_), channel_id=1, source_target_pairs={{0,12},{4,8},{8,4},{12,0},{1,13},{5,9},{9,5},{13,1},{2,14},{6,10},... | collective-permute-start | bytes 86024 | tf_op jit(solution)/shard_map/ppermute | solution.py:506
  65.7 1.1 %copy-start.2 = (bf16[768,384]{1,0:T(8,128)(2,1)S(1)}, bf16[768,384]{1,0:T(8,128)(2,1)}, u32[]{:S(2)}) copy-start(bf16[768,384]{1,0:T(8,128)(2,1)} %w_out.1) | copy-start | bytes 1769476
  65.8 1.8 %collective-permute-start.20 = (bf16[4,128,384]{2,1,0:T(8,128)(2,1)S(1)}, bf16[4,128,384]{2,1,0:T(8,128)(2,1)S(1)}, u32[]{:S(2)}, u32[]{:S(2)}) collective-permute-start(bf16[4,128,384]{2,1,0:T(8,128)(2,1)S(1)} %get-tuple-element.55.rest_0_), channel_id=1, source_target_pairs={{0,1},{1,0},{2,3},{3,2},{4,5},{5,4},{6,7},{7,6},{8,9},{9,8},{10,11... | collective-permute-start | bytes 1179656 | tf_op jit(solution)/shard_map/ppermute | solution.py:28
  66.2 1.9 %collective-permute-start.19 = (bf16[4,128,384]{2,1,0:T(8,128)(2,1)S(1)}, bf16[4,128,384]{2,1,0:T(8,128)(2,1)S(1)}, u32[]{:S(2)}, u32[]{:S(2)}) collective-permute-start(bf16[4,128,384]{2,1,0:T(8,128)(2,1)S(1)} %shard_map.95.rest_1_), channel_id=1, source_target_pairs={{0,1},{1,0},{2,3},{3,2},{4,5},{5,4},{6,7},{7,6},{8,9},{9,8},{10,11... | collective-permute-start | bytes 1179656 | tf_op jit(solution)/shard_map/ppermute | solution.py:28
